TPU v7x, 256 devices: a whole 4x4x8 slice. The times are simulated.
256 devices in a mesh: blk: 32 (over z_hi, y, core), head: 8 (over z_lo, x).
Axes of the slice: x: 4, y: 4, z: 8 (z_hi: 4, z_lo: 2; z = z_hi * 2 + z_lo), core: 2. Of those that a mesh axis runs over, the one named last changes fastest.
Arguments:
- query: bfloat16 [32768, 3072], P(('blk', 'head')), may hold values from -6 to 6
- keys: bfloat16 [32768, 3072], P(('blk', 'head')), may hold values from -6 to 6
- values: bfloat16 [32768, 3072], P(('blk', 'head')), may hold values from -6 to 6
- cotangent: bfloat16 [32768, 3072], P(('blk', 'head')), may hold values from -6 to 6
- kv_tiles: int32 [24, 256, 9], P('head'), may hold values from 0 to 255, as said below
Outputs:
- attended: bfloat16 [32768, 3072], P(('blk', 'head'))
- d_query: bfloat16 [32768, 3072], P(('blk', 'head'))
- d_keys: bfloat16 [32768, 3072], P(('blk', 'head'))
- d_values: bfloat16 [32768, 3072], P(('blk', 'head'))
Inputs may be any that keep to these rules, and one draw needn't show every extreme that they name: `kv_tiles`: the 9 entries of a row are distinct; the first 2 entries are the same in every row of one head (that head's global tiles); every other entry lies within 8 tiles of the row's query tile and is not a global tile of that head.
All inputs are finite; a program needn't handle non-finite values.
Results may differ from a plain program's by a relative error of at most 0.017.
Values may be sent and summed in bfloat16 or wider, within the bound.
A program may use at most 192 MiB of HBM per device.

v0:
```python
import functools

import jax
import jax.numpy as jnp
from jax import lax
from jax.experimental import pallas as pl
from jax.experimental.pallas import tpu as pltpu
from jax.sharding import PartitionSpec as P

MESH = pl.DeviceIdType.MESH
HD = 128
TILE = 128
GLOBALS = 2
HALF = 8


def passed_along(block, axis, distance):
    devices = range(lax.axis_size(axis))
    route = [(i - distance, i) for i in devices if i - distance in devices]
    return lax.ppermute(block, axis, route)


def reduce_kernel(count, x_ref, out_ref, inbox, gathered, mine, send_sem, recv_sem, back_send, back_recv):
    me = lax.axis_index("blk")
    column = lax.axis_index("head")
    barrier = pltpu.get_barrier_semaphore()
    for k in range(1, count):
        pl.semaphore_signal(
            barrier, 1, device_id=(lax.rem(me + k, count), column), device_id_type=MESH
        )
    pl.semaphore_wait(barrier, count - 1)
    outgoing = []
    for k in range(1, count):
        peer = lax.rem(me + k, count)
        copy = pltpu.make_async_remote_copy(
            src_ref=x_ref.at[peer],
            dst_ref=inbox.at[me],
            send_sem=send_sem.at[k],
            recv_sem=recv_sem.at[me],
            device_id=(peer, column),
            device_id_type=MESH,
        )
        copy.start()
        outgoing.append(copy)
    total = x_ref[me].astype(jnp.float32)
    for k in range(1, count):
        source = lax.rem(me + count - k, count)
        pltpu.make_async_remote_copy(
            src_ref=x_ref.at[source],
            dst_ref=inbox.at[source],
            send_sem=send_sem.at[k],
            recv_sem=recv_sem.at[source],
            device_id=(source, column),
            device_id_type=MESH,
        ).wait_recv()
        total = total + inbox[source].astype(jnp.float32)
    mine[...] = total.astype(mine.dtype)
    for k in range(1, count):
        peer = lax.rem(me + k, count)
        copy = pltpu.make_async_remote_copy(
            src_ref=mine,
            dst_ref=gathered.at[me],
            send_sem=back_send.at[k],
            recv_sem=back_recv.at[me],
            device_id=(peer, column),
            device_id_type=MESH,
        )
        copy.start()
        outgoing.append(copy)
    gathered[me] = mine[...]
    for k in range(1, count):
        source = lax.rem(me + count - k, count)
        pltpu.make_async_remote_copy(
            src_ref=mine,
            dst_ref=gathered.at[source],
            send_sem=back_send.at[k],
            recv_sem=back_recv.at[source],
            device_id=(source, column),
            device_id_type=MESH,
        ).wait_recv()
    for copy in outgoing:
        copy.wait_send()
    out_ref[...] = gathered[...]


def butterfly_sum(block, axis, collective):
    count = lax.axis_size(axis)
    if block.size % (count * 8 * 128):
        return lax.psum(block, axis)
    pieces = block.reshape(count, -1, 128)
    vmem = pltpu.VMEM
    summed = pl.pallas_call(
        functools.partial(reduce_kernel, count),
        out_shape=jax.ShapeDtypeStruct(pieces.shape, pieces.dtype),
        in_specs=[pl.BlockSpec(memory_space=vmem)],
        out_specs=pl.BlockSpec(memory_space=vmem),
        scratch_shapes=[
            pltpu.VMEM(pieces.shape, pieces.dtype),
            pltpu.VMEM(pieces.shape, pieces.dtype),
            pltpu.VMEM(pieces.shape[1:], pieces.dtype),
            pltpu.SemaphoreType.DMA((count,)),
            pltpu.SemaphoreType.DMA((count,)),
            pltpu.SemaphoreType.DMA((count,)),
            pltpu.SemaphoreType.DMA((count,)),
        ],
        compiler_params=pltpu.CompilerParams(collective_id=collective, has_side_effects=True),
    )(pieces)
    return summed.reshape(block.shape)


def split_heads(field, count):
    heads = field.shape[1] // HD
    return field.reshape(count, TILE, heads, HD).transpose(2, 0, 1, 3)


def merge_heads(field):
    heads = field.shape[0]
    count = field.shape[1]
    return field.transpose(1, 2, 0, 3).reshape(count * TILE, heads * HD)


def attention_kernel(index_ref, q_ref, do_ref, k_ref, v_ref, att_ref, dq_ref, dk_ref, dv_ref, kbuf, vbuf):
    heads = q_ref.shape[1] // HD
    tiles = q_ref.shape[0] // TILE
    slots = index_ref.shape[0] // (heads * tiles)
    scale = HD ** (-0.5)
    dk_ref[...] = jnp.zeros_like(dk_ref)
    dv_ref[...] = jnp.zeros_like(dv_ref)
    nt = (((1,), (1,)), ((), ()))
    tn = (((0,), (0,)), ((), ()))

    def step(item, carry):
        head = item // tiles
        tile = item % tiles
        cols = pl.ds(pl.multiple_of(head * HD, HD), HD)
        rows = pl.ds(pl.multiple_of(tile * TILE, TILE), TILE)
        picks = [
            pl.ds(pl.multiple_of(index_ref[item * slots + s] * TILE, TILE), TILE)
            for s in range(slots)
        ]
        for s in range(slots):
            kbuf[s * TILE : (s + 1) * TILE, :] = k_ref[picks[s], cols]
            vbuf[s * TILE : (s + 1) * TILE, :] = v_ref[picks[s], cols]
        query = q_ref[rows, cols]
        grad_out = do_ref[rows, cols]
        chosen_keys = kbuf[...]
        chosen_values = vbuf[...]
        scores = (
            lax.dot_general(query, chosen_keys, nt, preferred_element_type=jnp.float32) * scale
        )
        peak = jnp.max(scores, axis=1, keepdims=True)
        log_total = peak + jnp.log(jnp.sum(jnp.exp(scores - peak), axis=1, keepdims=True))
        probs = jnp.exp(scores - log_total)
        weights = probs.astype(jnp.bfloat16)
        attended = jnp.dot(weights, chosen_values, preferred_element_type=jnp.float32).astype(
            jnp.bfloat16
        )
        att_ref[rows, cols] = attended
        delta = jnp.sum(
            grad_out.astype(jnp.float32) * attended.astype(jnp.float32), axis=1, keepdims=True
        )
        grad_probs = lax.dot_general(
            grad_out, chosen_values, nt, preferred_element_type=jnp.float32
        )
        grad_scores = (probs * (grad_probs - delta)).astype(jnp.bfloat16)
        dq_ref[rows, cols] = (
            jnp.dot(grad_scores, chosen_keys, preferred_element_type=jnp.float32) * scale
        ).astype(jnp.bfloat16)
        key_slots = (
            lax.dot_general(grad_scores, query, tn, preferred_element_type=jnp.float32) * scale
        )
        value_slots = lax.dot_general(weights, grad_out, tn, preferred_element_type=jnp.float32)
        for s in range(slots):
            dk_ref[picks[s], cols] += key_slots[s * TILE : (s + 1) * TILE]
            dv_ref[picks[s], cols] += value_slots[s * TILE : (s + 1) * TILE]
        return carry

    lax.fori_loop(0, heads * tiles, step, 0)


def attend(pool_index, query_rows, grad_rows, pool_keys, pool_values):
    count, width = query_rows.shape
    pool_rows = pool_keys.shape[0]
    slots = pool_index.shape[-1]
    vmem = pltpu.VMEM
    flops = 2 * 7 * count * slots * TILE * width
    return pl.pallas_call(
        attention_kernel,
        out_shape=(
            jax.ShapeDtypeStruct((count, width), jnp.bfloat16),
            jax.ShapeDtypeStruct((count, width), jnp.bfloat16),
            jax.ShapeDtypeStruct((pool_rows, width), jnp.float32),
            jax.ShapeDtypeStruct((pool_rows, width), jnp.float32),
        ),
        in_specs=[pl.BlockSpec(memory_space=pltpu.SMEM)] + [pl.BlockSpec(memory_space=vmem)] * 4,
        out_specs=tuple(pl.BlockSpec(memory_space=vmem) for _ in range(4)),
        scratch_shapes=[
            pltpu.VMEM((slots * TILE, HD), jnp.bfloat16),
            pltpu.VMEM((slots * TILE, HD), jnp.bfloat16),
        ],
        compiler_params=pltpu.CompilerParams(vmem_limit_bytes=60 * 1024 * 1024),
        cost_estimate=pl.CostEstimate(
            flops=flops,
            transcendentals=count * slots * TILE * width // HD,
            bytes_accessed=8 * count * width + 12 * pool_rows * width,
        ),
    )(pool_index.reshape(-1), query_rows, grad_rows, pool_keys, pool_values)


def per_device(query, keys, values, cotangent, kv_tiles):
    head_count = lax.axis_size("head")
    cycle_pos = lax.axis_index("blk")
    per_frame = query.shape[0] * head_count // TILE
    reach = -(-HALF // per_frame)
    span = (2 * reach + 1) * per_frame
    global_tiles = kv_tiles[:, 0, :GLOBALS]
    own_tiles = lax.dynamic_slice_in_dim(kv_tiles, cycle_pos * per_frame, per_frame, 1)
    moved = lax.all_to_all(
        jnp.stack([query, keys, values, cotangent]), "head", split_axis=2, concat_axis=1, tiled=True
    )
    frame_keys = moved[1]
    frame_values = moved[2]
    offset = 1
    earlier = passed_along((frame_keys, frame_values), "blk", offset)
    later = passed_along((frame_keys, frame_values), "blk", -offset)
    earlier_keys = [earlier[0]]
    earlier_values = [earlier[1]]
    later_keys = [later[0]]
    later_values = [later[1]]
    near_keys = jnp.stack(earlier_keys[::-1] + later_keys, axis=0)
    near_values = jnp.stack(earlier_values[::-1] + later_values, axis=0)
    width = frame_keys.shape[1]
    all_keys = jnp.concatenate(
        [near_keys[:reach], frame_keys[None], near_keys[reach:]], axis=0
    ).reshape(span * TILE, width)
    all_values = jnp.concatenate(
        [near_values[:reach], frame_values[None], near_values[reach:]], axis=0
    ).reshape(span * TILE, width)
    heads = width // HD
    tile_ids = cycle_pos * per_frame + jnp.arange(per_frame, dtype=jnp.int32)
    owner = global_tiles[:, :, None] == tile_ids[None, None, :]
    owner_mask = owner.astype(jnp.bfloat16)
    frame_key_tiles = frame_keys.reshape(per_frame, TILE, heads, HD)
    frame_value_tiles = frame_values.reshape(per_frame, TILE, heads, HD)
    global_keys = jnp.einsum(
        "hjt,tkhd->jkhd", owner_mask, frame_key_tiles, preferred_element_type=jnp.float32
    )
    global_values = jnp.einsum(
        "hjt,tkhd->jkhd", owner_mask, frame_value_tiles, preferred_element_type=jnp.float32
    )
    global_both = butterfly_sum(
        jnp.stack([global_keys.astype(jnp.bfloat16), global_values.astype(jnp.bfloat16)]), "blk", 0
    )
    global_rows = GLOBALS * TILE
    pool_keys = jnp.concatenate([all_keys, global_both[0].reshape(global_rows, width)], axis=0)
    pool_values = jnp.concatenate([all_values, global_both[1].reshape(global_rows, width)], axis=0)
    relative = own_tiles - (cycle_pos - reach) * per_frame
    inside = (relative >= 0) & (relative < span)
    matches = own_tiles[:, :, :, None] == global_tiles[:, None, None, :]
    slot_numbers = jnp.arange(global_tiles.shape[1], dtype=jnp.int32)
    global_slot = jnp.sum(jnp.where(matches, slot_numbers[None, None, None, :], 0), axis=-1)
    pool_index = jnp.where(inside, relative, span + global_slot)
    attended, query_rows, key_pool, value_pool = attend(
        pool_index, moved[0], moved[3], pool_keys, pool_values
    )
    frame_rows = per_frame * TILE
    centre = reach * frame_rows
    key_grad = key_pool[centre : centre + frame_rows]
    value_grad = value_pool[centre : centre + frame_rows]
    offset = 1
    lower = (reach - offset) * frame_rows
    returned = (
        passed_along(
            key_pool[lower : lower + frame_rows].astype(jnp.bfloat16), "blk", -offset
        ).astype(jnp.float32),
        passed_along(
            value_pool[lower : lower + frame_rows].astype(jnp.bfloat16), "blk", -offset
        ).astype(jnp.float32),
    )
    key_grad = key_grad + returned[0]
    value_grad = value_grad + returned[1]
    upper = (reach + offset) * frame_rows
    returned = (
        passed_along(
            key_pool[upper : upper + frame_rows].astype(jnp.bfloat16), "blk", offset
        ).astype(jnp.float32),
        passed_along(
            value_pool[upper : upper + frame_rows].astype(jnp.bfloat16), "blk", offset
        ).astype(jnp.float32),
    )
    key_grad = key_grad + returned[0]
    value_grad = value_grad + returned[1]
    pool_end = span * TILE
    summed = butterfly_sum(
        jnp.stack([key_pool[pool_end:], value_pool[pool_end:]]).reshape(
            2, GLOBALS, TILE, heads, HD
        ),
        "blk",
        1,
    )
    owner_float = owner.astype(jnp.float32)
    key_grad = key_grad + jnp.einsum(
        "hjt,jkhd->tkhd", owner_float, summed[0], precision=lax.Precision.HIGHEST
    ).reshape(frame_rows, width)
    value_grad = value_grad + jnp.einsum(
        "hjt,jkhd->tkhd", owner_float, summed[1], precision=lax.Precision.HIGHEST
    ).reshape(frame_rows, width)
    key_rows = key_grad.astype(jnp.bfloat16)
    value_rows = value_grad.astype(jnp.bfloat16)
    forward_back = lax.all_to_all(
        jnp.stack([attended, query_rows]), "head", split_axis=1, concat_axis=2, tiled=True
    )
    backward_back = lax.all_to_all(
        jnp.stack([key_rows, value_rows]), "head", split_axis=1, concat_axis=2, tiled=True
    )
    results = (forward_back[0], forward_back[1], backward_back[0], backward_back[1])
    return (results[0], results[1], results[2], results[3])


def solution(mesh):
    placed = (
        P(("blk", "head"), None),
        P(("blk", "head"), None),
        P(("blk", "head"), None),
        P(("blk", "head"), None),
        P("head", None, None),
    )
    return jax.shard_map(
        per_device,
        mesh=mesh,
        in_specs=placed,
        out_specs=(
            P(("blk", "head"), None),
            P(("blk", "head"), None),
            P(("blk", "head"), None),
            P(("blk", "head"), None),
        ),
        check_vma=False,
    )
```

profile of v0, /device:TPU:160, one launch (start us, length us, event | category | flops | bytes accessed | tf_op | source)
XLA Modules:
  0.0 326.7 jit_solution(17050815994437383635)
XLA Ops:
  0.6 2.0 pad_maximum_fusion
  2.7 3.6 %copy.147 = bf16[4,128,3072]{1,0,2:T(4,128)(2,1)} copy(bf16[4,128,3072]{2,1,0:T(8,128)(2,1)S(1)} %pad_maximum_fusion) | data formatting | bytes 6291456 | tf_op jit(solution)/shard_map/stack | solution.py:219
  6.3 5.9 %all-to-all-start = ((bf16[4,128,3072]{1,0,2:T(4,128)(2,1)}), bf16[4,128,3072]{1,0,2:T(4,128)(2,1)S(1)}, u32[]{:S(2)}, u32[]{:S(2)}) async-start(bf16[4,128,3072]{1,0,2:T(4,128)(2,1)} %copy.147), calls=%async_computation | async-start | bytes 6291456 | tf_op jit(solution)/shard_map/all_to_all | solution.py:218
  12.6 36.3 %all-to-all-done = bf16[4,128,3072]{1,0,2:T(4,128)(2,1)S(1)} async-done(((bf16[4,128,3072]{1,0,2:T(4,128)(2,1)}), bf16[4,128,3072]{1,0,2:T(4,128)(2,1)S(1)}, u32[]{:S(2)}, u32[]{:S(2)}) %all-to-all-start) | async-done | bytes 3145760 | tf_op jit(solution)/shard_map/all_to_all | solution.py:218
  51.1 1.9 collective-permute-start.2
  53.1 7.9 %collective-permute-start.3 = (bf16[1024,384]{1,0:T(8,128)(2,1)S(1)}, bf16[1024,384]{1,0:T(8,128)(2,1)}, u32[]{:S(2)}, u32[]{:S(2)}) collective-permute-start(bf16[1024,384]{1,0:T(8,128)(2,1)S(1)} %bitcast.101), channel_id=1, source_target_pairs={{8,0},{16,8},{24,16},{32,24},{40,32},{48,40},{56,48},{64,56},{72,6... | collective-permute-start | bytes 2359304 | tf_op jit(solution)/shard_map/ppermute | solution.py:20
  61.9 1.9 collective-permute-start
  63.9 8.0 %collective-permute-start.1 = (bf16[1024,384]{1,0:T(8,128)(2,1)S(1)}, bf16[1024,384]{1,0:T(8,128)(2,1)}, u32[]{:S(2)}, u32[]{:S(2)}) collective-permute-start(bf16[1024,384]{1,0:T(8,128)(2,1)S(1)} %bitcast.104), channel_id=1, source_target_pairs={{8,0},{16,8},{24,16},{32,24},{40,32},{48,40},{56,48},{64,56},{72,6... | collective-permute-start | bytes 2359304 | tf_op jit(solution)/shard_map/ppermute | solution.py:20
  77.3 2.1 reshape.63.x_ref
  79.4 36.1 %shard_map.84 = bf16[32,48,128]{2,1,0:T(8,128)(2,1)} custom-call(bf16[32,48,128]{2,1,0:T(8,128)(2,1)} %reshape.63.x_ref), custom_call_target="tpu_custom_call" | custom-call | tf_op jit(solution)/shard_map/pallas_call | solution.py:92
  122.4 1.8 pad_maximum_fusion.2.v_ref
  127.5 36.7 %shard_map.85 = (bf16[1024,384]{1,0:T(8,128)(2,1)}, bf16[1024,384]{1,0:T(8,128)(2,1)}, f32[3328,384]{1,0:T(8,128)}, f32[3328,384]{1,0:T(8,128)}) custom-call(s32[216]{0:T(256)} %reshape.61.index_ref, bf16[1024,384]{1,0:T(8,128)(2,1)} %bitcast.114, bf16[1024,384]{1,0:T(8,128)(2,1)} %bitcast.115, bf16[3328,384]{1,0:T(8,128)(2,1)} %pad_maximum_fusion.1.k_ref, ...), custom_call_target="tpu_custom_call" | custom-call | flops 6341787648 | bytes 18481152 | tf_op jit(solution)/shard_map/pallas_call | solution.py:187
  165.7 2.8 copy.159
  168.5 9.7 %all-to-all-start.1 = ((bf16[2,1024,384]{2,0,1:T(2,128)(2,1)}), bf16[2,1024,384]{2,0,1:T(2,128)(2,1)S(1)}, u32[]{:S(2)}, u32[]{:S(2)}) async-start(bf16[2,1024,384]{2,0,1:T(2,128)(2,1)} %copy.159), calls=%async_computation.1 | async-start | bytes 3145728 | tf_op jit(solution)/shard_map/all_to_all | solution.py:310
  178.2 4.2 %convert.8 = bf16[3328,384]{1,0:T(8,128)(2,1)} convert(f32[3328,384]{1,0:T(8,128)} %get-tuple-element.10) | non-fusion elementwise | flops 1277952 | bytes 7667712 | tf_op jit(solution)/shard_map/convert.3
  182.3 4.2 %convert.9 = bf16[3328,384]{1,0:T(8,128)(2,1)} convert(f32[3328,384]{1,0:T(8,128)} %get-tuple-element.11) | non-fusion elementwise | flops 1277952 | bytes 7667712 | tf_op jit(solution)/shard_map/convert.1
  188.7 53.1 %shard_map.86 = f32[32,48,128]{2,1,0:T(8,128)} custom-call(f32[32,48,128]{2,1,0:T(8,128)} %reshape_reshape.3.x_ref), custom_call_target="tpu_custom_call" | custom-call | tf_op jit(solution)/shard_map/pallas_call | solution.py:92
  243.2 2.6 fusion.25
  245.8 4.0 %collective-permute-start.4 = (bf16[1024,384]{1,0:T(8,128)(2,1)}, bf16[1024,384]{1,0:T(8,128)(2,1)}, u32[]{:S(2)}, u32[]{:S(2)}) collective-permute-start(bf16[1024,384]{1,0:T(8,128)(2,1)} %get-tuple-element.16), channel_id=1, source_target_pairs={{8,0},{16,8},{24,16},{32,24},{40,32},{48,40},{56,48},{64,56},{72,6... | collective-permute-start | bytes 2359304 | tf_op jit(solution)/shard_map/ppermute | solution.py:20
  249.8 1.9 collective-permute-start.5
  253.0 7.9 %collective-permute-start.6 = (bf16[1024,384]{1,0:T(8,128)(2,1)}, bf16[1024,384]{1,0:T(8,128)(2,1)}, u32[]{:S(2)}, u32[]{:S(2)}) collective-permute-start(bf16[1024,384]{1,0:T(8,128)(2,1)} %get-tuple-element.18), channel_id=1, source_target_pairs={{8,0},{16,8},{24,16},{32,24},{40,32},{48,40},{56,48},{64,56},{72,6... | collective-permute-start | bytes 2359304 | tf_op jit(solution)/shard_map/ppermute | solution.py:20
  260.9 1.9 collective-permute-start.7
  263.9 2.4 copy.172
  268.7 14.9 %collective-permute-done.5 = bf16[1024,384]{1,0:T(8,128)(2,1)} collective-permute-done((bf16[1024,384]{1,0:T(8,128)(2,1)S(1)}, bf16[1024,384]{1,0:T(8,128)(2,1)}, u32[]{:S(2)}, u32[]{:S(2)}) %collective-permute-start.5) | collective-permute-done | bytes 786464 | tf_op jit(solution)/shard_map/ppermute | solution.py:20
  283.6 2.3 fusion.4
  285.9 6.2 %collective-permute-done.7 = bf16[1024,384]{1,0:T(8,128)(2,1)} collective-permute-done((bf16[1024,384]{1,0:T(8,128)(2,1)}, bf16[1024,384]{1,0:T(8,128)(2,1)}, u32[]{:S(2)}, u32[]{:S(2)}) %collective-permute-start.7) | collective-permute-done | bytes 786464 | tf_op jit(solution)/shard_map/ppermute | solution.py:20
  292.0 2.3 fusion.5
  294.5 2.8 copy.168
  297.3 10.0 %all-to-all-start.2 = ((bf16[2,1024,384]{2,0,1:T(2,128)(2,1)}), bf16[2,1024,384]{2,0,1:T(2,128)(2,1)S(1)}, u32[]{:S(2)}, u32[]{:S(2)}) async-start(bf16[2,1024,384]{2,0,1:T(2,128)(2,1)} %copy.168), calls=%async_computation.2 | async-start | bytes 3145728 | tf_op jit(solution)/shard_map/all_to_all | solution.py:313
  307.2 2.9 fusion.28
  313.9 6.2 %all-to-all-done.2 = bf16[2,1024,384]{2,0,1:T(2,128)(2,1)S(1)} async-done(((bf16[2,1024,384]{2,0,1:T(2,128)(2,1)}), bf16[2,1024,384]{2,0,1:T(2,128)(2,1)S(1)}, u32[]{:S(2)}, u32[]{:S(2)}) %all-to-all-start.2) | async-done | bytes 1572896 | tf_op jit(solution)/shard_map/all_to_all | solution.py:313
  320.1 2.9 fusion.27
  (63 shorter events, 36.6 us)
Async XLA Ops:
  6.3 5.9 %copy-start.4 = (s32[3,256,9]{1,0,2:T(4,128)S(1)}, s32[3,256,9]{1,0,2:T(4,128)}, u32[]{:S(2)}) copy-start(s32[3,256,9]{1,0,2:T(4,128)} %param.9) | copy-start | bytes 82948
  6.3 42.6 %all-to-all-start = ((bf16[4,128,3072]{1,0,2:T(4,128)(2,1)}), bf16[4,128,3072]{1,0,2:T(4,128)(2,1)S(1)}, u32[]{:S(2)}, u32[]{:S(2)}) async-start(bf16[4,128,3072]{1,0,2:T(4,128)(2,1)} %copy.147), calls=%async_computation | async-start | bytes 6291456 | tf_op jit(solution)/shard_map/all_to_all | solution.py:218
  51.1 69.6 %collective-permute-start.2 = (bf16[1024,384]{1,0:T(8,128)(2,1)S(1)}, bf16[1024,384]{1,0:T(8,128)(2,1)}, u32[]{:S(2)}, u32[]{:S(2)}) collective-permute-start(bf16[1024,384]{1,0:T(8,128)(2,1)S(1)} %bitcast.100), channel_id=1, source_target_pairs={{0,8},{8,16},{16,24},{24,32},{32,40},{40,48},{48,56},{56,64},{64,7... | collective-permute-start | bytes 2359304 | tf_op jit(solution)/shard_map/ppermute | solution.py:20
  53.1 67.6 %collective-permute-start.3 = (bf16[1024,384]{1,0:T(8,128)(2,1)S(1)}, bf16[1024,384]{1,0:T(8,128)(2,1)}, u32[]{:S(2)}, u32[]{:S(2)}) collective-permute-start(bf16[1024,384]{1,0:T(8,128)(2,1)S(1)} %bitcast.101), channel_id=1, source_target_pairs={{8,0},{16,8},{24,16},{32,24},{40,32},{48,40},{56,48},{64,56},{72,6... | collective-permute-start | bytes 2359304 | tf_op jit(solution)/shard_map/ppermute | solution.py:20
  61.9 62.2 %collective-permute-start = (bf16[1024,384]{1,0:T(8,128)(2,1)S(1)}, bf16[1024,384]{1,0:T(8,128)(2,1)}, u32[]{:S(2)}, u32[]{:S(2)}) collective-permute-start(bf16[1024,384]{1,0:T(8,128)(2,1)S(1)} %bitcast.103), channel_id=1, source_target_pairs={{0,8},{8,16},{16,24},{24,32},{32,40},{40,48},{48,56},{56,64},{64,7... | collective-permute-start | bytes 2359304 | tf_op jit(solution)/shard_map/ppermute | solution.py:20
  63.9 60.3 %collective-permute-start.1 = (bf16[1024,384]{1,0:T(8,128)(2,1)S(1)}, bf16[1024,384]{1,0:T(8,128)(2,1)}, u32[]{:S(2)}, u32[]{:S(2)}) collective-permute-start(bf16[1024,384]{1,0:T(8,128)(2,1)S(1)} %bitcast.104), channel_id=1, source_target_pairs={{8,0},{16,8},{24,16},{32,24},{40,32},{48,40},{56,48},{64,56},{72,6... | collective-permute-start | bytes 2359304 | tf_op jit(solution)/shard_map/ppermute | solution.py:20
  75.6 42.7 %copy-start.3 = (bf16[1,8,128,384]{2,3,1,0:T(8,128)(2,1)S(1)}, bf16[1,8,128,384]{2,3,1,0:T(8,128)(2,1)}, u32[]{:S(2)}) copy-start(bf16[1,8,128,384]{2,3,1,0:T(8,128)(2,1)} %get-tuple-element.15) | copy-start | bytes 2359300
  77.3 42.2 %copy-start.2 = (bf16[1,8,128,384]{2,3,1,0:T(8,128)(2,1)S(1)}, bf16[1,8,128,384]{2,3,1,0:T(8,128)(2,1)}, u32[]{:S(2)}) copy-start(bf16[1,8,128,384]{2,3,1,0:T(8,128)(2,1)} %get-tuple-element.14) | copy-start | bytes 2359300
  168.5 128.8 %all-to-all-start.1 = ((bf16[2,1024,384]{2,0,1:T(2,128)(2,1)}), bf16[2,1024,384]{2,0,1:T(2,128)(2,1)S(1)}, u32[]{:S(2)}, u32[]{:S(2)}) async-start(bf16[2,1024,384]{2,0,1:T(2,128)(2,1)} %copy.159), calls=%async_computation.1 | async-start | bytes 3145728 | tf_op jit(solution)/shard_map/all_to_all | solution.py:310
  243.2 8.6 %copy-start.1 = (bf16[3328,384]{1,0:T(8,128)(2,1)S(1)}, bf16[3328,384]{1,0:T(8,128)(2,1)}, u32[]{:S(2)}) copy-start(bf16[3328,384]{1,0:T(8,128)(2,1)} %convert.9) | copy-start | bytes 7667716
  245.8 23.0 %collective-permute-start.4 = (bf16[1024,384]{1,0:T(8,128)(2,1)}, bf16[1024,384]{1,0:T(8,128)(2,1)}, u32[]{:S(2)}, u32[]{:S(2)}) collective-permute-start(bf16[1024,384]{1,0:T(8,128)(2,1)} %get-tuple-element.16), channel_id=1, source_target_pairs={{8,0},{16,8},{24,16},{32,24},{40,32},{48,40},{56,48},{64,56},{72,6... | collective-permute-start | bytes 2359304 | tf_op jit(solution)/shard_map/ppermute | solution.py:20
  249.8 33.8 %collective-permute-start.5 = (bf16[1024,384]{1,0:T(8,128)(2,1)S(1)}, bf16[1024,384]{1,0:T(8,128)(2,1)}, u32[]{:S(2)}, u32[]{:S(2)}) collective-permute-start(bf16[1024,384]{1,0:T(8,128)(2,1)S(1)} %get-tuple-element.17), channel_id=1, source_target_pairs={{0,8},{8,16},{16,24},{24,32},{32,40},{40,48},{48,56},{56,64},{64,7... | collective-permute-start | bytes 2359304 | tf_op jit(solution)/shard_map/ppermute | solution.py:20
  253.0 32.8 %collective-permute-start.6 = (bf16[1024,384]{1,0:T(8,128)(2,1)}, bf16[1024,384]{1,0:T(8,128)(2,1)}, u32[]{:S(2)}, u32[]{:S(2)}) collective-permute-start(bf16[1024,384]{1,0:T(8,128)(2,1)} %get-tuple-element.18), channel_id=1, source_target_pairs={{8,0},{16,8},{24,16},{32,24},{40,32},{48,40},{56,48},{64,56},{72,6... | collective-permute-start | bytes 2359304 | tf_op jit(solution)/shard_map/ppermute | solution.py:20
  260.9 31.1 %collective-permute-start.7 = (bf16[1024,384]{1,0:T(8,128)(2,1)}, bf16[1024,384]{1,0:T(8,128)(2,1)}, u32[]{:S(2)}, u32[]{:S(2)}) collective-permute-start(bf16[1024,384]{1,0:T(8,128)(2,1)} %get-tuple-element.19), channel_id=1, source_target_pairs={{0,8},{8,16},{16,24},{24,32},{32,40},{40,48},{48,56},{56,64},{64,7... | collective-permute-start | bytes 2359304 | tf_op jit(solution)/shard_map/ppermute | solution.py:20
  266.5 17.1 %copy-start = (f32[8,128,3,128]{3,2,1,0:T(4,128)S(1)}, f32[8,128,3,128]{3,2,1,0:T(4,128)}, u32[]{:S(2)}) copy-start(f32[8,128,3,128]{3,2,1,0:T(4,128)} %copy.172) | copy-start | bytes 4718596
  297.3 22.8 %all-to-all-start.2 = ((bf16[2,1024,384]{2,0,1:T(2,128)(2,1)}), bf16[2,1024,384]{2,0,1:T(2,128)(2,1)S(1)}, u32[]{:S(2)}, u32[]{:S(2)}) async-start(bf16[2,1024,384]{2,0,1:T(2,128)(2,1)} %copy.168), calls=%async_computation.2 | async-start | bytes 3145728 | tf_op jit(solution)/shard_map/all_to_all | solution.py:313
where the time goes:
time: 328 us; the launch traced here: 327 us
  Pallas kernels  126 us (38%)
  waiting for transfers between devices  63.6 us (19%)
  starting transfers between devices  61 us (19%)
  local copies, waits for them, and re-layouts  46.9 us (14%)
  other arithmetic  24.2 us (7%)
  matrix products  4.15 us (1%)
    pallas_call x2, Pallas kernels, butterfly_sum(): pl.pallas_call(functools.partial(reduce_kernel, count), out_shape=jax.Sha...  89.2 us
    pallas_call x1, Pallas kernels, attend(): pl.pallas_call(attention_kernel, out_shape=(jax.ShapeDtypeStruct((count,...  36.7 us
    all_to_all x1, waiting for transfers between devices, per_device(): lax.all_to_all(jnp.stack([query, keys, values, cotangent]), 'head', split...  36.3 us
    ppermute x8, starting transfers between devices, passed_along(): return lax.ppermute(block, axis, route)  35.5 us
    ppermute x8, waiting for transfers between devices, passed_along(): return lax.ppermute(block, axis, route)  21.1 us
    all_to_all x1, starting transfers between devices, per_device(): lax.all_to_all(jnp.stack([key_rows, value_rows]), 'head', split_axis=1, c...  9.96 us
    all_to_all x1, starting transfers between devices, per_device(): lax.all_to_all(jnp.stack([attended, query_rows]), 'head', split_axis=1, c...  9.67 us
    another operation x2, other arithmetic  8.4 us
  transfers between devices with their start and end apart: 11, of which 4 were waited for; matrix products, arithmetic and copies ran while one was open for 16% of the time, Pallas kernels for 27%

commit v1 on v0

--- a/solution.py
+++ b/solution.py
@@ -119,13 +119,16 @@
     return field.transpose(1, 2, 0, 3).reshape(count * TILE, heads * HD)
 
 
-def attention_kernel(index_ref, q_ref, do_ref, k_ref, v_ref, att_ref, dq_ref, dk_ref, dv_ref, kbuf, vbuf):
+def attention_kernel(
+    index_ref, q_ref, do_ref, k_ref, v_ref, att_ref, dq_ref, dk_ref, dv_ref, kbuf, vbuf, dkt, dvt
+):
     heads = q_ref.shape[1] // HD
     tiles = q_ref.shape[0] // TILE
     slots = index_ref.shape[0] // (heads * tiles)
+    pool_tiles = k_ref.shape[0] // TILE
     scale = HD ** (-0.5)
-    dk_ref[...] = jnp.zeros_like(dk_ref)
-    dv_ref[...] = jnp.zeros_like(dv_ref)
+    dkt[...] = jnp.zeros_like(dkt)
+    dvt[...] = jnp.zeros_like(dvt)
     nt = (((1,), (1,)), ((), ()))
     tn = (((0,), (0,)), ((), ()))
 
@@ -149,8 +152,8 @@
             lax.dot_general(query, chosen_keys, nt, preferred_element_type=jnp.float32) * scale
         )
         peak = jnp.max(scores, axis=1, keepdims=True)
-        log_total = peak + jnp.log(jnp.sum(jnp.exp(scores - peak), axis=1, keepdims=True))
-        probs = jnp.exp(scores - log_total)
+        lifted = jnp.exp(scores - peak)
+        probs = lifted * (1.0 / jnp.sum(lifted, axis=1, keepdims=True))
         weights = probs.astype(jnp.bfloat16)
         attended = jnp.dot(weights, chosen_values, preferred_element_type=jnp.float32).astype(
             jnp.bfloat16
@@ -167,15 +170,26 @@
             jnp.dot(grad_scores, chosen_keys, preferred_element_type=jnp.float32) * scale
         ).astype(jnp.bfloat16)
         key_slots = (
-            lax.dot_general(grad_scores, query, tn, preferred_element_type=jnp.float32) * scale
-        )
-        value_slots = lax.dot_general(weights, grad_out, tn, preferred_element_type=jnp.float32)
+            lax.dot_general(query, grad_scores, tn, preferred_element_type=jnp.float32) * scale
+        )
+        value_slots = lax.dot_general(grad_out, weights, tn, preferred_element_type=jnp.float32)
         for s in range(slots):
-            dk_ref[picks[s], cols] += key_slots[s * TILE : (s + 1) * TILE]
-            dv_ref[picks[s], cols] += value_slots[s * TILE : (s + 1) * TILE]
+            dkt[cols, picks[s]] += key_slots[:, s * TILE : (s + 1) * TILE]
+            dvt[cols, picks[s]] += value_slots[:, s * TILE : (s + 1) * TILE]
         return carry
 
     lax.fori_loop(0, heads * tiles, step, 0)
+
+    def flip(item, carry):
+        head = item // pool_tiles
+        tile = item % pool_tiles
+        cols = pl.ds(pl.multiple_of(head * HD, HD), HD)
+        rows = pl.ds(pl.multiple_of(tile * TILE, TILE), TILE)
+        dk_ref[rows, cols] = dkt[cols, rows].T
+        dv_ref[rows, cols] = dvt[cols, rows].T
+        return carry
+
+    lax.fori_loop(0, heads * pool_tiles, flip, 0)
 
 
 def attend(pool_index, query_rows, grad_rows, pool_keys, pool_values):
@@ -197,6 +211,8 @@
         scratch_shapes=[
             pltpu.VMEM((slots * TILE, HD), jnp.bfloat16),
             pltpu.VMEM((slots * TILE, HD), jnp.bfloat16),
+            pltpu.VMEM((width, pool_rows), jnp.float32),
+            pltpu.VMEM((width, pool_rows), jnp.float32),
         ],
         compiler_params=pltpu.CompilerParams(vmem_limit_bytes=60 * 1024 * 1024),
         cost_estimate=pl.CostEstimate(

time: 328 us -> 337 us (1.027)
  Pallas kernels: 126 us -> 135 us
    pallas_call x1, Pallas kernels: 36.7 us -> 45.5 us  [attend(): pl.pallas_call(attention_kernel, out_shape=(jax.ShapeDtypeStruct((count,...]
where the time goes in v1:
time: 337 us; the launch traced here: 336 us
  Pallas kernels  135 us (40%)
  waiting for transfers between devices  63.6 us (19%)
  starting transfers between devices  61 us (18%)
  local copies, waits for them, and re-layouts  46.9 us (14%)
  other arithmetic  24.2 us (7%)
  matrix products  4.16 us (1%)
    pallas_call x2, Pallas kernels, butterfly_sum(): pl.pallas_call(functools.partial(reduce_kernel, count), out_shape=jax.Sha...  89.2 us
    pallas_call x1, Pallas kernels, attend(): pl.pallas_call(attention_kernel, out_shape=(jax.ShapeDtypeStruct((count,...  45.5 us
    all_to_all x1, waiting for transfers between devices, per_device(): lax.all_to_all(jnp.stack([query, keys, values, cotangent]), 'head', split...  36.3 us
    ppermute x8, starting transfers between devices, passed_along(): return lax.ppermute(block, axis, route)  35.5 us
    ppermute x8, waiting for transfers between devices, passed_along(): return lax.ppermute(block, axis, route)  21.1 us
    all_to_all x1, starting transfers between devices, per_device(): lax.all_to_all(jnp.stack([key_rows, value_rows]), 'head', split_axis=1, c...  9.99 us
    all_to_all x1, starting transfers between devices, per_device(): lax.all_to_all(jnp.stack([attended, query_rows]), 'head', split_axis=1, c...  9.66 us
    another operation x2, other arithmetic  8.4 us
  transfers between devices with their start and end apart: 11, of which 4 were waited for; matrix products, arithmetic and copies ran while one was open for 16% of the time, Pallas kernels for 27%

profile of v1, /device:TPU:160, one launch (start us, length us, event | category | flops | bytes accessed | tf_op | source)
XLA Modules:
  0.0 335.6 jit_solution(2632954927828038428)
XLA Ops:
  0.6 2.0 pad_maximum_fusion
  2.7 3.6 %copy.147 = bf16[4,128,3072]{1,0,2:T(4,128)(2,1)} copy(bf16[4,128,3072]{2,1,0:T(8,128)(2,1)S(1)} %pad_maximum_fusion) | data formatting | bytes 6291456 | tf_op jit(solution)/shard_map/stack | solution.py:235
  6.3 5.9 %all-to-all-start = ((bf16[4,128,3072]{1,0,2:T(4,128)(2,1)}), bf16[4,128,3072]{1,0,2:T(4,128)(2,1)S(1)}, u32[]{:S(2)}, u32[]{:S(2)}) async-start(bf16[4,128,3072]{1,0,2:T(4,128)(2,1)} %copy.147), calls=%async_computation | async-start | bytes 6291456 | tf_op jit(solution)/shard_map/all_to_all | solution.py:234
  12.6 36.3 %all-to-all-done = bf16[4,128,3072]{1,0,2:T(4,128)(2,1)S(1)} async-done(((bf16[4,128,3072]{1,0,2:T(4,128)(2,1)}), bf16[4,128,3072]{1,0,2:T(4,128)(2,1)S(1)}, u32[]{:S(2)}, u32[]{:S(2)}) %all-to-all-start) | async-done | bytes 3145760 | tf_op jit(solution)/shard_map/all_to_all | solution.py:234
  51.1 1.9 collective-permute-start.2
  53.1 7.9 %collective-permute-start.3 = (bf16[1024,384]{1,0:T(8,128)(2,1)S(1)}, bf16[1024,384]{1,0:T(8,128)(2,1)}, u32[]{:S(2)}, u32[]{:S(2)}) collective-permute-start(bf16[1024,384]{1,0:T(8,128)(2,1)S(1)} %bitcast.101), channel_id=1, source_target_pairs={{8,0},{16,8},{24,16},{32,24},{40,32},{48,40},{56,48},{64,56},{72,6... | collective-permute-start | bytes 2359304 | tf_op jit(solution)/shard_map/ppermute | solution.py:20
  61.9 1.9 collective-permute-start
  63.9 8.0 %collective-permute-start.1 = (bf16[1024,384]{1,0:T(8,128)(2,1)S(1)}, bf16[1024,384]{1,0:T(8,128)(2,1)}, u32[]{:S(2)}, u32[]{:S(2)}) collective-permute-start(bf16[1024,384]{1,0:T(8,128)(2,1)S(1)} %bitcast.104), channel_id=1, source_target_pairs={{8,0},{16,8},{24,16},{32,24},{40,32},{48,40},{56,48},{64,56},{72,6... | collective-permute-start | bytes 2359304 | tf_op jit(solution)/shard_map/ppermute | solution.py:20
  77.3 2.1 reshape.63.x_ref
  79.4 36.1 %shard_map.84 = bf16[32,48,128]{2,1,0:T(8,128)(2,1)} custom-call(bf16[32,48,128]{2,1,0:T(8,128)(2,1)} %reshape.63.x_ref), custom_call_target="tpu_custom_call" | custom-call | tf_op jit(solution)/shard_map/pallas_call | solution.py:92
  122.4 1.8 pad_maximum_fusion.2.v_ref
  127.5 45.5 %shard_map.85 = (bf16[1024,384]{1,0:T(8,128)(2,1)}, bf16[1024,384]{1,0:T(8,128)(2,1)}, f32[3328,384]{1,0:T(8,128)}, f32[3328,384]{1,0:T(8,128)}) custom-call(s32[216]{0:T(256)} %reshape.61.index_ref, bf16[1024,384]{1,0:T(8,128)(2,1)} %bitcast.114, bf16[1024,384]{1,0:T(8,128)(2,1)} %bitcast.115, bf16[3328,384]{1,0:T(8,128)(2,1)} %pad_maximum_fusion.1.k_ref, ...), custom_call_target="tpu_custom_call" | custom-call | flops 6341787648 | bytes 18481152 | tf_op jit(solution)/shard_map/pallas_call | solution.py:201
  174.6 2.8 copy.159
  177.4 9.7 %all-to-all-start.1 = ((bf16[2,1024,384]{2,0,1:T(2,128)(2,1)}), bf16[2,1024,384]{2,0,1:T(2,128)(2,1)S(1)}, u32[]{:S(2)}, u32[]{:S(2)}) async-start(bf16[2,1024,384]{2,0,1:T(2,128)(2,1)} %copy.159), calls=%async_computation.1 | async-start | bytes 3145728 | tf_op jit(solution)/shard_map/all_to_all | solution.py:326
  187.0 4.2 %convert.8 = bf16[3328,384]{1,0:T(8,128)(2,1)} convert(f32[3328,384]{1,0:T(8,128)} %get-tuple-element.10) | non-fusion elementwise | flops 1277952 | bytes 7667712 | tf_op jit(solution)/shard_map/convert.3
  191.2 4.2 %convert.9 = bf16[3328,384]{1,0:T(8,128)(2,1)} convert(f32[3328,384]{1,0:T(8,128)} %get-tuple-element.11) | non-fusion elementwise | flops 1277952 | bytes 7667712 | tf_op jit(solution)/shard_map/convert.1
  197.6 53.1 %shard_map.86 = f32[32,48,128]{2,1,0:T(8,128)} custom-call(f32[32,48,128]{2,1,0:T(8,128)} %reshape_reshape.3.x_ref), custom_call_target="tpu_custom_call" | custom-call | tf_op jit(solution)/shard_map/pallas_call | solution.py:92
  252.1 2.6 fusion.25
  254.6 4.0 %collective-permute-start.4 = (bf16[1024,384]{1,0:T(8,128)(2,1)}, bf16[1024,384]{1,0:T(8,128)(2,1)}, u32[]{:S(2)}, u32[]{:S(2)}) collective-permute-start(bf16[1024,384]{1,0:T(8,128)(2,1)} %get-tuple-element.16), channel_id=1, source_target_pairs={{8,0},{16,8},{24,16},{32,24},{40,32},{48,40},{56,48},{64,56},{72,6... | collective-permute-start | bytes 2359304 | tf_op jit(solution)/shard_map/ppermute | solution.py:20
  258.7 1.9 collective-permute-start.5
  261.9 7.9 %collective-permute-start.6 = (bf16[1024,384]{1,0:T(8,128)(2,1)}, bf16[1024,384]{1,0:T(8,128)(2,1)}, u32[]{:S(2)}, u32[]{:S(2)}) collective-permute-start(bf16[1024,384]{1,0:T(8,128)(2,1)} %get-tuple-element.18), channel_id=1, source_target_pairs={{8,0},{16,8},{24,16},{32,24},{40,32},{48,40},{56,48},{64,56},{72,6... | collective-permute-start | bytes 2359304 | tf_op jit(solution)/shard_map/ppermute | solution.py:20
  269.8 1.9 collective-permute-start.7
  272.8 2.4 copy.172
  277.6 14.9 %collective-permute-done.5 = bf16[1024,384]{1,0:T(8,128)(2,1)} collective-permute-done((bf16[1024,384]{1,0:T(8,128)(2,1)S(1)}, bf16[1024,384]{1,0:T(8,128)(2,1)}, u32[]{:S(2)}, u32[]{:S(2)}) %collective-permute-start.5) | collective-permute-done | bytes 786464 | tf_op jit(solution)/shard_map/ppermute | solution.py:20
  292.5 2.3 fusion.4
  294.7 6.2 %collective-permute-done.7 = bf16[1024,384]{1,0:T(8,128)(2,1)} collective-permute-done((bf16[1024,384]{1,0:T(8,128)(2,1)}, bf16[1024,384]{1,0:T(8,128)(2,1)}, u32[]{:S(2)}, u32[]{:S(2)}) %collective-permute-start.7) | collective-permute-done | bytes 786464 | tf_op jit(solution)/shard_map/ppermute | solution.py:20
  300.9 2.3 fusion.5
  303.3 2.8 copy.168
  306.1 10.0 %all-to-all-start.2 = ((bf16[2,1024,384]{2,0,1:T(2,128)(2,1)}), bf16[2,1024,384]{2,0,1:T(2,128)(2,1)S(1)}, u32[]{:S(2)}, u32[]{:S(2)}) async-start(bf16[2,1024,384]{2,0,1:T(2,128)(2,1)} %copy.168), calls=%async_computation.2 | async-start | bytes 3145728 | tf_op jit(solution)/shard_map/all_to_all | solution.py:329
  316.1 2.9 fusion.28
  322.8 6.2 %all-to-all-done.2 = bf16[2,1024,384]{2,0,1:T(2,128)(2,1)S(1)} async-done(((bf16[2,1024,384]{2,0,1:T(2,128)(2,1)}), bf16[2,1024,384]{2,0,1:T(2,128)(2,1)S(1)}, u32[]{:S(2)}, u32[]{:S(2)}) %all-to-all-start.2) | async-done | bytes 1572896 | tf_op jit(solution)/shard_map/all_to_all | solution.py:329
  329.0 2.9 fusion.27
  (63 shorter events, 36.6 us)
Async XLA Ops:
  6.3 5.9 %copy-start.4 = (s32[3,256,9]{1,0,2:T(4,128)S(1)}, s32[3,256,9]{1,0,2:T(4,128)}, u32[]{:S(2)}) copy-start(s32[3,256,9]{1,0,2:T(4,128)} %param.9) | copy-start | bytes 82948
  6.3 42.6 %all-to-all-start = ((bf16[4,128,3072]{1,0,2:T(4,128)(2,1)}), bf16[4,128,3072]{1,0,2:T(4,128)(2,1)S(1)}, u32[]{:S(2)}, u32[]{:S(2)}) async-start(bf16[4,128,3072]{1,0,2:T(4,128)(2,1)} %copy.147), calls=%async_computation | async-start | bytes 6291456 | tf_op jit(solution)/shard_map/all_to_all | solution.py:234
  51.1 69.6 %collective-permute-start.2 = (bf16[1024,384]{1,0:T(8,128)(2,1)S(1)}, bf16[1024,384]{1,0:T(8,128)(2,1)}, u32[]{:S(2)}, u32[]{:S(2)}) collective-permute-start(bf16[1024,384]{1,0:T(8,128)(2,1)S(1)} %bitcast.100), channel_id=1, source_target_pairs={{0,8},{8,16},{16,24},{24,32},{32,40},{40,48},{48,56},{56,64},{64,7... | collective-permute-start | bytes 2359304 | tf_op jit(solution)/shard_map/ppermute | solution.py:20
  53.1 67.6 %collective-permute-start.3 = (bf16[1024,384]{1,0:T(8,128)(2,1)S(1)}, bf16[1024,384]{1,0:T(8,128)(2,1)}, u32[]{:S(2)}, u32[]{:S(2)}) collective-permute-start(bf16[1024,384]{1,0:T(8,128)(2,1)S(1)} %bitcast.101), channel_id=1, source_target_pairs={{8,0},{16,8},{24,16},{32,24},{40,32},{48,40},{56,48},{64,56},{72,6... | collective-permute-start | bytes 2359304 | tf_op jit(solution)/shard_map/ppermute | solution.py:20
  61.9 62.2 %collective-permute-start = (bf16[1024,384]{1,0:T(8,128)(2,1)S(1)}, bf16[1024,384]{1,0:T(8,128)(2,1)}, u32[]{:S(2)}, u32[]{:S(2)}) collective-permute-start(bf16[1024,384]{1,0:T(8,128)(2,1)S(1)} %bitcast.103), channel_id=1, source_target_pairs={{0,8},{8,16},{16,24},{24,32},{32,40},{40,48},{48,56},{56,64},{64,7... | collective-permute-start | bytes 2359304 | tf_op jit(solution)/shard_map/ppermute | solution.py:20
  63.9 60.3 %collective-permute-start.1 = (bf16[1024,384]{1,0:T(8,128)(2,1)S(1)}, bf16[1024,384]{1,0:T(8,128)(2,1)}, u32[]{:S(2)}, u32[]{:S(2)}) collective-permute-start(bf16[1024,384]{1,0:T(8,128)(2,1)S(1)} %bitcast.104), channel_id=1, source_target_pairs={{8,0},{16,8},{24,16},{32,24},{40,32},{48,40},{56,48},{64,56},{72,6... | collective-permute-start | bytes 2359304 | tf_op jit(solution)/shard_map/ppermute | solution.py:20
  75.6 42.7 %copy-start.3 = (bf16[1,8,128,384]{2,3,1,0:T(8,128)(2,1)S(1)}, bf16[1,8,128,384]{2,3,1,0:T(8,128)(2,1)}, u32[]{:S(2)}) copy-start(bf16[1,8,128,384]{2,3,1,0:T(8,128)(2,1)} %get-tuple-element.15) | copy-start | bytes 2359300
  77.3 42.2 %copy-start.2 = (bf16[1,8,128,384]{2,3,1,0:T(8,128)(2,1)S(1)}, bf16[1,8,128,384]{2,3,1,0:T(8,128)(2,1)}, u32[]{:S(2)}) copy-start(bf16[1,8,128,384]{2,3,1,0:T(8,128)(2,1)} %get-tuple-element.14) | copy-start | bytes 2359300
  177.4 128.8 %all-to-all-start.1 = ((bf16[2,1024,384]{2,0,1:T(2,128)(2,1)}), bf16[2,1024,384]{2,0,1:T(2,128)(2,1)S(1)}, u32[]{:S(2)}, u32[]{:S(2)}) async-start(bf16[2,1024,384]{2,0,1:T(2,128)(2,1)} %copy.159), calls=%async_computation.1 | async-start | bytes 3145728 | tf_op jit(solution)/shard_map/all_to_all | solution.py:326
  252.1 8.5 %copy-start.1 = (bf16[3328,384]{1,0:T(8,128)(2,1)S(1)}, bf16[3328,384]{1,0:T(8,128)(2,1)}, u32[]{:S(2)}) copy-start(bf16[3328,384]{1,0:T(8,128)(2,1)} %convert.9) | copy-start | bytes 7667716
  254.6 23.0 %collective-permute-start.4 = (bf16[1024,384]{1,0:T(8,128)(2,1)}, bf16[1024,384]{1,0:T(8,128)(2,1)}, u32[]{:S(2)}, u32[]{:S(2)}) collective-permute-start(bf16[1024,384]{1,0:T(8,128)(2,1)} %get-tuple-element.16), channel_id=1, source_target_pairs={{8,0},{16,8},{24,16},{32,24},{40,32},{48,40},{56,48},{64,56},{72,6... | collective-permute-start | bytes 2359304 | tf_op jit(solution)/shard_map/ppermute | solution.py:20
  258.7 33.8 %collective-permute-start.5 = (bf16[1024,384]{1,0:T(8,128)(2,1)S(1)}, bf16[1024,384]{1,0:T(8,128)(2,1)}, u32[]{:S(2)}, u32[]{:S(2)}) collective-permute-start(bf16[1024,384]{1,0:T(8,128)(2,1)S(1)} %get-tuple-element.17), channel_id=1, source_target_pairs={{0,8},{8,16},{16,24},{24,32},{32,40},{40,48},{48,56},{56,64},{64,7... | collective-permute-start | bytes 2359304 | tf_op jit(solution)/shard_map/ppermute | solution.py:20
  261.9 32.8 %collective-permute-start.6 = (bf16[1024,384]{1,0:T(8,128)(2,1)}, bf16[1024,384]{1,0:T(8,128)(2,1)}, u32[]{:S(2)}, u32[]{:S(2)}) collective-permute-start(bf16[1024,384]{1,0:T(8,128)(2,1)} %get-tuple-element.18), channel_id=1, source_target_pairs={{8,0},{16,8},{24,16},{32,24},{40,32},{48,40},{56,48},{64,56},{72,6... | collective-permute-start | bytes 2359304 | tf_op jit(solution)/shard_map/ppermute | solution.py:20
  269.8 31.1 %collective-permute-start.7 = (bf16[1024,384]{1,0:T(8,128)(2,1)}, bf16[1024,384]{1,0:T(8,128)(2,1)}, u32[]{:S(2)}, u32[]{:S(2)}) collective-permute-start(bf16[1024,384]{1,0:T(8,128)(2,1)} %get-tuple-element.19), channel_id=1, source_target_pairs={{0,8},{8,16},{16,24},{24,32},{32,40},{40,48},{48,56},{56,64},{64,7... | collective-permute-start | bytes 2359304 | tf_op jit(solution)/shard_map/ppermute | solution.py:20
  275.4 17.1 %copy-start = (f32[8,128,3,128]{3,2,1,0:T(4,128)S(1)}, f32[8,128,3,128]{3,2,1,0:T(4,128)}, u32[]{:S(2)}) copy-start(f32[8,128,3,128]{3,2,1,0:T(4,128)} %copy.172) | copy-start | bytes 4718596
  306.1 22.8 %all-to-all-start.2 = ((bf16[2,1024,384]{2,0,1:T(2,128)(2,1)}), bf16[2,1024,384]{2,0,1:T(2,128)(2,1)S(1)}, u32[]{:S(2)}, u32[]{:S(2)}) async-start(bf16[2,1024,384]{2,0,1:T(2,128)(2,1)} %copy.168), calls=%async_computation.2 | async-start | bytes 3145728 | tf_op jit(solution)/shard_map/all_to_all | solution.py:329

commit v2 on v0

--- a/solution.py
+++ b/solution.py
@@ -106,6 +106,153 @@
         compiler_params=pltpu.CompilerParams(collective_id=collective, has_side_effects=True),
     )(pieces)
     return summed.reshape(block.shape)
+
+
+def swap_kernel(count, x_ref, down_ref, up_ref, out_ref, above_ref, below_ref, *scratch):
+    inbox, gathered, mine, send_sem, recv_sem, back_send, back_recv = scratch[:7]
+    from_above, from_below, near_send, near_recv = scratch[7:]
+    me = lax.axis_index("blk")
+    column = lax.axis_index("head")
+    barrier = pltpu.get_barrier_semaphore()
+    for k in range(1, count):
+        pl.semaphore_signal(
+            barrier, 1, device_id=(lax.rem(me + k, count), column), device_id_type=MESH
+        )
+    pl.semaphore_wait(barrier, count - 1)
+
+    def downward():
+        return pltpu.make_async_remote_copy(
+            src_ref=down_ref,
+            dst_ref=from_above,
+            send_sem=near_send.at[0],
+            recv_sem=near_recv.at[0],
+            device_id=(me - 1, column),
+            device_id_type=MESH,
+        )
+
+    def upward():
+        return pltpu.make_async_remote_copy(
+            src_ref=up_ref,
+            dst_ref=from_below,
+            send_sem=near_send.at[1],
+            recv_sem=near_recv.at[1],
+            device_id=(me + 1, column),
+            device_id_type=MESH,
+        )
+
+    @pl.when(me > 0)
+    def _():
+        downward().start()
+
+    @pl.when(me < count - 1)
+    def _():
+        upward().start()
+
+    outgoing = []
+    for k in range(1, count):
+        peer = lax.rem(me + k, count)
+        copy = pltpu.make_async_remote_copy(
+            src_ref=x_ref.at[peer],
+            dst_ref=inbox.at[me],
+            send_sem=send_sem.at[k],
+            recv_sem=recv_sem.at[me],
+            device_id=(peer, column),
+            device_id_type=MESH,
+        )
+        copy.start()
+        outgoing.append(copy)
+    total = x_ref[me].astype(jnp.float32)
+    for k in range(1, count):
+        source = lax.rem(me + count - k, count)
+        pltpu.make_async_remote_copy(
+            src_ref=x_ref.at[source],
+            dst_ref=inbox.at[source],
+            send_sem=send_sem.at[k],
+            recv_sem=recv_sem.at[source],
+            device_id=(source, column),
+            device_id_type=MESH,
+        ).wait_recv()
+        total = total + inbox[source].astype(jnp.float32)
+    mine[...] = total.astype(mine.dtype)
+    for k in range(1, count):
+        peer = lax.rem(me + k, count)
+        copy = pltpu.make_async_remote_copy(
+            src_ref=mine,
+            dst_ref=gathered.at[me],
+            send_sem=back_send.at[k],
+            recv_sem=back_recv.at[me],
+            device_id=(peer, column),
+            device_id_type=MESH,
+        )
+        copy.start()
+        outgoing.append(copy)
+    gathered[me] = mine[...]
+    for k in range(1, count):
+        source = lax.rem(me + count - k, count)
+        pltpu.make_async_remote_copy(
+            src_ref=mine,
+            dst_ref=gathered.at[source],
+            send_sem=back_send.at[k],
+            recv_sem=back_recv.at[source],
+            device_id=(source, column),
+            device_id_type=MESH,
+        ).wait_recv()
+    for copy in outgoing:
+        copy.wait_send()
+    out_ref[...] = gathered[...]
+
+    @pl.when(me > 0)
+    def _():
+        downward().wait_send()
+        upward().wait_recv()
+        below_ref[...] = from_below[...]
+
+    @pl.when(me == 0)
+    def _():
+        below_ref[...] = jnp.zeros_like(below_ref)
+
+    @pl.when(me < count - 1)
+    def _():
+        upward().wait_send()
+        downward().wait_recv()
+        above_ref[...] = from_above[...]
+
+    @pl.when(me == count - 1)
+    def _():
+        above_ref[...] = jnp.zeros_like(above_ref)
+
+
+def sum_and_swap(block, down, up, axis, collective):
+    count = lax.axis_size(axis)
+    pieces = block.reshape(count, -1, 128)
+    vmem = pltpu.VMEM
+    summed, above, below = pl.pallas_call(
+        functools.partial(swap_kernel, count),
+        out_shape=(
+            jax.ShapeDtypeStruct(pieces.shape, pieces.dtype),
+            jax.ShapeDtypeStruct(down.shape, down.dtype),
+            jax.ShapeDtypeStruct(up.shape, up.dtype),
+        ),
+        in_specs=[pl.BlockSpec(memory_space=vmem)] * 3,
+        out_specs=tuple(pl.BlockSpec(memory_space=vmem) for _ in range(3)),
+        scratch_shapes=[
+            pltpu.VMEM(pieces.shape, pieces.dtype),
+            pltpu.VMEM(pieces.shape, pieces.dtype),
+            pltpu.VMEM(pieces.shape[1:], pieces.dtype),
+            pltpu.SemaphoreType.DMA((count,)),
+            pltpu.SemaphoreType.DMA((count,)),
+            pltpu.SemaphoreType.DMA((count,)),
+            pltpu.SemaphoreType.DMA((count,)),
+            pltpu.VMEM(down.shape, down.dtype),
+            pltpu.VMEM(up.shape, up.dtype),
+            pltpu.SemaphoreType.DMA((2,)),
+            pltpu.SemaphoreType.DMA((2,)),
+        ],
+        compiler_params=pltpu.CompilerParams(
+            collective_id=collective, has_side_effects=True, vmem_limit_bytes=48 * 1024 * 1024
+        ),
+    )(pieces, down, up)
+    return summed.reshape(block.shape), above, below
 
 
 def split_heads(field, count):
@@ -267,37 +414,23 @@
     centre = reach * frame_rows
     key_grad = key_pool[centre : centre + frame_rows]
     value_grad = value_pool[centre : centre + frame_rows]
-    offset = 1
-    lower = (reach - offset) * frame_rows
-    returned = (
-        passed_along(
-            key_pool[lower : lower + frame_rows].astype(jnp.bfloat16), "blk", -offset
-        ).astype(jnp.float32),
-        passed_along(
-            value_pool[lower : lower + frame_rows].astype(jnp.bfloat16), "blk", -offset
-        ).astype(jnp.float32),
-    )
+    lower = (reach - 1) * frame_rows
+    upper = (reach + 1) * frame_rows
+    down = jnp.stack([key_pool[lower : lower + frame_rows], value_pool[lower : lower + frame_rows]])
+    up = jnp.stack([key_pool[upper : upper + frame_rows], value_pool[upper : upper + frame_rows]])
+    pool_end = span * TILE
+    summed, above, below = sum_and_swap(
+        jnp.stack([key_pool[pool_end:], value_pool[pool_end:]]).reshape(
+            2, GLOBALS, TILE, heads, HD
+        ),
+        down.astype(jnp.bfloat16),
+        up.astype(jnp.bfloat16),
+        "blk",
+        1,
+    )
+    returned = above.astype(jnp.float32) + below.astype(jnp.float32)
     key_grad = key_grad + returned[0]
     value_grad = value_grad + returned[1]
-    upper = (reach + offset) * frame_rows
-    returned = (
-        passed_along(
-            key_pool[upper : upper + frame_rows].astype(jnp.bfloat16), "blk", offset
-        ).astype(jnp.float32),
-        passed_along(
-            value_pool[upper : upper + frame_rows].astype(jnp.bfloat16), "blk", offset
-        ).astype(jnp.float32),
-    )
-    key_grad = key_grad + returned[0]
-    value_grad = value_grad + returned[1]
-    pool_end = span * TILE
-    summed = butterfly_sum(
-        jnp.stack([key_pool[pool_end:], value_pool[pool_end:]]).reshape(
-            2, GLOBALS, TILE, heads, HD
-        ),
-        "blk",
-        1,
-    )
     owner_float = owner.astype(jnp.float32)
     key_grad = key_grad + jnp.einsum(
         "hjt,jkhd->tkhd", owner_float, summed[0], precision=lax.Precision.HIGHEST

time: 328 us -> 333 us (1.015)
  the two profiles are of different devices: /device:TPU:160 before, /device:TPU:24 now
where the time goes in v2:
time: 333 us
  Pallas kernels  183 us (55%)
  waiting for transfers between devices  49.4 us (15%)
  local copies, waits for them, and re-layouts  44.5 us (13%)
  starting transfers between devices  27 us (8%)
  other arithmetic  22.5 us (7%)
  matrix products  5.35 us (2%)
    pallas_call x1, Pallas kernels, sum_and_swap(): pl.pallas_call(functools.partial(swap_kernel, count), out_shape=(jax.Shap...  95.4 us
    pallas_call x1, Pallas kernels, butterfly_sum(): pl.pallas_call(functools.partial(reduce_kernel, count), out_shape=jax.Sha...  50.7 us
    all_to_all x1, waiting for transfers between devices, per_device(): lax.all_to_all(jnp.stack([query, keys, values, cotangent]), 'head', split...  36.9 us
    pallas_call x1, Pallas kernels, attend(): pl.pallas_call(attention_kernel, out_shape=(jax.ShapeDtypeStruct((count,...  36.7 us
    all_to_all x1, waiting for transfers between devices, per_device(): lax.all_to_all(jnp.stack([key_rows, value_rows]), 'head', split_axis=1, c...  12.5 us
    ppermute x4, starting transfers between devices, passed_along(): return lax.ppermute(block, axis, route)  12.3 us
  transfers between devices with their start and end apart: 7, of which 2 were waited for; matrix products, arithmetic and copies ran while one was open for 15% of the time, Pallas kernels for 44%

profile of v2, /device:TPU:24, one launch (start us, length us, event | category | flops | bytes accessed | tf_op | source)
XLA Modules:
  0.0 332.5 jit_solution(3714948679739443672)
XLA Ops:
  0.6 2.0 pad_maximum_fusion
  2.7 3.7 %copy.147 = bf16[4,128,3072]{1,0,2:T(4,128)(2,1)} copy(bf16[4,128,3072]{2,1,0:T(8,128)(2,1)S(1)} %pad_maximum_fusion) | data formatting | bytes 6291456 | tf_op jit(solution)/shard_map/stack | solution.py:366
  6.3 5.8 %all-to-all-start = ((bf16[4,128,3072]{1,0,2:T(4,128)(2,1)}), bf16[4,128,3072]{1,0,2:T(4,128)(2,1)S(1)}, u32[]{:S(2)}, u32[]{:S(2)}) async-start(bf16[4,128,3072]{1,0,2:T(4,128)(2,1)} %copy.147), calls=%async_computation | async-start | bytes 6291456 | tf_op jit(solution)/shard_map/all_to_all | solution.py:365
  12.5 36.9 %all-to-all-done = bf16[4,128,3072]{1,0,2:T(4,128)(2,1)S(1)} async-done(((bf16[4,128,3072]{1,0,2:T(4,128)(2,1)}), bf16[4,128,3072]{1,0,2:T(4,128)(2,1)S(1)}, u32[]{:S(2)}, u32[]{:S(2)}) %all-to-all-start) | async-done | bytes 3145760 | tf_op jit(solution)/shard_map/all_to_all | solution.py:365
  49.8 1.4 fusion.26
  51.6 2.0 collective-permute-start.3
  53.6 2.4 collective-permute-start.2
  57.0 3.2 collective-permute-start.1
  60.2 4.8 %collective-permute-start = (bf16[1024,384]{1,0:T(8,128)(2,1)S(1)}, bf16[1024,384]{1,0:T(8,128)(2,1)}, u32[]{:S(2)}, u32[]{:S(2)}) collective-permute-start(bf16[1024,384]{1,0:T(8,128)(2,1)S(1)} %bitcast.129), channel_id=1, source_target_pairs={{0,8},{8,16},{16,24},{24,32},{32,40},{40,48},{48,56},{56,64},{64,7... | collective-permute-start | bytes 2359304 | tf_op jit(solution)/shard_map/ppermute | solution.py:20
  67.6 1.5 fusion.5
  69.1 1.6 fusion.4
  72.5 2.0 reshape.63.x_ref
  74.5 50.7 %shard_map.84 = bf16[32,48,128]{2,1,0:T(8,128)(2,1)} custom-call(bf16[32,48,128]{2,1,0:T(8,128)(2,1)} %reshape.63.x_ref), custom_call_target="tpu_custom_call" | custom-call | tf_op jit(solution)/shard_map/pallas_call | solution.py:92
  128.7 1.7 pad_maximum_fusion.4
  130.4 1.8 pad_maximum_fusion.2.v_ref
  132.2 1.7 pad_maximum_fusion.3
  133.9 1.7 pad_maximum_fusion.1.k_ref
  135.6 36.7 %shard_map.85 = (bf16[1024,384]{1,0:T(8,128)(2,1)}, bf16[1024,384]{1,0:T(8,128)(2,1)}, f32[3328,384]{1,0:T(8,128)}, f32[3328,384]{1,0:T(8,128)}) custom-call(s32[216]{0:T(256)} %reshape.61.index_ref, bf16[1024,384]{1,0:T(8,128)(2,1)} %bitcast.140, bf16[1024,384]{1,0:T(8,128)(2,1)} %bitcast.139, bf16[3328,384]{1,0:T(8,128)(2,1)} %pad_maximum_fusion.1.k_ref, ...), custom_call_target="tpu_custom_call" | custom-call | flops 6341787648 | bytes 18481152 | tf_op jit(solution)/shard_map/pallas_call | solution.py:334
  172.3 1.5 pad_maximum_fusion.5
  173.9 2.8 copy.159
  176.7 4.5 %all-to-all-start.1 = ((bf16[2,1024,384]{2,0,1:T(2,128)(2,1)}), bf16[2,1024,384]{2,0,1:T(2,128)(2,1)}, u32[]{:S(2)}, u32[]{:S(2)}) async-start(bf16[2,1024,384]{2,0,1:T(2,128)(2,1)} %copy.159), calls=%async_computation.1 | async-start | bytes 3145728 | tf_op jit(solution)/shard_map/all_to_all | solution.py:443
  182.5 4.3 %convert.16 = bf16[3328,384]{1,0:T(8,128)(2,1)} convert(f32[3328,384]{1,0:T(8,128)} %get-tuple-element.13) | non-fusion elementwise | flops 1277952 | bytes 7667712 | tf_op jit(solution)/shard_map/convert.11
  186.9 1.8 convert.17
  188.8 1.7 slice_bitcast_fusion.3
  191.2 2.1 pad_maximum_fusion.6
  193.3 95.4 %shard_map.86 = (f32[32,48,128]{2,1,0:T(8,128)S(1)}, bf16[2,1024,384]{2,1,0:T(8,128)(2,1)S(1)}, bf16[2,1024,384]{2,1,0:T(8,128)(2,1)S(1)}) custom-call(f32[32,48,128]{2,1,0:T(8,128)S(1)} %reshape_reshape.3.x_ref, bf16[2,1024,384]{2,1,0:T(8,128)(2,1)} %get-tuple-element.38.down_ref, bf16[2,1024,384]{2,1,0:T(8,128)(2,1)} %get-tuple-element.39.up_ref), custom_call_target="tpu_custom_call" | custom-call | tf_op jit(solution)/shard_map/pallas_call | solution.py:229
  295.0 2.6 fusion.6
  297.8 2.8 copy.168
  300.6 4.4 %all-to-all-start.2 = ((bf16[2,1024,384]{2,0,1:T(2,128)(2,1)}), bf16[2,1024,384]{2,0,1:T(2,128)(2,1)S(1)}, u32[]{:S(2)}, u32[]{:S(2)}) async-start(bf16[2,1024,384]{2,0,1:T(2,128)(2,1)} %copy.168), calls=%async_computation.2 | async-start | bytes 3145728 | tf_op jit(solution)/shard_map/all_to_all | solution.py:446
  305.0 4.7 %fusion.28 = (bf16[1,128,8,384]{3,0,1,2:T(2,128)(2,1)S(1)}, bf16[1,128,8,384]{3,0,1,2:T(2,128)(2,1)S(1)}) fusion(bf16[2,128,8,384]{3,0,1,2:T(2,128)(2,1)} %bitcast.31), kind=kLoop, calls=%fused_computation.58 | loop fusion | bytes 3145728 | tf_op jit(solution)/shard_map/slice | solution.py:449
  313.4 12.5 %all-to-all-done.2 = bf16[2,1024,384]{2,0,1:T(2,128)(2,1)S(1)} async-done(((bf16[2,1024,384]{2,0,1:T(2,128)(2,1)}), bf16[2,1024,384]{2,0,1:T(2,128)(2,1)S(1)}, u32[]{:S(2)}, u32[]{:S(2)}) %all-to-all-start.2) | async-done | bytes 1572896 | tf_op jit(solution)/shard_map/all_to_all | solution.py:446
  325.9 2.9 fusion.27
  (63 shorter events, 26.0 us)
Async XLA Ops:
  6.3 5.8 %copy-start.5 = (s32[3,256,9]{1,0,2:T(4,128)S(1)}, s32[3,256,9]{1,0,2:T(4,128)}, u32[]{:S(2)}) copy-start(s32[3,256,9]{1,0,2:T(4,128)} %param.9) | copy-start | bytes 82948
  6.3 43.1 %all-to-all-start = ((bf16[4,128,3072]{1,0,2:T(4,128)(2,1)}), bf16[4,128,3072]{1,0,2:T(4,128)(2,1)S(1)}, u32[]{:S(2)}, u32[]{:S(2)}) async-start(bf16[4,128,3072]{1,0,2:T(4,128)(2,1)} %copy.147), calls=%async_computation | async-start | bytes 6291456 | tf_op jit(solution)/shard_map/all_to_all | solution.py:365
  51.6 77.1 %collective-permute-start.3 = (bf16[1024,384]{1,0:T(8,128)(2,1)S(1)}, bf16[1024,384]{1,0:T(8,128)(2,1)}, u32[]{:S(2)}, u32[]{:S(2)}) collective-permute-start(bf16[1024,384]{1,0:T(8,128)(2,1)S(1)} %bitcast.125), channel_id=1, source_target_pairs={{8,0},{16,8},{24,16},{32,24},{40,32},{48,40},{56,48},{64,56},{72,6... | collective-permute-start | bytes 2359304 | tf_op jit(solution)/shard_map/ppermute | solution.py:20
  53.6 75.2 %collective-permute-start.2 = (bf16[1024,384]{1,0:T(8,128)(2,1)S(1)}, bf16[1024,384]{1,0:T(8,128)(2,1)}, u32[]{:S(2)}, u32[]{:S(2)}) collective-permute-start(bf16[1024,384]{1,0:T(8,128)(2,1)S(1)} %bitcast.126), channel_id=1, source_target_pairs={{0,8},{8,16},{16,24},{24,32},{32,40},{40,48},{48,56},{56,64},{64,7... | collective-permute-start | bytes 2359304 | tf_op jit(solution)/shard_map/ppermute | solution.py:20
  57.0 75.2 %collective-permute-start.1 = (bf16[1024,384]{1,0:T(8,128)(2,1)S(1)}, bf16[1024,384]{1,0:T(8,128)(2,1)}, u32[]{:S(2)}, u32[]{:S(2)}) collective-permute-start(bf16[1024,384]{1,0:T(8,128)(2,1)S(1)} %bitcast.128), channel_id=1, source_target_pairs={{8,0},{16,8},{24,16},{32,24},{40,32},{48,40},{56,48},{64,56},{72,6... | collective-permute-start | bytes 2359304 | tf_op jit(solution)/shard_map/ppermute | solution.py:20
  60.2 72.0 %collective-permute-start = (bf16[1024,384]{1,0:T(8,128)(2,1)S(1)}, bf16[1024,384]{1,0:T(8,128)(2,1)}, u32[]{:S(2)}, u32[]{:S(2)}) collective-permute-start(bf16[1024,384]{1,0:T(8,128)(2,1)S(1)} %bitcast.129), channel_id=1, source_target_pairs={{0,8},{8,16},{16,24},{24,32},{32,40},{40,48},{48,56},{56,64},{64,7... | collective-permute-start | bytes 2359304 | tf_op jit(solution)/shard_map/ppermute | solution.py:20
  69.1 57.1 %copy-start.4 = (bf16[1,8,128,384]{2,3,1,0:T(8,128)(2,1)S(1)}, bf16[1,8,128,384]{2,3,1,0:T(8,128)(2,1)}, u32[]{:S(2)}) copy-start(bf16[1,8,128,384]{2,3,1,0:T(8,128)(2,1)} %get-tuple-element.22) | copy-start | bytes 2359300
  71.3 56.0 %copy-start.3 = (bf16[1,8,128,384]{2,3,1,0:T(8,128)(2,1)S(1)}, bf16[1,8,128,384]{2,3,1,0:T(8,128)(2,1)}, u32[]{:S(2)}) copy-start(bf16[1,8,128,384]{2,3,1,0:T(8,128)(2,1)} %get-tuple-element.23) | copy-start | bytes 2359300
  176.7 123.9 %all-to-all-start.1 = ((bf16[2,1024,384]{2,0,1:T(2,128)(2,1)}), bf16[2,1024,384]{2,0,1:T(2,128)(2,1)}, u32[]{:S(2)}, u32[]{:S(2)}) async-start(bf16[2,1024,384]{2,0,1:T(2,128)(2,1)} %copy.159), calls=%async_computation.1 | async-start | bytes 3145728 | tf_op jit(solution)/shard_map/all_to_all | solution.py:443
  181.2 5.7 %slice-start = ((s8[5111808]{0:T(1024)(128)(4,1)}), s8[4194304]{0:T(1024)(128)(4,1)S(1)}, s32[]{:S(2)}) async-start(s8[5111808]{0:T(1024)(128)(4,1)} %bitcast.117), calls=%async_computation.3 | async-start | bytes 8388608
  182.5 4.4 %slice-start.1 = ((s8[5111808]{0:T(1024)(128)(4,1)}), s8[917504]{0:T(1024)(128)(4,1)S(1)}, s32[]{:S(2)}) async-start(s8[5111808]{0:T(1024)(128)(4,1)} %bitcast.117), calls=%async_computation.4 | async-start | bytes 1835008
  188.8 2.2 copy-start.2
  288.7 1.2 copy-start
  292.5 2.2 copy-start.1
  300.6 25.3 %all-to-all-start.2 = ((bf16[2,1024,384]{2,0,1:T(2,128)(2,1)}), bf16[2,1024,384]{2,0,1:T(2,128)(2,1)S(1)}, u32[]{:S(2)}, u32[]{:S(2)}) async-start(bf16[2,1024,384]{2,0,1:T(2,128)(2,1)} %copy.168), calls=%async_computation.2 | async-start | bytes 3145728 | tf_op jit(solution)/shard_map/all_to_all | solution.py:446

commit v3 on v0

--- a/solution.py
+++ b/solution.py
@@ -149,8 +149,8 @@
             lax.dot_general(query, chosen_keys, nt, preferred_element_type=jnp.float32) * scale
         )
         peak = jnp.max(scores, axis=1, keepdims=True)
-        log_total = peak + jnp.log(jnp.sum(jnp.exp(scores - peak), axis=1, keepdims=True))
-        probs = jnp.exp(scores - log_total)
+        lifted = jnp.exp(scores - peak)
+        probs = lifted * (1.0 / jnp.sum(lifted, axis=1, keepdims=True))
         weights = probs.astype(jnp.bfloat16)
         attended = jnp.dot(weights, chosen_values, preferred_element_type=jnp.float32).astype(
             jnp.bfloat16

time: 328 us -> 328 us (level)
  no operation moved by 1% of the time
where the time goes in v3:
time: 328 us; the launch traced here: 327 us
  Pallas kernels  126 us (38%)
  waiting for transfers between devices  63.6 us (19%)
  starting transfers between devices  60.9 us (19%)
  local copies, waits for them, and re-layouts  46.9 us (14%)
  other arithmetic  24.2 us (7%)
  matrix products  4.15 us (1%)
    pallas_call x2, Pallas kernels, butterfly_sum(): pl.pallas_call(functools.partial(reduce_kernel, count), out_shape=jax.Sha...  89.2 us
    pallas_call x1, Pallas kernels, attend(): pl.pallas_call(attention_kernel, out_shape=(jax.ShapeDtypeStruct((count,...  37 us
    all_to_all x1, waiting for transfers between devices, per_device(): lax.all_to_all(jnp.stack([query, keys, values, cotangent]), 'head', split...  36.3 us
    ppermute x8, starting transfers between devices, passed_along(): return lax.ppermute(block, axis, route)  35.5 us
    ppermute x8, waiting for transfers between devices, passed_along(): return lax.ppermute(block, axis, route)  21.1 us
    all_to_all x1, starting transfers between devices, per_device(): lax.all_to_all(jnp.stack([key_rows, value_rows]), 'head', split_axis=1, c...  9.9 us
    all_to_all x1, starting transfers between devices, per_device(): lax.all_to_all(jnp.stack([attended, query_rows]), 'head', split_axis=1, c...  9.64 us
    another operation x2, other arithmetic  8.4 us
  transfers between devices with their start and end apart: 11, of which 4 were waited for; matrix products, arithmetic and copies ran while one was open for 16% of the time, Pallas kernels for 27%

profile of v3, /device:TPU:160, one launch (start us, length us, event | category | flops | bytes accessed | tf_op | source)
XLA Modules:
  0.0 326.9 jit_solution(10732537965119179636)
XLA Ops:
  0.6 2.0 pad_maximum_fusion
  2.7 3.6 %copy.147 = bf16[4,128,3072]{1,0,2:T(4,128)(2,1)} copy(bf16[4,128,3072]{2,1,0:T(8,128)(2,1)S(1)} %pad_maximum_fusion) | data formatting | bytes 6291456 | tf_op jit(solution)/shard_map/stack | solution.py:219
  6.3 5.9 %all-to-all-start = ((bf16[4,128,3072]{1,0,2:T(4,128)(2,1)}), bf16[4,128,3072]{1,0,2:T(4,128)(2,1)S(1)}, u32[]{:S(2)}, u32[]{:S(2)}) async-start(bf16[4,128,3072]{1,0,2:T(4,128)(2,1)} %copy.147), calls=%async_computation | async-start | bytes 6291456 | tf_op jit(solution)/shard_map/all_to_all | solution.py:218
  12.6 36.3 %all-to-all-done = bf16[4,128,3072]{1,0,2:T(4,128)(2,1)S(1)} async-done(((bf16[4,128,3072]{1,0,2:T(4,128)(2,1)}), bf16[4,128,3072]{1,0,2:T(4,128)(2,1)S(1)}, u32[]{:S(2)}, u32[]{:S(2)}) %all-to-all-start) | async-done | bytes 3145760 | tf_op jit(solution)/shard_map/all_to_all | solution.py:218
  51.1 1.9 collective-permute-start.2
  53.1 7.9 %collective-permute-start.3 = (bf16[1024,384]{1,0:T(8,128)(2,1)S(1)}, bf16[1024,384]{1,0:T(8,128)(2,1)}, u32[]{:S(2)}, u32[]{:S(2)}) collective-permute-start(bf16[1024,384]{1,0:T(8,128)(2,1)S(1)} %bitcast.101), channel_id=1, source_target_pairs={{8,0},{16,8},{24,16},{32,24},{40,32},{48,40},{56,48},{64,56},{72,6... | collective-permute-start | bytes 2359304 | tf_op jit(solution)/shard_map/ppermute | solution.py:20
  61.9 1.9 collective-permute-start
  63.9 8.0 %collective-permute-start.1 = (bf16[1024,384]{1,0:T(8,128)(2,1)S(1)}, bf16[1024,384]{1,0:T(8,128)(2,1)}, u32[]{:S(2)}, u32[]{:S(2)}) collective-permute-start(bf16[1024,384]{1,0:T(8,128)(2,1)S(1)} %bitcast.104), channel_id=1, source_target_pairs={{8,0},{16,8},{24,16},{32,24},{40,32},{48,40},{56,48},{64,56},{72,6... | collective-permute-start | bytes 2359304 | tf_op jit(solution)/shard_map/ppermute | solution.py:20
  77.3 2.1 reshape.63.x_ref
  79.4 36.1 %shard_map.84 = bf16[32,48,128]{2,1,0:T(8,128)(2,1)} custom-call(bf16[32,48,128]{2,1,0:T(8,128)(2,1)} %reshape.63.x_ref), custom_call_target="tpu_custom_call" | custom-call | tf_op jit(solution)/shard_map/pallas_call | solution.py:92
  122.4 1.8 pad_maximum_fusion.2.v_ref
  127.5 37.0 %shard_map.85 = (bf16[1024,384]{1,0:T(8,128)(2,1)}, bf16[1024,384]{1,0:T(8,128)(2,1)}, f32[3328,384]{1,0:T(8,128)}, f32[3328,384]{1,0:T(8,128)}) custom-call(s32[216]{0:T(256)} %reshape.61.index_ref, bf16[1024,384]{1,0:T(8,128)(2,1)} %bitcast.114, bf16[1024,384]{1,0:T(8,128)(2,1)} %bitcast.115, bf16[3328,384]{1,0:T(8,128)(2,1)} %pad_maximum_fusion.1.k_ref, ...), custom_call_target="tpu_custom_call" | custom-call | flops 6341787648 | bytes 18481152 | tf_op jit(solution)/shard_map/pallas_call | solution.py:187
  166.0 2.8 copy.159
  168.8 9.6 %all-to-all-start.1 = ((bf16[2,1024,384]{2,0,1:T(2,128)(2,1)}), bf16[2,1024,384]{2,0,1:T(2,128)(2,1)S(1)}, u32[]{:S(2)}, u32[]{:S(2)}) async-start(bf16[2,1024,384]{2,0,1:T(2,128)(2,1)} %copy.159), calls=%async_computation.1 | async-start | bytes 3145728 | tf_op jit(solution)/shard_map/all_to_all | solution.py:310
  178.4 4.2 %convert.8 = bf16[3328,384]{1,0:T(8,128)(2,1)} convert(f32[3328,384]{1,0:T(8,128)} %get-tuple-element.10) | non-fusion elementwise | flops 1277952 | bytes 7667712 | tf_op jit(solution)/shard_map/convert.3
  182.6 4.2 %convert.9 = bf16[3328,384]{1,0:T(8,128)(2,1)} convert(f32[3328,384]{1,0:T(8,128)} %get-tuple-element.11) | non-fusion elementwise | flops 1277952 | bytes 7667712 | tf_op jit(solution)/shard_map/convert.1
  189.0 53.1 %shard_map.86 = f32[32,48,128]{2,1,0:T(8,128)} custom-call(f32[32,48,128]{2,1,0:T(8,128)} %reshape_reshape.3.x_ref), custom_call_target="tpu_custom_call" | custom-call | tf_op jit(solution)/shard_map/pallas_call | solution.py:92
  243.5 2.6 fusion.25
  246.0 4.1 %collective-permute-start.4 = (bf16[1024,384]{1,0:T(8,128)(2,1)}, bf16[1024,384]{1,0:T(8,128)(2,1)}, u32[]{:S(2)}, u32[]{:S(2)}) collective-permute-start(bf16[1024,384]{1,0:T(8,128)(2,1)} %get-tuple-element.16), channel_id=1, source_target_pairs={{8,0},{16,8},{24,16},{32,24},{40,32},{48,40},{56,48},{64,56},{72,6... | collective-permute-start | bytes 2359304 | tf_op jit(solution)/shard_map/ppermute | solution.py:20
  250.1 1.9 collective-permute-start.5
  253.3 7.9 %collective-permute-start.6 = (bf16[1024,384]{1,0:T(8,128)(2,1)}, bf16[1024,384]{1,0:T(8,128)(2,1)}, u32[]{:S(2)}, u32[]{:S(2)}) collective-permute-start(bf16[1024,384]{1,0:T(8,128)(2,1)} %get-tuple-element.18), channel_id=1, source_target_pairs={{8,0},{16,8},{24,16},{32,24},{40,32},{48,40},{56,48},{64,56},{72,6... | collective-permute-start | bytes 2359304 | tf_op jit(solution)/shard_map/ppermute | solution.py:20
  261.2 1.9 collective-permute-start.7
  264.2 2.4 copy.172
  269.0 14.9 %collective-permute-done.5 = bf16[1024,384]{1,0:T(8,128)(2,1)} collective-permute-done((bf16[1024,384]{1,0:T(8,128)(2,1)S(1)}, bf16[1024,384]{1,0:T(8,128)(2,1)}, u32[]{:S(2)}, u32[]{:S(2)}) %collective-permute-start.5) | collective-permute-done | bytes 786464 | tf_op jit(solution)/shard_map/ppermute | solution.py:20
  283.9 2.3 fusion.4
  286.2 6.2 %collective-permute-done.7 = bf16[1024,384]{1,0:T(8,128)(2,1)} collective-permute-done((bf16[1024,384]{1,0:T(8,128)(2,1)}, bf16[1024,384]{1,0:T(8,128)(2,1)}, u32[]{:S(2)}, u32[]{:S(2)}) %collective-permute-start.7) | collective-permute-done | bytes 786464 | tf_op jit(solution)/shard_map/ppermute | solution.py:20
  292.3 2.3 fusion.5
  294.8 2.8 copy.168
  297.6 9.9 %all-to-all-start.2 = ((bf16[2,1024,384]{2,0,1:T(2,128)(2,1)}), bf16[2,1024,384]{2,0,1:T(2,128)(2,1)S(1)}, u32[]{:S(2)}, u32[]{:S(2)}) async-start(bf16[2,1024,384]{2,0,1:T(2,128)(2,1)} %copy.168), calls=%async_computation.2 | async-start | bytes 3145728 | tf_op jit(solution)/shard_map/all_to_all | solution.py:313
  307.5 2.9 fusion.28
  314.1 6.2 %all-to-all-done.2 = bf16[2,1024,384]{2,0,1:T(2,128)(2,1)S(1)} async-done(((bf16[2,1024,384]{2,0,1:T(2,128)(2,1)}), bf16[2,1024,384]{2,0,1:T(2,128)(2,1)S(1)}, u32[]{:S(2)}, u32[]{:S(2)}) %all-to-all-start.2) | async-done | bytes 1572896 | tf_op jit(solution)/shard_map/all_to_all | solution.py:313
  320.3 2.9 fusion.27
  (63 shorter events, 36.6 us)
Async XLA Ops:
  6.3 5.9 %copy-start.4 = (s32[3,256,9]{1,0,2:T(4,128)S(1)}, s32[3,256,9]{1,0,2:T(4,128)}, u32[]{:S(2)}) copy-start(s32[3,256,9]{1,0,2:T(4,128)} %param.9) | copy-start | bytes 82948
  6.3 42.6 %all-to-all-start = ((bf16[4,128,3072]{1,0,2:T(4,128)(2,1)}), bf16[4,128,3072]{1,0,2:T(4,128)(2,1)S(1)}, u32[]{:S(2)}, u32[]{:S(2)}) async-start(bf16[4,128,3072]{1,0,2:T(4,128)(2,1)} %copy.147), calls=%async_computation | async-start | bytes 6291456 | tf_op jit(solution)/shard_map/all_to_all | solution.py:218
  51.1 69.6 %collective-permute-start.2 = (bf16[1024,384]{1,0:T(8,128)(2,1)S(1)}, bf16[1024,384]{1,0:T(8,128)(2,1)}, u32[]{:S(2)}, u32[]{:S(2)}) collective-permute-start(bf16[1024,384]{1,0:T(8,128)(2,1)S(1)} %bitcast.100), channel_id=1, source_target_pairs={{0,8},{8,16},{16,24},{24,32},{32,40},{40,48},{48,56},{56,64},{64,7... | collective-permute-start | bytes 2359304 | tf_op jit(solution)/shard_map/ppermute | solution.py:20
  53.1 67.6 %collective-permute-start.3 = (bf16[1024,384]{1,0:T(8,128)(2,1)S(1)}, bf16[1024,384]{1,0:T(8,128)(2,1)}, u32[]{:S(2)}, u32[]{:S(2)}) collective-permute-start(bf16[1024,384]{1,0:T(8,128)(2,1)S(1)} %bitcast.101), channel_id=1, source_target_pairs={{8,0},{16,8},{24,16},{32,24},{40,32},{48,40},{56,48},{64,56},{72,6... | collective-permute-start | bytes 2359304 | tf_op jit(solution)/shard_map/ppermute | solution.py:20
  61.9 62.2 %collective-permute-start = (bf16[1024,384]{1,0:T(8,128)(2,1)S(1)}, bf16[1024,384]{1,0:T(8,128)(2,1)}, u32[]{:S(2)}, u32[]{:S(2)}) collective-permute-start(bf16[1024,384]{1,0:T(8,128)(2,1)S(1)} %bitcast.103), channel_id=1, source_target_pairs={{0,8},{8,16},{16,24},{24,32},{32,40},{40,48},{48,56},{56,64},{64,7... | collective-permute-start | bytes 2359304 | tf_op jit(solution)/shard_map/ppermute | solution.py:20
  63.9 60.3 %collective-permute-start.1 = (bf16[1024,384]{1,0:T(8,128)(2,1)S(1)}, bf16[1024,384]{1,0:T(8,128)(2,1)}, u32[]{:S(2)}, u32[]{:S(2)}) collective-permute-start(bf16[1024,384]{1,0:T(8,128)(2,1)S(1)} %bitcast.104), channel_id=1, source_target_pairs={{8,0},{16,8},{24,16},{32,24},{40,32},{48,40},{56,48},{64,56},{72,6... | collective-permute-start | bytes 2359304 | tf_op jit(solution)/shard_map/ppermute | solution.py:20
  75.6 42.7 %copy-start.3 = (bf16[1,8,128,384]{2,3,1,0:T(8,128)(2,1)S(1)}, bf16[1,8,128,384]{2,3,1,0:T(8,128)(2,1)}, u32[]{:S(2)}) copy-start(bf16[1,8,128,384]{2,3,1,0:T(8,128)(2,1)} %get-tuple-element.15) | copy-start | bytes 2359300
  77.3 42.2 %copy-start.2 = (bf16[1,8,128,384]{2,3,1,0:T(8,128)(2,1)S(1)}, bf16[1,8,128,384]{2,3,1,0:T(8,128)(2,1)}, u32[]{:S(2)}) copy-start(bf16[1,8,128,384]{2,3,1,0:T(8,128)(2,1)} %get-tuple-element.14) | copy-start | bytes 2359300
  168.8 128.8 %all-to-all-start.1 = ((bf16[2,1024,384]{2,0,1:T(2,128)(2,1)}), bf16[2,1024,384]{2,0,1:T(2,128)(2,1)S(1)}, u32[]{:S(2)}, u32[]{:S(2)}) async-start(bf16[2,1024,384]{2,0,1:T(2,128)(2,1)} %copy.159), calls=%async_computation.1 | async-start | bytes 3145728 | tf_op jit(solution)/shard_map/all_to_all | solution.py:310
  243.5 8.6 %copy-start.1 = (bf16[3328,384]{1,0:T(8,128)(2,1)S(1)}, bf16[3328,384]{1,0:T(8,128)(2,1)}, u32[]{:S(2)}) copy-start(bf16[3328,384]{1,0:T(8,128)(2,1)} %convert.9) | copy-start | bytes 7667716
  246.0 23.0 %collective-permute-start.4 = (bf16[1024,384]{1,0:T(8,128)(2,1)}, bf16[1024,384]{1,0:T(8,128)(2,1)}, u32[]{:S(2)}, u32[]{:S(2)}) collective-permute-start(bf16[1024,384]{1,0:T(8,128)(2,1)} %get-tuple-element.16), channel_id=1, source_target_pairs={{8,0},{16,8},{24,16},{32,24},{40,32},{48,40},{56,48},{64,56},{72,6... | collective-permute-start | bytes 2359304 | tf_op jit(solution)/shard_map/ppermute | solution.py:20
  250.1 33.8 %collective-permute-start.5 = (bf16[1024,384]{1,0:T(8,128)(2,1)S(1)}, bf16[1024,384]{1,0:T(8,128)(2,1)}, u32[]{:S(2)}, u32[]{:S(2)}) collective-permute-start(bf16[1024,384]{1,0:T(8,128)(2,1)S(1)} %get-tuple-element.17), channel_id=1, source_target_pairs={{0,8},{8,16},{16,24},{24,32},{32,40},{40,48},{48,56},{56,64},{64,7... | collective-permute-start | bytes 2359304 | tf_op jit(solution)/shard_map/ppermute | solution.py:20
  253.3 32.8 %collective-permute-start.6 = (bf16[1024,384]{1,0:T(8,128)(2,1)}, bf16[1024,384]{1,0:T(8,128)(2,1)}, u32[]{:S(2)}, u32[]{:S(2)}) collective-permute-start(bf16[1024,384]{1,0:T(8,128)(2,1)} %get-tuple-element.18), channel_id=1, source_target_pairs={{8,0},{16,8},{24,16},{32,24},{40,32},{48,40},{56,48},{64,56},{72,6... | collective-permute-start | bytes 2359304 | tf_op jit(solution)/shard_map/ppermute | solution.py:20
  261.2 31.1 %collective-permute-start.7 = (bf16[1024,384]{1,0:T(8,128)(2,1)}, bf16[1024,384]{1,0:T(8,128)(2,1)}, u32[]{:S(2)}, u32[]{:S(2)}) collective-permute-start(bf16[1024,384]{1,0:T(8,128)(2,1)} %get-tuple-element.19), channel_id=1, source_target_pairs={{0,8},{8,16},{16,24},{24,32},{32,40},{40,48},{48,56},{56,64},{64,7... | collective-permute-start | bytes 2359304 | tf_op jit(solution)/shard_map/ppermute | solution.py:20
  266.8 17.1 %copy-start = (f32[8,128,3,128]{3,2,1,0:T(4,128)S(1)}, f32[8,128,3,128]{3,2,1,0:T(4,128)}, u32[]{:S(2)}) copy-start(f32[8,128,3,128]{3,2,1,0:T(4,128)} %copy.172) | copy-start | bytes 4718596
  297.6 22.7 %all-to-all-start.2 = ((bf16[2,1024,384]{2,0,1:T(2,128)(2,1)}), bf16[2,1024,384]{2,0,1:T(2,128)(2,1)S(1)}, u32[]{:S(2)}, u32[]{:S(2)}) async-start(bf16[2,1024,384]{2,0,1:T(2,128)(2,1)} %copy.168), calls=%async_computation.2 | async-start | bytes 3145728 | tf_op jit(solution)/shard_map/all_to_all | solution.py:313

commit v4 on v0

--- a/solution.py
+++ b/solution.py
@@ -215,9 +215,13 @@
     span = (2 * reach + 1) * per_frame
     global_tiles = kv_tiles[:, 0, :GLOBALS]
     own_tiles = lax.dynamic_slice_in_dim(kv_tiles, cycle_pos * per_frame, per_frame, 1)
-    moved = lax.all_to_all(
-        jnp.stack([query, keys, values, cotangent]), "head", split_axis=2, concat_axis=1, tiled=True
-    )
+    moved_kv = lax.all_to_all(
+        jnp.stack([keys, values]), "head", split_axis=2, concat_axis=1, tiled=True
+    )
+    moved_qg = lax.all_to_all(
+        jnp.stack([query, cotangent]), "head", split_axis=2, concat_axis=1, tiled=True
+    )
+    moved = (moved_qg[0], moved_kv[0], moved_kv[1], moved_qg[1])
     frame_keys = moved[1]
     frame_values = moved[2]
     offset = 1

time: 328 us -> 314 us (0.957)
  waiting for transfers between devices: 63.6 us -> 42.9 us
  starting transfers between devices: 61 us -> 66.5 us
    all_to_all x1 -> x2, waiting for transfers between devices: 36.3 us -> 15.4 us  [the longest x1 15.4 us: per_device(): lax.all_to_all(jnp.stack([keys, values]), 'head', split_axis=2, concat_ax...]
    ppermute x8, starting transfers between devices: 35.5 us -> 42.9 us  [passed_along(): return lax.ppermute(block, axis, route)]
    all_to_all x1 -> x2, starting transfers between devices: 5.89 us -> 9.95 us  [the longest x1 5.76 us: per_device(): lax.all_to_all(jnp.stack([keys, values]), 'head', split_axis=2, concat_ax...]
    all_to_all x1, starting transfers between devices: 9.96 us -> 6.4 us  [per_device(): lax.all_to_all(jnp.stack([key_rows, value_rows]), 'head', split_axis=1, c...]
    another operation x3 -> x4, other arithmetic: 10.4 us -> 11.5 us
  transfers between devices with their start and end apart: 11 -> 12, of which waited for: 4 -> 5; matrix products, arithmetic and copies ran while one was open for 16% -> 18% of each run, Pallas kernels for 27% -> 29%
where the time goes in v4:
time: 314 us; the launch traced here: 313 us
  Pallas kernels  127 us (40%)
  starting transfers between devices  66.5 us (21%)
  local copies, waits for them, and re-layouts  47 us (15%)
  waiting for transfers between devices  42.9 us (14%)
  other arithmetic  25.2 us (8%)
  matrix products  4.15 us (1%)
    pallas_call x2, Pallas kernels, butterfly_sum(): pl.pallas_call(functools.partial(reduce_kernel, count), out_shape=jax.Sha...  90 us
    ppermute x8, starting transfers between devices, passed_along(): return lax.ppermute(block, axis, route)  42.9 us
    pallas_call x1, Pallas kernels, attend(): pl.pallas_call(attention_kernel, out_shape=(jax.ShapeDtypeStruct((count,...  36.7 us
    ppermute x8, waiting for transfers between devices, passed_along(): return lax.ppermute(block, axis, route)  21.3 us
    all_to_all x1, waiting for transfers between devices, per_device(): lax.all_to_all(jnp.stack([keys, values]), 'head', split_axis=2, concat_ax...  15.4 us
    another operation x2, other arithmetic  8.42 us
    all_to_all x1, starting transfers between devices, per_device(): lax.all_to_all(jnp.stack([attended, query_rows]), 'head', split_axis=1, c...  7.19 us
    all_to_all x1, starting transfers between devices, per_device(): lax.all_to_all(jnp.stack([key_rows, value_rows]), 'head', split_axis=1, c...  6.4 us
  transfers between devices with their start and end apart: 12, of which 5 were waited for; matrix products, arithmetic and copies ran while one was open for 18% of the time, Pallas kernels for 29%

profile of v4, /device:TPU:160, one launch (start us, length us, event | category | flops | bytes accessed | tf_op | source)
XLA Modules:
  0.0 313.4 jit_solution(15194897795844761591)
XLA Ops:
  2.1 2.9 copy.149
  5.1 5.8 %all-to-all-start.1 = ((bf16[2,128,3072]{1,0,2:T(2,128)(2,1)}), bf16[2,128,3072]{1,0,2:T(2,128)(2,1)S(1)}, u32[]{:S(2)}, u32[]{:S(2)}) async-start(bf16[2,128,3072]{1,0,2:T(2,128)(2,1)} %copy.149), calls=%async_computation.1 | async-start | bytes 3145728 | tf_op jit(solution)/shard_map/all_to_all | solution.py:218
  12.3 2.9 copy.147
  15.3 15.4 %all-to-all-done.1 = bf16[2,128,3072]{1,0,2:T(2,128)(2,1)S(1)} async-done(((bf16[2,128,3072]{1,0,2:T(2,128)(2,1)}), bf16[2,128,3072]{1,0,2:T(2,128)(2,1)S(1)}, u32[]{:S(2)}, u32[]{:S(2)}) %all-to-all-start.1) | async-done | bytes 1572896 | tf_op jit(solution)/shard_map/all_to_all | solution.py:218
  30.7 4.2 %all-to-all-start = ((bf16[2,128,3072]{1,0,2:T(2,128)(2,1)}), bf16[2,128,3072]{1,0,2:T(2,128)(2,1)S(1)}, u32[]{:S(2)}, u32[]{:S(2)}) async-start(bf16[2,128,3072]{1,0,2:T(2,128)(2,1)} %copy.147), calls=%async_computation | async-start | bytes 3145728 | tf_op jit(solution)/shard_map/all_to_all | solution.py:221
  37.4 1.9 collective-permute-start.2
  39.4 7.9 %collective-permute-start.3 = (bf16[1024,384]{1,0:T(8,128)(2,1)}, bf16[1024,384]{1,0:T(8,128)(2,1)}, u32[]{:S(2)}, u32[]{:S(2)}) collective-permute-start(bf16[1024,384]{1,0:T(8,128)(2,1)} %bitcast.108), channel_id=1, source_target_pairs={{8,0},{16,8},{24,16},{32,24},{40,32},{48,40},{56,48},{64,56},{72,6... | collective-permute-start | bytes 2359304 | tf_op jit(solution)/shard_map/ppermute | solution.py:20
  48.4 1.9 collective-permute-start
  50.3 8.0 %collective-permute-start.1 = (bf16[1024,384]{1,0:T(8,128)(2,1)}, bf16[1024,384]{1,0:T(8,128)(2,1)}, u32[]{:S(2)}, u32[]{:S(2)}) collective-permute-start(bf16[1024,384]{1,0:T(8,128)(2,1)} %bitcast.105), channel_id=1, source_target_pairs={{8,0},{16,8},{24,16},{32,24},{40,32},{48,40},{56,48},{64,56},{72,6... | collective-permute-start | bytes 2359304 | tf_op jit(solution)/shard_map/ppermute | solution.py:20
  64.9 44.3 %shard_map.84 = bf16[32,48,128]{2,1,0:T(8,128)(2,1)} custom-call(bf16[32,48,128]{2,1,0:T(8,128)(2,1)} %reshape.63.x_ref), custom_call_target="tpu_custom_call" | custom-call | tf_op jit(solution)/shard_map/pallas_call | solution.py:92
  120.0 36.7 %shard_map.85 = (bf16[1024,384]{1,0:T(8,128)(2,1)}, bf16[1024,384]{1,0:T(8,128)(2,1)}, f32[3328,384]{1,0:T(8,128)}, f32[3328,384]{1,0:T(8,128)}) custom-call(s32[216]{0:T(256)} %reshape.61.index_ref, bf16[1024,384]{1,0:T(8,128)(2,1)} %bitcast.123, bf16[1024,384]{1,0:T(8,128)(2,1)} %bitcast.122, bf16[3328,384]{1,0:T(8,128)(2,1)} %pad_maximum_fusion.k_ref, ...), custom_call_target="tpu_custom_call" | custom-call | flops 6341787648 | bytes 18481152 | tf_op jit(solution)/shard_map/pallas_call | solution.py:187
  158.2 2.7 copy.159
  161.0 7.2 %all-to-all-start.2 = ((bf16[2,1024,384]{2,0,1:T(2,128)(2,1)}), bf16[2,1024,384]{2,0,1:T(2,128)(2,1)S(1)}, u32[]{:S(2)}, u32[]{:S(2)}) async-start(bf16[2,1024,384]{2,0,1:T(2,128)(2,1)} %copy.159), calls=%async_computation.2 | async-start | bytes 3145728 | tf_op jit(solution)/shard_map/all_to_all | solution.py:314
  168.1 4.2 %convert.8 = bf16[3328,384]{1,0:T(8,128)(2,1)} convert(f32[3328,384]{1,0:T(8,128)} %get-tuple-element.10) | non-fusion elementwise | flops 1277952 | bytes 7667712 | tf_op jit(solution)/shard_map/convert.3
  172.3 4.3 %convert.9 = bf16[3328,384]{1,0:T(8,128)(2,1)} convert(f32[3328,384]{1,0:T(8,128)} %get-tuple-element.11) | non-fusion elementwise | flops 1277952 | bytes 7667712 | tf_op jit(solution)/shard_map/convert.1
  178.7 45.7 %shard_map.86 = f32[32,48,128]{2,1,0:T(8,128)} custom-call(f32[32,48,128]{2,1,0:T(8,128)} %reshape_reshape.3.x_ref), custom_call_target="tpu_custom_call" | custom-call | tf_op jit(solution)/shard_map/pallas_call | solution.py:92
  225.8 2.6 fusion.24
  228.3 11.5 %collective-permute-start.4 = (bf16[1024,384]{1,0:T(8,128)(2,1)}, bf16[1024,384]{1,0:T(8,128)(2,1)}, u32[]{:S(2)}, u32[]{:S(2)}) collective-permute-start(bf16[1024,384]{1,0:T(8,128)(2,1)} %get-tuple-element.12), channel_id=1, source_target_pairs={{8,0},{16,8},{24,16},{32,24},{40,32},{48,40},{56,48},{64,56},{72,6... | collective-permute-start | bytes 2359304 | tf_op jit(solution)/shard_map/ppermute | solution.py:20
  239.8 1.9 collective-permute-start.5
  243.1 7.9 %collective-permute-start.6 = (bf16[1024,384]{1,0:T(8,128)(2,1)}, bf16[1024,384]{1,0:T(8,128)(2,1)}, u32[]{:S(2)}, u32[]{:S(2)}) collective-permute-start(bf16[1024,384]{1,0:T(8,128)(2,1)} %get-tuple-element.14), channel_id=1, source_target_pairs={{8,0},{16,8},{24,16},{32,24},{40,32},{48,40},{56,48},{64,56},{72,6... | collective-permute-start | bytes 2359304 | tf_op jit(solution)/shard_map/ppermute | solution.py:20
  250.9 1.9 collective-permute-start.7
  254.0 2.4 copy.172
  258.7 13.2 %collective-permute-done.5 = bf16[1024,384]{1,0:T(8,128)(2,1)} collective-permute-done((bf16[1024,384]{1,0:T(8,128)(2,1)S(1)}, bf16[1024,384]{1,0:T(8,128)(2,1)}, u32[]{:S(2)}, u32[]{:S(2)}) %collective-permute-start.5) | collective-permute-done | bytes 786464 | tf_op jit(solution)/shard_map/ppermute | solution.py:20
  271.9 2.3 fusion.4
  274.2 4.5 %collective-permute-done.6 = bf16[1024,384]{1,0:T(8,128)(2,1)} collective-permute-done((bf16[1024,384]{1,0:T(8,128)(2,1)}, bf16[1024,384]{1,0:T(8,128)(2,1)}, u32[]{:S(2)}, u32[]{:S(2)}) %collective-permute-start.6) | collective-permute-done | bytes 786464 | tf_op jit(solution)/shard_map/ppermute | solution.py:20
  278.6 3.6 %collective-permute-done.7 = bf16[1024,384]{1,0:T(8,128)(2,1)} collective-permute-done((bf16[1024,384]{1,0:T(8,128)(2,1)}, bf16[1024,384]{1,0:T(8,128)(2,1)}, u32[]{:S(2)}, u32[]{:S(2)}) %collective-permute-start.7) | collective-permute-done | bytes 786464 | tf_op jit(solution)/shard_map/ppermute | solution.py:20
  282.3 2.3 fusion.5
  284.7 2.8 copy.168
  287.5 6.4 %all-to-all-start.3 = ((bf16[2,1024,384]{2,0,1:T(2,128)(2,1)}), bf16[2,1024,384]{2,0,1:T(2,128)(2,1)S(1)}, u32[]{:S(2)}, u32[]{:S(2)}) async-start(bf16[2,1024,384]{2,0,1:T(2,128)(2,1)} %copy.168), calls=%async_computation.3 | async-start | bytes 3145728 | tf_op jit(solution)/shard_map/all_to_all | solution.py:317
  293.9 2.9 fusion.27
  300.6 6.2 %all-to-all-done.3 = bf16[2,1024,384]{2,0,1:T(2,128)(2,1)S(1)} async-done(((bf16[2,1024,384]{2,0,1:T(2,128)(2,1)}), bf16[2,1024,384]{2,0,1:T(2,128)(2,1)S(1)}, u32[]{:S(2)}, u32[]{:S(2)}) %all-to-all-start.3) | async-done | bytes 1572896 | tf_op jit(solution)/shard_map/all_to_all | solution.py:317
  306.8 2.9 fusion.26
  (71 shorter events, 41.4 us)
Async XLA Ops:
  5.1 25.6 %all-to-all-start.1 = ((bf16[2,128,3072]{1,0,2:T(2,128)(2,1)}), bf16[2,128,3072]{1,0,2:T(2,128)(2,1)S(1)}, u32[]{:S(2)}, u32[]{:S(2)}) async-start(bf16[2,128,3072]{1,0,2:T(2,128)(2,1)} %copy.149), calls=%async_computation.1 | async-start | bytes 3145728 | tf_op jit(solution)/shard_map/all_to_all | solution.py:218
  15.3 19.6 %copy-start.6 = (s32[3,256,9]{1,0,2:T(4,128)S(1)}, s32[3,256,9]{1,0,2:T(4,128)}, u32[]{:S(2)}) copy-start(s32[3,256,9]{1,0,2:T(4,128)} %param.9) | copy-start | bytes 82948
  30.7 78.5 %all-to-all-start = ((bf16[2,128,3072]{1,0,2:T(2,128)(2,1)}), bf16[2,128,3072]{1,0,2:T(2,128)(2,1)S(1)}, u32[]{:S(2)}, u32[]{:S(2)}) async-start(bf16[2,128,3072]{1,0,2:T(2,128)(2,1)} %copy.147), calls=%async_computation | async-start | bytes 3145728 | tf_op jit(solution)/shard_map/all_to_all | solution.py:221
  37.4 74.7 %collective-permute-start.2 = (bf16[1024,384]{1,0:T(8,128)(2,1)}, bf16[1024,384]{1,0:T(8,128)(2,1)}, u32[]{:S(2)}, u32[]{:S(2)}) collective-permute-start(bf16[1024,384]{1,0:T(8,128)(2,1)} %bitcast.107), channel_id=1, source_target_pairs={{0,8},{8,16},{16,24},{24,32},{32,40},{40,48},{48,56},{56,64},{64,7... | collective-permute-start | bytes 2359304 | tf_op jit(solution)/shard_map/ppermute | solution.py:20
  39.4 72.8 %collective-permute-start.3 = (bf16[1024,384]{1,0:T(8,128)(2,1)}, bf16[1024,384]{1,0:T(8,128)(2,1)}, u32[]{:S(2)}, u32[]{:S(2)}) collective-permute-start(bf16[1024,384]{1,0:T(8,128)(2,1)} %bitcast.108), channel_id=1, source_target_pairs={{8,0},{16,8},{24,16},{32,24},{40,32},{48,40},{56,48},{64,56},{72,6... | collective-permute-start | bytes 2359304 | tf_op jit(solution)/shard_map/ppermute | solution.py:20
  48.4 68.2 %collective-permute-start = (bf16[1024,384]{1,0:T(8,128)(2,1)}, bf16[1024,384]{1,0:T(8,128)(2,1)}, u32[]{:S(2)}, u32[]{:S(2)}) collective-permute-start(bf16[1024,384]{1,0:T(8,128)(2,1)} %bitcast.104), channel_id=1, source_target_pairs={{0,8},{8,16},{16,24},{24,32},{32,40},{40,48},{48,56},{56,64},{64,7... | collective-permute-start | bytes 2359304 | tf_op jit(solution)/shard_map/ppermute | solution.py:20
  50.3 66.2 %collective-permute-start.1 = (bf16[1024,384]{1,0:T(8,128)(2,1)}, bf16[1024,384]{1,0:T(8,128)(2,1)}, u32[]{:S(2)}, u32[]{:S(2)}) collective-permute-start(bf16[1024,384]{1,0:T(8,128)(2,1)} %bitcast.105), channel_id=1, source_target_pairs={{8,0},{16,8},{24,16},{32,24},{40,32},{48,40},{56,48},{64,56},{72,6... | collective-permute-start | bytes 2359304 | tf_op jit(solution)/shard_map/ppermute | solution.py:20
  59.6 1.3 copy-start.4
  110.6 1.3 copy-start.5
  111.9 1.1 copy-start.3
  114.8 1.8 copy-start.2
  161.0 126.6 %all-to-all-start.2 = ((bf16[2,1024,384]{2,0,1:T(2,128)(2,1)}), bf16[2,1024,384]{2,0,1:T(2,128)(2,1)S(1)}, u32[]{:S(2)}, u32[]{:S(2)}) async-start(bf16[2,1024,384]{2,0,1:T(2,128)(2,1)} %copy.159), calls=%async_computation.2 | async-start | bytes 3145728 | tf_op jit(solution)/shard_map/all_to_all | solution.py:314
  225.8 16.0 %copy-start.1 = (bf16[3328,384]{1,0:T(8,128)(2,1)S(1)}, bf16[3328,384]{1,0:T(8,128)(2,1)}, u32[]{:S(2)}) copy-start(bf16[3328,384]{1,0:T(8,128)(2,1)} %convert.9) | copy-start | bytes 7667716
  228.3 30.4 %collective-permute-start.4 = (bf16[1024,384]{1,0:T(8,128)(2,1)}, bf16[1024,384]{1,0:T(8,128)(2,1)}, u32[]{:S(2)}, u32[]{:S(2)}) collective-permute-start(bf16[1024,384]{1,0:T(8,128)(2,1)} %get-tuple-element.12), channel_id=1, source_target_pairs={{8,0},{16,8},{24,16},{32,24},{40,32},{48,40},{56,48},{64,56},{72,6... | collective-permute-start | bytes 2359304 | tf_op jit(solution)/shard_map/ppermute | solution.py:20
  239.8 32.1 %collective-permute-start.5 = (bf16[1024,384]{1,0:T(8,128)(2,1)S(1)}, bf16[1024,384]{1,0:T(8,128)(2,1)}, u32[]{:S(2)}, u32[]{:S(2)}) collective-permute-start(bf16[1024,384]{1,0:T(8,128)(2,1)S(1)} %get-tuple-element.13), channel_id=1, source_target_pairs={{0,8},{8,16},{16,24},{24,32},{32,40},{40,48},{48,56},{56,64},{64,7... | collective-permute-start | bytes 2359304 | tf_op jit(solution)/shard_map/ppermute | solution.py:20
  243.1 35.6 %collective-permute-start.6 = (bf16[1024,384]{1,0:T(8,128)(2,1)}, bf16[1024,384]{1,0:T(8,128)(2,1)}, u32[]{:S(2)}, u32[]{:S(2)}) collective-permute-start(bf16[1024,384]{1,0:T(8,128)(2,1)} %get-tuple-element.14), channel_id=1, source_target_pairs={{8,0},{16,8},{24,16},{32,24},{40,32},{48,40},{56,48},{64,56},{72,6... | collective-permute-start | bytes 2359304 | tf_op jit(solution)/shard_map/ppermute | solution.py:20
  250.9 31.3 %collective-permute-start.7 = (bf16[1024,384]{1,0:T(8,128)(2,1)}, bf16[1024,384]{1,0:T(8,128)(2,1)}, u32[]{:S(2)}, u32[]{:S(2)}) collective-permute-start(bf16[1024,384]{1,0:T(8,128)(2,1)} %get-tuple-element.15), channel_id=1, source_target_pairs={{0,8},{8,16},{16,24},{24,32},{32,40},{40,48},{48,56},{56,64},{64,7... | collective-permute-start | bytes 2359304 | tf_op jit(solution)/shard_map/ppermute | solution.py:20
  257.6 14.3 %copy-start = (f32[8,128,3,128]{3,2,1,0:T(4,128)S(1)}, f32[8,128,3,128]{3,2,1,0:T(4,128)}, u32[]{:S(2)}) copy-start(f32[8,128,3,128]{3,2,1,0:T(4,128)} %copy.172) | copy-start | bytes 4718596
  287.5 19.3 %all-to-all-start.3 = ((bf16[2,1024,384]{2,0,1:T(2,128)(2,1)}), bf16[2,1024,384]{2,0,1:T(2,128)(2,1)S(1)}, u32[]{:S(2)}, u32[]{:S(2)}) async-start(bf16[2,1024,384]{2,0,1:T(2,128)(2,1)} %copy.168), calls=%async_computation.3 | async-start | bytes 3145728 | tf_op jit(solution)/shard_map/all_to_all | solution.py:317

commit v5 on v4

--- a/solution.py
+++ b/solution.py
@@ -273,25 +273,23 @@
     value_grad = value_pool[centre : centre + frame_rows]
     offset = 1
     lower = (reach - offset) * frame_rows
-    returned = (
-        passed_along(
-            key_pool[lower : lower + frame_rows].astype(jnp.bfloat16), "blk", -offset
-        ).astype(jnp.float32),
-        passed_along(
-            value_pool[lower : lower + frame_rows].astype(jnp.bfloat16), "blk", -offset
-        ).astype(jnp.float32),
-    )
+    returned = passed_along(
+        jnp.stack([key_pool[lower : lower + frame_rows], value_pool[lower : lower + frame_rows]]).astype(
+            jnp.bfloat16
+        ),
+        "blk",
+        -offset,
+    ).astype(jnp.float32)
     key_grad = key_grad + returned[0]
     value_grad = value_grad + returned[1]
     upper = (reach + offset) * frame_rows
-    returned = (
-        passed_along(
-            key_pool[upper : upper + frame_rows].astype(jnp.bfloat16), "blk", offset
-        ).astype(jnp.float32),
-        passed_along(
-            value_pool[upper : upper + frame_rows].astype(jnp.bfloat16), "blk", offset
-        ).astype(jnp.float32),
-    )
+    returned = passed_along(
+        jnp.stack([key_pool[upper : upper + frame_rows], value_pool[upper : upper + frame_rows]]).astype(
+            jnp.bfloat16
+        ),
+        "blk",
+        offset,
+    ).astype(jnp.float32)
     key_grad = key_grad + returned[0]
     value_grad = value_grad + returned[1]
     pool_end = span * TILE

time: 314 us -> 327 us (1.041)
  the two profiles are of different devices: /device:TPU:160 before, /device:TPU:16 now
where the time goes in v5:
time: 327 us; the launch traced here: 326 us
  Pallas kernels  176 us (54%)
  local copies, waits for them, and re-layouts  43.5 us (13%)
  starting transfers between devices  38 us (12%)
  waiting for transfers between devices  37.5 us (11%)
  other arithmetic  26.7 us (8%)
    pallas_call x2, Pallas kernels, butterfly_sum(): pl.pallas_call(functools.partial(reduce_kernel, count), out_shape=jax.Sha...  139 us
    pallas_call x1, Pallas kernels, attend(): pl.pallas_call(attention_kernel, out_shape=(jax.ShapeDtypeStruct((count,...  36.7 us
    all_to_all x1, waiting for transfers between devices, per_device(): lax.all_to_all(jnp.stack([keys, values]), 'head', split_axis=2, concat_ax...  16 us
    ppermute x6, starting transfers between devices, passed_along(): return lax.ppermute(block, axis, route)  15.3 us
    all_to_all x1, waiting for transfers between devices, per_device(): lax.all_to_all(jnp.stack([key_rows, value_rows]), 'head', split_axis=1, c...  14.2 us
    all_to_all x1, starting transfers between devices, per_device(): lax.all_to_all(jnp.stack([attended, query_rows]), 'head', split_axis=1, c...  8.86 us
    all_to_all x1, waiting for transfers between devices, per_device(): lax.all_to_all(jnp.stack([query, cotangent]), 'head', split_axis=2, conca...  7.24 us
  transfers between devices with their start and end apart: 10, of which 3 were waited for; matrix products, arithmetic and copies ran while one was open for 16% of the time, Pallas kernels for 43%

profile of v5, /device:TPU:16, one launch (start us, length us, event | category | flops | bytes accessed | tf_op | source)
XLA Modules:
  0.0 325.8 jit_solution(7049453350304335089)
XLA Ops:
  2.1 2.9 copy.149
  5.1 5.7 %all-to-all-start.1 = ((bf16[2,128,3072]{1,0,2:T(2,128)(2,1)}), bf16[2,128,3072]{1,0,2:T(2,128)(2,1)S(1)}, u32[]{:S(2)}, u32[]{:S(2)}) async-start(bf16[2,128,3072]{1,0,2:T(2,128)(2,1)} %copy.149), calls=%async_computation.1 | async-start | bytes 3145728 | tf_op jit(solution)/shard_map/all_to_all | solution.py:218
  12.2 2.9 copy.147
  15.1 16.0 %all-to-all-done.1 = bf16[2,128,3072]{1,0,2:T(2,128)(2,1)S(1)} async-done(((bf16[2,128,3072]{1,0,2:T(2,128)(2,1)}), bf16[2,128,3072]{1,0,2:T(2,128)(2,1)S(1)}, u32[]{:S(2)}, u32[]{:S(2)}) %all-to-all-start.1) | async-done | bytes 1572896 | tf_op jit(solution)/shard_map/all_to_all | solution.py:218
  31.1 3.6 %all-to-all-start = ((bf16[2,128,3072]{1,0,2:T(2,128)(2,1)}), bf16[2,128,3072]{1,0,2:T(2,128)(2,1)S(1)}, u32[]{:S(2)}, u32[]{:S(2)}) async-start(bf16[2,128,3072]{1,0,2:T(2,128)(2,1)} %copy.147), calls=%async_computation | async-start | bytes 3145728 | tf_op jit(solution)/shard_map/all_to_all | solution.py:221
  37.4 1.9 collective-permute-start.1
  39.3 2.4 collective-permute-start
  42.9 3.1 collective-permute-start.3
  46.0 2.1 collective-permute-start.2
  48.1 7.2 %all-to-all-done = bf16[2,128,3072]{1,0,2:T(2,128)(2,1)S(1)} async-done(((bf16[2,128,3072]{1,0,2:T(2,128)(2,1)}), bf16[2,128,3072]{1,0,2:T(2,128)(2,1)S(1)}, u32[]{:S(2)}, u32[]{:S(2)}) %all-to-all-start) | async-done | bytes 1572896 | tf_op jit(solution)/shard_map/all_to_all | solution.py:221
  55.4 2.9 copy.148
  62.0 48.5 %shard_map.84 = bf16[32,48,128]{2,1,0:T(8,128)(2,1)} custom-call(bf16[32,48,128]{2,1,0:T(8,128)(2,1)} %reshape.63.x_ref), custom_call_target="tpu_custom_call" | custom-call | tf_op jit(solution)/shard_map/pallas_call | solution.py:92
  113.0 1.7 pad_maximum_fusion.2
  114.7 1.8 pad_maximum_fusion.k_ref
  116.5 1.7 pad_maximum_fusion.3
  118.2 1.7 pad_maximum_fusion.1.v_ref
  119.9 36.7 %shard_map.85 = (bf16[1024,384]{1,0:T(8,128)(2,1)}, bf16[1024,384]{1,0:T(8,128)(2,1)}, f32[3328,384]{1,0:T(8,128)}, f32[3328,384]{1,0:T(8,128)}) custom-call(s32[216]{0:T(256)} %reshape.61.index_ref, bf16[1024,384]{1,0:T(8,128)(2,1)} %bitcast.163, bf16[1024,384]{1,0:T(8,128)(2,1)} %bitcast.162, bf16[3328,384]{1,0:T(8,128)(2,1)} %pad_maximum_fusion.k_ref, ...), custom_call_target="tpu_custom_call" | custom-call | flops 6341787648 | bytes 18481152 | tf_op jit(solution)/shard_map/pallas_call | solution.py:187
  158.1 2.8 copy.159
  160.9 8.9 %all-to-all-start.2 = ((bf16[2,1024,384]{2,0,1:T(2,128)(2,1)}), bf16[2,1024,384]{2,0,1:T(2,128)(2,1)S(1)}, u32[]{:S(2)}, u32[]{:S(2)}) async-start(bf16[2,1024,384]{2,0,1:T(2,128)(2,1)} %copy.159), calls=%async_computation.2 | async-start | bytes 3145728 | tf_op jit(solution)/shard_map/all_to_all | solution.py:312
  169.8 2.7 convert.17
  172.5 2.7 convert.16
  176.9 1.9 collective-permute-start.5
  180.1 3.9 %collective-permute-start.4 = (bf16[2,1024,384]{2,1,0:T(8,128)(2,1)}, bf16[2,1024,384]{2,1,0:T(8,128)(2,1)}, u32[]{:S(2)}, u32[]{:S(2)}) collective-permute-start(bf16[2,1024,384]{2,1,0:T(8,128)(2,1)} %pad_maximum_fusion.7), channel_id=1, source_target_pairs={{8,0},{16,8},{24,16},{32,24},{40,32},{48,40},{56,48},{64,56},{72,6... | collective-permute-start | bytes 4718600 | tf_op jit(solution)/shard_map/ppermute | solution.py:20
  186.2 90.8 %shard_map.86 = f32[32,48,128]{2,1,0:T(8,128)} custom-call(f32[32,48,128]{2,1,0:T(8,128)} %reshape_reshape.3.x_ref), custom_call_target="tpu_custom_call" | custom-call | tf_op jit(solution)/shard_map/pallas_call | solution.py:92
  279.4 2.4 copy.172
  285.8 1.8 convert_element_type.32
  287.9 2.9 fusion.8
  291.0 2.8 copy.168
  293.8 4.5 %all-to-all-start.3 = ((bf16[2,1024,384]{2,0,1:T(2,128)(2,1)}), bf16[2,1024,384]{2,0,1:T(2,128)(2,1)S(1)}, u32[]{:S(2)}, u32[]{:S(2)}) async-start(bf16[2,1024,384]{2,0,1:T(2,128)(2,1)} %copy.168), calls=%async_computation.3 | async-start | bytes 3145728 | tf_op jit(solution)/shard_map/all_to_all | solution.py:315
  298.3 2.9 fusion.29
  304.9 14.2 %all-to-all-done.3 = bf16[2,1024,384]{2,0,1:T(2,128)(2,1)S(1)} async-done(((bf16[2,1024,384]{2,0,1:T(2,128)(2,1)}), bf16[2,1024,384]{2,0,1:T(2,128)(2,1)S(1)}, u32[]{:S(2)}, u32[]{:S(2)}) %all-to-all-start.3) | async-done | bytes 1572896 | tf_op jit(solution)/shard_map/all_to_all | solution.py:315
  319.2 2.9 fusion.28
  (67 shorter events, 33.9 us)
Async XLA Ops:
  5.1 26.1 %all-to-all-start.1 = ((bf16[2,128,3072]{1,0,2:T(2,128)(2,1)}), bf16[2,128,3072]{1,0,2:T(2,128)(2,1)S(1)}, u32[]{:S(2)}, u32[]{:S(2)}) async-start(bf16[2,128,3072]{1,0,2:T(2,128)(2,1)} %copy.149), calls=%async_computation.1 | async-start | bytes 3145728 | tf_op jit(solution)/shard_map/all_to_all | solution.py:218
  15.1 19.7 %copy-start.5 = (s32[3,256,9]{1,0,2:T(4,128)S(1)}, s32[3,256,9]{1,0,2:T(4,128)}, u32[]{:S(2)}) copy-start(s32[3,256,9]{1,0,2:T(4,128)} %param.9) | copy-start | bytes 82948
  31.1 24.2 %all-to-all-start = ((bf16[2,128,3072]{1,0,2:T(2,128)(2,1)}), bf16[2,128,3072]{1,0,2:T(2,128)(2,1)S(1)}, u32[]{:S(2)}, u32[]{:S(2)}) async-start(bf16[2,128,3072]{1,0,2:T(2,128)(2,1)} %copy.147), calls=%async_computation | async-start | bytes 3145728 | tf_op jit(solution)/shard_map/all_to_all | solution.py:221
  37.4 74.8 %collective-permute-start.1 = (bf16[1024,384]{1,0:T(8,128)(2,1)}, bf16[1024,384]{1,0:T(8,128)(2,1)}, u32[]{:S(2)}, u32[]{:S(2)}) collective-permute-start(bf16[1024,384]{1,0:T(8,128)(2,1)} %bitcast.147), channel_id=1, source_target_pairs={{8,0},{16,8},{24,16},{32,24},{40,32},{48,40},{56,48},{64,56},{72,6... | collective-permute-start | bytes 2359304 | tf_op jit(solution)/shard_map/ppermute | solution.py:20
  39.3 72.8 %collective-permute-start = (bf16[1024,384]{1,0:T(8,128)(2,1)}, bf16[1024,384]{1,0:T(8,128)(2,1)}, u32[]{:S(2)}, u32[]{:S(2)}) collective-permute-start(bf16[1024,384]{1,0:T(8,128)(2,1)} %bitcast.148), channel_id=1, source_target_pairs={{0,8},{8,16},{16,24},{24,32},{32,40},{40,48},{48,56},{56,64},{64,7... | collective-permute-start | bytes 2359304 | tf_op jit(solution)/shard_map/ppermute | solution.py:20
  42.9 73.6 %collective-permute-start.3 = (bf16[1024,384]{1,0:T(8,128)(2,1)}, bf16[1024,384]{1,0:T(8,128)(2,1)}, u32[]{:S(2)}, u32[]{:S(2)}) collective-permute-start(bf16[1024,384]{1,0:T(8,128)(2,1)} %bitcast.144), channel_id=1, source_target_pairs={{8,0},{16,8},{24,16},{32,24},{40,32},{48,40},{56,48},{64,56},{72,6... | collective-permute-start | bytes 2359304 | tf_op jit(solution)/shard_map/ppermute | solution.py:20
  46.0 70.5 %collective-permute-start.2 = (bf16[1024,384]{1,0:T(8,128)(2,1)}, bf16[1024,384]{1,0:T(8,128)(2,1)}, u32[]{:S(2)}, u32[]{:S(2)}) collective-permute-start(bf16[1024,384]{1,0:T(8,128)(2,1)} %bitcast.145), channel_id=1, source_target_pairs={{0,8},{8,16},{16,24},{24,32},{32,40},{40,48},{48,56},{56,64},{64,7... | collective-permute-start | bytes 2359304 | tf_op jit(solution)/shard_map/ppermute | solution.py:20
  60.0 50.5 %copy-start.1 = (bf16[2,128,8,384]{3,1,2,0:T(8,128)(2,1)S(1)}, bf16[2,128,8,384]{3,1,2,0:T(8,128)(2,1)}, u32[]{:S(2)}) copy-start(bf16[2,128,8,384]{3,1,2,0:T(8,128)(2,1)} %copy.148) | copy-start | bytes 4718596
  110.5 1.3 copy-start.4
  111.9 1.1 copy-start.3
  114.7 1.8 copy-start.2
  160.9 132.9 %all-to-all-start.2 = ((bf16[2,1024,384]{2,0,1:T(2,128)(2,1)}), bf16[2,1024,384]{2,0,1:T(2,128)(2,1)S(1)}, u32[]{:S(2)}, u32[]{:S(2)}) async-start(bf16[2,1024,384]{2,0,1:T(2,128)(2,1)} %copy.159), calls=%async_computation.2 | async-start | bytes 3145728 | tf_op jit(solution)/shard_map/all_to_all | solution.py:312
  176.9 107.3 %collective-permute-start.5 = (bf16[2,1024,384]{2,1,0:T(8,128)(2,1)}, bf16[2,1024,384]{2,1,0:T(8,128)(2,1)}, u32[]{:S(2)}, u32[]{:S(2)}) collective-permute-start(bf16[2,1024,384]{2,1,0:T(8,128)(2,1)} %pad_maximum_fusion.8), channel_id=1, source_target_pairs={{0,8},{8,16},{16,24},{24,32},{32,40},{40,48},{48,56},{56,64},{64,7... | collective-permute-start | bytes 4718600 | tf_op jit(solution)/shard_map/ppermute | solution.py:20
  180.1 105.7 %collective-permute-start.4 = (bf16[2,1024,384]{2,1,0:T(8,128)(2,1)}, bf16[2,1024,384]{2,1,0:T(8,128)(2,1)}, u32[]{:S(2)}, u32[]{:S(2)}) collective-permute-start(bf16[2,1024,384]{2,1,0:T(8,128)(2,1)} %pad_maximum_fusion.7), channel_id=1, source_target_pairs={{8,0},{16,8},{24,16},{32,24},{40,32},{48,40},{56,48},{64,56},{72,6... | collective-permute-start | bytes 4718600 | tf_op jit(solution)/shard_map/ppermute | solution.py:20
  285.8 2.1 copy-start
  293.8 25.4 %all-to-all-start.3 = ((bf16[2,1024,384]{2,0,1:T(2,128)(2,1)}), bf16[2,1024,384]{2,0,1:T(2,128)(2,1)S(1)}, u32[]{:S(2)}, u32[]{:S(2)}) async-start(bf16[2,1024,384]{2,0,1:T(2,128)(2,1)} %copy.168), calls=%async_computation.3 | async-start | bytes 3145728 | tf_op jit(solution)/shard_map/all_to_all | solution.py:315

commit v6 on v4

--- a/solution.py
+++ b/solution.py
@@ -119,7 +119,9 @@
     return field.transpose(1, 2, 0, 3).reshape(count * TILE, heads * HD)
 
 
-def attention_kernel(index_ref, q_ref, do_ref, k_ref, v_ref, att_ref, dq_ref, dk_ref, dv_ref, kbuf, vbuf):
+def attention_kernel(
+    edges, index_ref, q_ref, do_ref, k_ref, v_ref, att_ref, dq_ref, dk_ref, dv_ref, near_ref, kbuf, vbuf
+):
     heads = q_ref.shape[1] // HD
     tiles = q_ref.shape[0] // TILE
     slots = index_ref.shape[0] // (heads * tiles)
@@ -176,24 +178,34 @@
         return carry
 
     lax.fori_loop(0, heads * tiles, step, 0)
-
-
-def attend(pool_index, query_rows, grad_rows, pool_keys, pool_values):
+    span_rows = near_ref.shape[1]
+    for part, start in enumerate(edges):
+        for row in range(0, span_rows, TILE):
+            near_ref[2 * part, row : row + TILE, :] = dk_ref[
+                start + row : start + row + TILE, :
+            ].astype(jnp.bfloat16)
+            near_ref[2 * part + 1, row : row + TILE, :] = dv_ref[
+                start + row : start + row + TILE, :
+            ].astype(jnp.bfloat16)
+
+
+def attend(pool_index, query_rows, grad_rows, pool_keys, pool_values, edges):
     count, width = query_rows.shape
     pool_rows = pool_keys.shape[0]
     slots = pool_index.shape[-1]
     vmem = pltpu.VMEM
     flops = 2 * 7 * count * slots * TILE * width
     return pl.pallas_call(
-        attention_kernel,
+        functools.partial(attention_kernel, edges),
         out_shape=(
             jax.ShapeDtypeStruct((count, width), jnp.bfloat16),
             jax.ShapeDtypeStruct((count, width), jnp.bfloat16),
             jax.ShapeDtypeStruct((pool_rows, width), jnp.float32),
             jax.ShapeDtypeStruct((pool_rows, width), jnp.float32),
+            jax.ShapeDtypeStruct((2 * len(edges), count, width), jnp.bfloat16),
         ),
         in_specs=[pl.BlockSpec(memory_space=pltpu.SMEM)] + [pl.BlockSpec(memory_space=vmem)] * 4,
-        out_specs=tuple(pl.BlockSpec(memory_space=vmem) for _ in range(4)),
+        out_specs=tuple(pl.BlockSpec(memory_space=vmem) for _ in range(5)),
         scratch_shapes=[
             pltpu.VMEM((slots * TILE, HD), jnp.bfloat16),
             pltpu.VMEM((slots * TILE, HD), jnp.bfloat16),
@@ -264,10 +276,11 @@
     slot_numbers = jnp.arange(global_tiles.shape[1], dtype=jnp.int32)
     global_slot = jnp.sum(jnp.where(matches, slot_numbers[None, None, None, :], 0), axis=-1)
     pool_index = jnp.where(inside, relative, span + global_slot)
-    attended, query_rows, key_pool, value_pool = attend(
-        pool_index, moved[0], moved[3], pool_keys, pool_values
-    )
     frame_rows = per_frame * TILE
+    edges = ((reach - 1) * frame_rows, (reach + 1) * frame_rows)
+    attended, query_rows, key_pool, value_pool, near = attend(
+        pool_index, moved[0], moved[3], pool_keys, pool_values, edges
+    )
     centre = reach * frame_rows
     key_grad = key_pool[centre : centre + frame_rows]
     value_grad = value_pool[centre : centre + frame_rows]
@@ -275,10 +288,10 @@
     lower = (reach - offset) * frame_rows
     returned = (
         passed_along(
-            key_pool[lower : lower + frame_rows].astype(jnp.bfloat16), "blk", -offset
+            near[0], "blk", -offset
         ).astype(jnp.float32),
         passed_along(
-            value_pool[lower : lower + frame_rows].astype(jnp.bfloat16), "blk", -offset
+            near[1], "blk", -offset
         ).astype(jnp.float32),
     )
     key_grad = key_grad + returned[0]
@@ -286,10 +299,10 @@
     upper = (reach + offset) * frame_rows
     returned = (
         passed_along(
-            key_pool[upper : upper + frame_rows].astype(jnp.bfloat16), "blk", offset
+            near[2], "blk", offset
         ).astype(jnp.float32),
         passed_along(
-            value_pool[upper : upper + frame_rows].astype(jnp.bfloat16), "blk", offset
+            near[3], "blk", offset
         ).astype(jnp.float32),
     )
     key_grad = key_grad + returned[0]

time: 314 us -> 315 us (level)
  other arithmetic: 25.2 us -> 16.5 us
  Pallas kernels: 127 us -> 135 us
    another operation x2 -> x0, other arithmetic: 8.42 us -> none
    pallas_call x2, Pallas kernels: 90 us -> 97.1 us  [butterfly_sum(): pl.pallas_call(functools.partial(reduce_kernel, count), out_shape=jax.Sha...]
    slice x2 -> x0, local copies, waits for them, and re-layouts: 3.86 us -> none  [the longest x1 2.56 us: per_device(): key_pool[lower:lower + frame_rows].astype(jnp.bfloat16)]
    squeeze x0 -> x1, local copies, waits for them, and re-layouts: none -> 3.65 us  [per_device(): near[0]]
  transfers between devices with their start and end apart: 12 -> 12, of which waited for: 5 -> 5; matrix products, arithmetic and copies ran while one was open for 18% -> 15% of each run, Pallas kernels for 29% -> 31%
where the time goes in v6:
time: 315 us; the launch traced here: 314 us
  Pallas kernels  135 us (43%)
  starting transfers between devices  67.4 us (21%)
  local copies, waits for them, and re-layouts  45.6 us (14%)
  waiting for transfers between devices  44.2 us (14%)
  other arithmetic  16.5 us (5%)
  matrix products  4.15 us (1%)
    pallas_call x2, Pallas kernels, butterfly_sum(): pl.pallas_call(functools.partial(reduce_kernel, count), out_shape=jax.Sha...  97.1 us
    ppermute x8, starting transfers between devices, passed_along(): return lax.ppermute(block, axis, route)  44.6 us
    pallas_call x1, Pallas kernels, attend(): pl.pallas_call(functools.partial(attention_kernel, edges), out_shape=(jax...  37.7 us
    ppermute x8, waiting for transfers between devices, passed_along(): return lax.ppermute(block, axis, route)  22.5 us
    all_to_all x1, waiting for transfers between devices, per_device(): lax.all_to_all(jnp.stack([keys, values]), 'head', split_axis=2, concat_ax...  15.4 us
    all_to_all x1, starting transfers between devices, per_device(): lax.all_to_all(jnp.stack([attended, query_rows]), 'head', split_axis=1, c...  7.19 us
  transfers between devices with their start and end apart: 12, of which 5 were waited for; matrix products, arithmetic and copies ran while one was open for 15% of the time, Pallas kernels for 31%

profile of v6, /device:TPU:160, one launch (start us, length us, event | category | flops | bytes accessed | tf_op | source)
XLA Modules:
  0.0 313.7 jit_solution(8326349519361228028)
XLA Ops:
  2.1 2.9 copy.149
  5.1 5.8 %all-to-all-start.1 = ((bf16[2,128,3072]{1,0,2:T(2,128)(2,1)}), bf16[2,128,3072]{1,0,2:T(2,128)(2,1)S(1)}, u32[]{:S(2)}, u32[]{:S(2)}) async-start(bf16[2,128,3072]{1,0,2:T(2,128)(2,1)} %copy.149), calls=%async_computation.1 | async-start | bytes 3145728 | tf_op jit(solution)/shard_map/all_to_all | solution.py:230
  12.3 2.9 copy.147
  15.2 15.4 %all-to-all-done.1 = bf16[2,128,3072]{1,0,2:T(2,128)(2,1)S(1)} async-done(((bf16[2,128,3072]{1,0,2:T(2,128)(2,1)}), bf16[2,128,3072]{1,0,2:T(2,128)(2,1)S(1)}, u32[]{:S(2)}, u32[]{:S(2)}) %all-to-all-start.1) | async-done | bytes 1572896 | tf_op jit(solution)/shard_map/all_to_all | solution.py:230
  30.7 4.2 %all-to-all-start = ((bf16[2,128,3072]{1,0,2:T(2,128)(2,1)}), bf16[2,128,3072]{1,0,2:T(2,128)(2,1)S(1)}, u32[]{:S(2)}, u32[]{:S(2)}) async-start(bf16[2,128,3072]{1,0,2:T(2,128)(2,1)} %copy.147), calls=%async_computation | async-start | bytes 3145728 | tf_op jit(solution)/shard_map/all_to_all | solution.py:233
  37.5 1.9 collective-permute-start.2
  39.4 7.9 %collective-permute-start.3 = (bf16[1024,384]{1,0:T(8,128)(2,1)}, bf16[1024,384]{1,0:T(8,128)(2,1)}, u32[]{:S(2)}, u32[]{:S(2)}) collective-permute-start(bf16[1024,384]{1,0:T(8,128)(2,1)} %bitcast.116), channel_id=1, source_target_pairs={{8,0},{16,8},{24,16},{32,24},{40,32},{48,40},{56,48},{64,56},{72,6... | collective-permute-start | bytes 2359304 | tf_op jit(solution)/shard_map/ppermute | solution.py:20
  48.4 1.9 collective-permute-start
  50.3 8.0 %collective-permute-start.1 = (bf16[1024,384]{1,0:T(8,128)(2,1)}, bf16[1024,384]{1,0:T(8,128)(2,1)}, u32[]{:S(2)}, u32[]{:S(2)}) collective-permute-start(bf16[1024,384]{1,0:T(8,128)(2,1)} %bitcast.113), channel_id=1, source_target_pairs={{8,0},{16,8},{24,16},{32,24},{40,32},{48,40},{56,48},{64,56},{72,6... | collective-permute-start | bytes 2359304 | tf_op jit(solution)/shard_map/ppermute | solution.py:20
  64.9 44.3 %shard_map.84 = bf16[32,48,128]{2,1,0:T(8,128)(2,1)} custom-call(bf16[32,48,128]{2,1,0:T(8,128)(2,1)} %reshape.63.x_ref), custom_call_target="tpu_custom_call" | custom-call | tf_op jit(solution)/shard_map/pallas_call | solution.py:92
  114.8 1.7 pad_maximum_fusion.1.v_ref
  118.2 1.7 pad_maximum_fusion.k_ref
  119.9 37.7 %shard_map.85 = (bf16[1024,384]{1,0:T(8,128)(2,1)}, bf16[1024,384]{1,0:T(8,128)(2,1)}, f32[3328,384]{1,0:T(8,128)}, f32[3328,384]{1,0:T(8,128)}, bf16[4,1024,384]{2,1,0:T(8,128)(2,1)}) custom-call(s32[216]{0:T(256)} %reshape.61.index_ref, bf16[1024,384]{1,0:T(8,128)(2,1)} %bitcast.131, bf16[1024,384]{1,0:T(8,128)(2,1)} %bitcast.130, ...), custom_call_target="tpu_custom_call" | custom-call | flops 6341787648 | bytes 18481152 | tf_op jit(solution)/shard_map/pallas_call | solution.py:198
  159.2 2.8 copy.159
  161.9 7.2 %all-to-all-start.2 = ((bf16[2,1024,384]{2,0,1:T(2,128)(2,1)}), bf16[2,1024,384]{2,0,1:T(2,128)(2,1)S(1)}, u32[]{:S(2)}, u32[]{:S(2)}) async-start(bf16[2,1024,384]{2,0,1:T(2,128)(2,1)} %copy.159), calls=%async_computation.2 | async-start | bytes 3145728 | tf_op jit(solution)/shard_map/all_to_all | solution.py:327
  171.3 52.8 %shard_map.86 = f32[32,48,128]{2,1,0:T(8,128)} custom-call(f32[32,48,128]{2,1,0:T(8,128)} %reshape_reshape.3.x_ref), custom_call_target="tpu_custom_call" | custom-call | tf_op jit(solution)/shard_map/pallas_call | solution.py:92
  224.1 3.7 %slice_bitcast_fusion.3 = (bf16[1024,384]{1,0:T(8,128)(2,1)}, bf16[1024,384]{1,0:T(8,128)(2,1)}, bf16[1024,384]{1,0:T(8,128)(2,1)}, bf16[1024,384]{1,0:T(8,128)(2,1)}) fusion(bf16[4,1024,384]{2,1,0:T(8,128)(2,1)} %get-tuple-element.12), kind=kLoop, calls=%fused_computation.24 | loop fusion | bytes 6291456 | tf_op jit(solution)/shard_map/squeeze | solution.py:291
  227.8 13.1 %collective-permute-start.4 = (bf16[1024,384]{1,0:T(8,128)(2,1)}, bf16[1024,384]{1,0:T(8,128)(2,1)}, u32[]{:S(2)}, u32[]{:S(2)}) collective-permute-start(bf16[1024,384]{1,0:T(8,128)(2,1)} %get-tuple-element.14), channel_id=1, source_target_pairs={{8,0},{16,8},{24,16},{32,24},{40,32},{48,40},{56,48},{64,56},{72,6... | collective-permute-start | bytes 2359304 | tf_op jit(solution)/shard_map/ppermute | solution.py:20
  240.9 1.9 collective-permute-start.5
  243.1 7.9 %collective-permute-start.6 = (bf16[1024,384]{1,0:T(8,128)(2,1)}, bf16[1024,384]{1,0:T(8,128)(2,1)S(1)}, u32[]{:S(2)}, u32[]{:S(2)}) collective-permute-start(bf16[1024,384]{1,0:T(8,128)(2,1)} %get-tuple-element.16), channel_id=1, source_target_pairs={{8,0},{16,8},{24,16},{32,24},{40,32},{48,40},{56,48},{64,56},{72,6... | collective-permute-start | bytes 2359304 | tf_op jit(solution)/shard_map/ppermute | solution.py:20
  251.0 1.9 collective-permute-start.7
  254.0 2.4 copy.172
  258.8 14.1 %collective-permute-done.5 = bf16[1024,384]{1,0:T(8,128)(2,1)} collective-permute-done((bf16[1024,384]{1,0:T(8,128)(2,1)}, bf16[1024,384]{1,0:T(8,128)(2,1)}, u32[]{:S(2)}, u32[]{:S(2)}) %collective-permute-start.5) | collective-permute-done | bytes 786464 | tf_op jit(solution)/shard_map/ppermute | solution.py:20
  272.9 2.3 fusion.4
  275.1 4.9 %collective-permute-done.6 = bf16[1024,384]{1,0:T(8,128)(2,1)S(1)} collective-permute-done((bf16[1024,384]{1,0:T(8,128)(2,1)}, bf16[1024,384]{1,0:T(8,128)(2,1)S(1)}, u32[]{:S(2)}, u32[]{:S(2)}) %collective-permute-start.6) | collective-permute-done | bytes 786464 | tf_op jit(solution)/shard_map/ppermute | solution.py:20
  280.0 3.5 %collective-permute-done.7 = bf16[1024,384]{1,0:T(8,128)(2,1)} collective-permute-done((bf16[1024,384]{1,0:T(8,128)(2,1)}, bf16[1024,384]{1,0:T(8,128)(2,1)}, u32[]{:S(2)}, u32[]{:S(2)}) %collective-permute-start.7) | collective-permute-done | bytes 786464 | tf_op jit(solution)/shard_map/ppermute | solution.py:20
  283.5 2.0 fusion.5
  285.7 2.8 copy.168
  288.5 5.7 %all-to-all-start.3 = ((bf16[2,1024,384]{2,0,1:T(2,128)(2,1)}), bf16[2,1024,384]{2,0,1:T(2,128)(2,1)S(1)}, u32[]{:S(2)}, u32[]{:S(2)}) async-start(bf16[2,1024,384]{2,0,1:T(2,128)(2,1)} %copy.168), calls=%async_computation.3 | async-start | bytes 3145728 | tf_op jit(solution)/shard_map/all_to_all | solution.py:330
  294.3 2.9 fusion.25
  300.9 6.2 %all-to-all-done.3 = bf16[2,1024,384]{2,0,1:T(2,128)(2,1)S(1)} async-done(((bf16[2,1024,384]{2,0,1:T(2,128)(2,1)}), bf16[2,1024,384]{2,0,1:T(2,128)(2,1)S(1)}, u32[]{:S(2)}, u32[]{:S(2)}) %all-to-all-start.3) | async-done | bytes 1572896 | tf_op jit(solution)/shard_map/all_to_all | solution.py:330
  307.1 2.9 fusion.24
  (68 shorter events, 35.5 us)
Async XLA Ops:
  5.1 25.6 %all-to-all-start.1 = ((bf16[2,128,3072]{1,0,2:T(2,128)(2,1)}), bf16[2,128,3072]{1,0,2:T(2,128)(2,1)S(1)}, u32[]{:S(2)}, u32[]{:S(2)}) async-start(bf16[2,128,3072]{1,0,2:T(2,128)(2,1)} %copy.149), calls=%async_computation.1 | async-start | bytes 3145728 | tf_op jit(solution)/shard_map/all_to_all | solution.py:230
  15.2 19.6 %copy-start.6 = (s32[3,256,9]{1,0,2:T(4,128)S(1)}, s32[3,256,9]{1,0,2:T(4,128)}, u32[]{:S(2)}) copy-start(s32[3,256,9]{1,0,2:T(4,128)} %param.9) | copy-start | bytes 82948
  30.7 78.5 %all-to-all-start = ((bf16[2,128,3072]{1,0,2:T(2,128)(2,1)}), bf16[2,128,3072]{1,0,2:T(2,128)(2,1)S(1)}, u32[]{:S(2)}, u32[]{:S(2)}) async-start(bf16[2,128,3072]{1,0,2:T(2,128)(2,1)} %copy.147), calls=%async_computation | async-start | bytes 3145728 | tf_op jit(solution)/shard_map/all_to_all | solution.py:233
  37.5 74.7 %collective-permute-start.2 = (bf16[1024,384]{1,0:T(8,128)(2,1)}, bf16[1024,384]{1,0:T(8,128)(2,1)}, u32[]{:S(2)}, u32[]{:S(2)}) collective-permute-start(bf16[1024,384]{1,0:T(8,128)(2,1)} %bitcast.115), channel_id=1, source_target_pairs={{0,8},{8,16},{16,24},{24,32},{32,40},{40,48},{48,56},{56,64},{64,7... | collective-permute-start | bytes 2359304 | tf_op jit(solution)/shard_map/ppermute | solution.py:20
  39.4 72.8 %collective-permute-start.3 = (bf16[1024,384]{1,0:T(8,128)(2,1)}, bf16[1024,384]{1,0:T(8,128)(2,1)}, u32[]{:S(2)}, u32[]{:S(2)}) collective-permute-start(bf16[1024,384]{1,0:T(8,128)(2,1)} %bitcast.116), channel_id=1, source_target_pairs={{8,0},{16,8},{24,16},{32,24},{40,32},{48,40},{56,48},{64,56},{72,6... | collective-permute-start | bytes 2359304 | tf_op jit(solution)/shard_map/ppermute | solution.py:20
  48.4 68.1 %collective-permute-start = (bf16[1024,384]{1,0:T(8,128)(2,1)}, bf16[1024,384]{1,0:T(8,128)(2,1)}, u32[]{:S(2)}, u32[]{:S(2)}) collective-permute-start(bf16[1024,384]{1,0:T(8,128)(2,1)} %bitcast.112), channel_id=1, source_target_pairs={{0,8},{8,16},{16,24},{24,32},{32,40},{40,48},{48,56},{56,64},{64,7... | collective-permute-start | bytes 2359304 | tf_op jit(solution)/shard_map/ppermute | solution.py:20
  50.3 66.2 %collective-permute-start.1 = (bf16[1024,384]{1,0:T(8,128)(2,1)}, bf16[1024,384]{1,0:T(8,128)(2,1)}, u32[]{:S(2)}, u32[]{:S(2)}) collective-permute-start(bf16[1024,384]{1,0:T(8,128)(2,1)} %bitcast.113), channel_id=1, source_target_pairs={{8,0},{16,8},{24,16},{32,24},{40,32},{48,40},{56,48},{64,56},{72,6... | collective-permute-start | bytes 2359304 | tf_op jit(solution)/shard_map/ppermute | solution.py:20
  59.7 1.3 copy-start.4
  110.6 1.3 copy-start.5
  111.9 1.1 copy-start.2
  114.8 1.7 copy-start.1
  161.9 126.6 %all-to-all-start.2 = ((bf16[2,1024,384]{2,0,1:T(2,128)(2,1)}), bf16[2,1024,384]{2,0,1:T(2,128)(2,1)S(1)}, u32[]{:S(2)}, u32[]{:S(2)}) async-start(bf16[2,1024,384]{2,0,1:T(2,128)(2,1)} %copy.159), calls=%async_computation.2 | async-start | bytes 3145728 | tf_op jit(solution)/shard_map/all_to_all | solution.py:327
  224.1 18.7 %copy-start.3 = (f32[32,48,128]{2,1,0:T(8,128)S(1)}, f32[32,48,128]{2,1,0:T(8,128)}, u32[]{:S(2)}) copy-start(f32[32,48,128]{2,1,0:T(8,128)} %shard_map.86) | copy-start | bytes 2359300
  227.8 31.0 %collective-permute-start.4 = (bf16[1024,384]{1,0:T(8,128)(2,1)}, bf16[1024,384]{1,0:T(8,128)(2,1)}, u32[]{:S(2)}, u32[]{:S(2)}) collective-permute-start(bf16[1024,384]{1,0:T(8,128)(2,1)} %get-tuple-element.14), channel_id=1, source_target_pairs={{8,0},{16,8},{24,16},{32,24},{40,32},{48,40},{56,48},{64,56},{72,6... | collective-permute-start | bytes 2359304 | tf_op jit(solution)/shard_map/ppermute | solution.py:20
  240.9 31.9 %collective-permute-start.5 = (bf16[1024,384]{1,0:T(8,128)(2,1)}, bf16[1024,384]{1,0:T(8,128)(2,1)}, u32[]{:S(2)}, u32[]{:S(2)}) collective-permute-start(bf16[1024,384]{1,0:T(8,128)(2,1)} %get-tuple-element.17), channel_id=1, source_target_pairs={{0,8},{8,16},{16,24},{24,32},{32,40},{40,48},{48,56},{56,64},{64,7... | collective-permute-start | bytes 2359304 | tf_op jit(solution)/shard_map/ppermute | solution.py:20
  243.1 36.9 %collective-permute-start.6 = (bf16[1024,384]{1,0:T(8,128)(2,1)}, bf16[1024,384]{1,0:T(8,128)(2,1)S(1)}, u32[]{:S(2)}, u32[]{:S(2)}) collective-permute-start(bf16[1024,384]{1,0:T(8,128)(2,1)} %get-tuple-element.16), channel_id=1, source_target_pairs={{8,0},{16,8},{24,16},{32,24},{40,32},{48,40},{56,48},{64,56},{72,6... | collective-permute-start | bytes 2359304 | tf_op jit(solution)/shard_map/ppermute | solution.py:20
  251.0 32.6 %collective-permute-start.7 = (bf16[1024,384]{1,0:T(8,128)(2,1)}, bf16[1024,384]{1,0:T(8,128)(2,1)}, u32[]{:S(2)}, u32[]{:S(2)}) collective-permute-start(bf16[1024,384]{1,0:T(8,128)(2,1)} %get-tuple-element.15), channel_id=1, source_target_pairs={{0,8},{8,16},{16,24},{24,32},{32,40},{40,48},{48,56},{56,64},{64,7... | collective-permute-start | bytes 2359304 | tf_op jit(solution)/shard_map/ppermute | solution.py:20
  257.7 15.2 %copy-start = (f32[8,128,3,128]{3,2,1,0:T(4,128)S(1)}, f32[8,128,3,128]{3,2,1,0:T(4,128)}, u32[]{:S(2)}) copy-start(f32[8,128,3,128]{3,2,1,0:T(4,128)} %copy.172) | copy-start | bytes 4718596
  288.5 18.6 %all-to-all-start.3 = ((bf16[2,1024,384]{2,0,1:T(2,128)(2,1)}), bf16[2,1024,384]{2,0,1:T(2,128)(2,1)S(1)}, u32[]{:S(2)}, u32[]{:S(2)}) async-start(bf16[2,1024,384]{2,0,1:T(2,128)(2,1)} %copy.168), calls=%async_computation.3 | async-start | bytes 3145728 | tf_op jit(solution)/shard_map/all_to_all | solution.py:330

commit v7 on v4

--- a/solution.py
+++ b/solution.py
@@ -314,10 +314,9 @@
     forward_back = lax.all_to_all(
         jnp.stack([attended, query_rows]), "head", split_axis=1, concat_axis=2, tiled=True
     )
-    backward_back = lax.all_to_all(
-        jnp.stack([key_rows, value_rows]), "head", split_axis=1, concat_axis=2, tiled=True
-    )
-    results = (forward_back[0], forward_back[1], backward_back[0], backward_back[1])
+    key_back = lax.all_to_all(key_rows, "head", split_axis=0, concat_axis=1, tiled=True)
+    value_back = lax.all_to_all(value_rows, "head", split_axis=0, concat_axis=1, tiled=True)
+    results = (forward_back[0], forward_back[1], key_back, value_back)
     return (results[0], results[1], results[2], results[3])
 
 

time: 314 us -> 324 us (1.032)
  waiting for transfers between devices: 42.9 us -> 55.1 us
  Pallas kernels: 127 us -> 136 us
  local copies, waits for them, and re-layouts: 47 us -> 38.7 us
  other arithmetic: 25.2 us -> 19.7 us
    all_to_all x1, waiting for transfers between devices: 0.01 us -> 10.9 us  [per_device(): lax.all_to_all(jnp.stack([attended, query_rows]), 'head', split_axis=1, c...]
    another operation x5 -> x2, other arithmetic: 13.1 us -> 3.15 us
    pallas_call x2, Pallas kernels: 90 us -> 99 us  [butterfly_sum(): pl.pallas_call(functools.partial(reduce_kernel, count), out_shape=jax.Sha...]
    all_to_all x1 -> x2, starting transfers between devices: 6.4 us -> 13.6 us  [the longest x1 7.49 us: per_device(): lax.all_to_all(value_rows, 'head', split_axis=0, concat_axis=1, tiled=True)]
    convert_element_type x0 -> x2, other arithmetic: none -> 5.82 us  [the longest x1 3.17 us: per_device(): value_rows = value_grad.astype(jnp.bfloat16)]
    ppermute x8, starting transfers between devices: 42.9 us -> 38.6 us  [passed_along(): return lax.ppermute(block, axis, route)]
    slice x7 -> x4, local copies, waits for them, and re-layouts: 10.3 us -> 6.51 us  [the longest x3 4.59 us: per_device(): results = (forward_back[0], forward_back[1], key_back, value_back)]
    all_to_all x1 -> x2, waiting for transfers between devices: 6.21 us -> 8.12 us  [the longest x1 8.12 us: per_device(): lax.all_to_all(key_rows, 'head', split_axis=0, concat_axis=1, tiled=True)]
  transfers between devices with their start and end apart: 12 -> 13, of which waited for: 5 -> 5; matrix products, arithmetic and copies ran while one was open for 18% -> 12% of each run, Pallas kernels for 29% -> 31%
where the time goes in v7:
time: 324 us; the launch traced here: 321 us
  Pallas kernels  136 us (42%)
  starting transfers between devices  66.9 us (21%)
  waiting for transfers between devices  55.1 us (17%)
  local copies, waits for them, and re-layouts  38.7 us (12%)
  other arithmetic  19.7 us (6%)
  matrix products  4.15 us (1%)
    pallas_call x2, Pallas kernels, butterfly_sum(): pl.pallas_call(functools.partial(reduce_kernel, count), out_shape=jax.Sha...  99 us
    ppermute x8, starting transfers between devices, passed_along(): return lax.ppermute(block, axis, route)  38.6 us
    pallas_call x1, Pallas kernels, attend(): pl.pallas_call(attention_kernel, out_shape=(jax.ShapeDtypeStruct((count,...  36.7 us
    ppermute x8, waiting for transfers between devices, passed_along(): return lax.ppermute(block, axis, route)  20.7 us
    all_to_all x1, waiting for transfers between devices, per_device(): lax.all_to_all(jnp.stack([keys, values]), 'head', split_axis=2, concat_ax...  15.4 us
    all_to_all x1, waiting for transfers between devices, per_device(): lax.all_to_all(jnp.stack([attended, query_rows]), 'head', split_axis=1, c...  10.9 us
    all_to_all x1, waiting for transfers between devices, per_device(): lax.all_to_all(key_rows, 'head', split_axis=0, concat_axis=1, tiled=True)  8.12 us
    all_to_all x1, starting transfers between devices, per_device(): lax.all_to_all(value_rows, 'head', split_axis=0, concat_axis=1, tiled=True)  7.49 us
  transfers between devices with their start and end apart: 13, of which 5 were waited for; matrix products, arithmetic and copies ran while one was open for 12% of the time, Pallas kernels for 31%

profile of v7, /device:TPU:160, one launch (start us, length us, event | category | flops | bytes accessed | tf_op | source)
XLA Modules:
  0.0 321.3 jit_solution(5800938059447618438)
XLA Ops:
  2.1 2.9 copy.147
  5.1 5.8 %all-to-all-start.1 = ((bf16[2,128,3072]{1,0,2:T(2,128)(2,1)}), bf16[2,128,3072]{1,0,2:T(2,128)(2,1)S(1)}, u32[]{:S(2)}, u32[]{:S(2)}) async-start(bf16[2,128,3072]{1,0,2:T(2,128)(2,1)} %copy.147), calls=%async_computation.1 | async-start | bytes 3145728 | tf_op jit(solution)/shard_map/all_to_all | solution.py:218
  12.4 2.9 copy.145
  15.3 15.4 %all-to-all-done.1 = bf16[2,128,3072]{1,0,2:T(2,128)(2,1)S(1)} async-done(((bf16[2,128,3072]{1,0,2:T(2,128)(2,1)}), bf16[2,128,3072]{1,0,2:T(2,128)(2,1)S(1)}, u32[]{:S(2)}, u32[]{:S(2)}) %all-to-all-start.1) | async-done | bytes 1572896 | tf_op jit(solution)/shard_map/all_to_all | solution.py:218
  30.7 4.2 %all-to-all-start = ((bf16[2,128,3072]{1,0,2:T(2,128)(2,1)}), bf16[2,128,3072]{1,0,2:T(2,128)(2,1)S(1)}, u32[]{:S(2)}, u32[]{:S(2)}) async-start(bf16[2,128,3072]{1,0,2:T(2,128)(2,1)} %copy.145), calls=%async_computation | async-start | bytes 3145728 | tf_op jit(solution)/shard_map/all_to_all | solution.py:221
  37.4 1.9 collective-permute-start.2
  39.4 7.9 %collective-permute-start.3 = (bf16[1024,384]{1,0:T(8,128)(2,1)}, bf16[1024,384]{1,0:T(8,128)(2,1)}, u32[]{:S(2)}, u32[]{:S(2)}) collective-permute-start(bf16[1024,384]{1,0:T(8,128)(2,1)} %bitcast.98), channel_id=1, source_target_pairs={{8,0},{16,8},{24,16},{32,24},{40,32},{48,40},{56,48},{64,56},{72,6... | collective-permute-start | bytes 2359304 | tf_op jit(solution)/shard_map/ppermute | solution.py:20
  48.4 1.9 collective-permute-start
  50.3 7.9 %collective-permute-start.1 = (bf16[1024,384]{1,0:T(8,128)(2,1)}, bf16[1024,384]{1,0:T(8,128)(2,1)}, u32[]{:S(2)}, u32[]{:S(2)}) collective-permute-start(bf16[1024,384]{1,0:T(8,128)(2,1)} %bitcast.95), channel_id=1, source_target_pairs={{8,0},{16,8},{24,16},{32,24},{40,32},{48,40},{56,48},{64,56},{72,6... | collective-permute-start | bytes 2359304 | tf_op jit(solution)/shard_map/ppermute | solution.py:20
  64.7 44.6 %shard_map.84 = bf16[32,48,128]{2,1,0:T(8,128)(2,1)} custom-call(bf16[32,48,128]{2,1,0:T(8,128)(2,1)} %reshape.65.x_ref), custom_call_target="tpu_custom_call" | custom-call | tf_op jit(solution)/shard_map/pallas_call | solution.py:92
  114.9 1.8 pad_maximum_fusion.1.v_ref
  116.7 1.7 pad_maximum_fusion.2
  118.3 1.7 pad_maximum_fusion.k_ref
  120.0 36.7 %shard_map.85 = (bf16[1024,384]{1,0:T(8,128)(2,1)}, bf16[1024,384]{1,0:T(8,128)(2,1)}, f32[3328,384]{1,0:T(8,128)}, f32[3328,384]{1,0:T(8,128)}) custom-call(s32[216]{0:T(256)} %reshape.63.index_ref, bf16[1024,384]{1,0:T(8,128)(2,1)} %bitcast.116, bf16[1024,384]{1,0:T(8,128)(2,1)} %bitcast.115, bf16[3328,384]{1,0:T(8,128)(2,1)} %pad_maximum_fusion.k_ref, ...), custom_call_target="tpu_custom_call" | custom-call | flops 6341787648 | bytes 18481152 | tf_op jit(solution)/shard_map/pallas_call | solution.py:187
  156.8 2.9 convert.9
  161.0 8.2 %collective-permute-start.6 = (bf16[1024,384]{1,0:T(8,128)(2,1)}, bf16[1024,384]{1,0:T(8,128)(2,1)}, u32[]{:S(2)}, u32[]{:S(2)}) collective-permute-start(bf16[1024,384]{1,0:T(8,128)(2,1)} %get-tuple-element.12), channel_id=1, source_target_pairs={{8,0},{16,8},{24,16},{32,24},{40,32},{48,40},{56,48},{64,56},{72,6... | collective-permute-start | bytes 2359304 | tf_op jit(solution)/shard_map/ppermute | solution.py:20
  169.1 2.1 collective-permute-start.7
  173.6 54.4 %shard_map.86 = f32[32,48,128]{2,1,0:T(8,128)} custom-call(f32[32,48,128]{2,1,0:T(8,128)} %reshape_reshape.3.x_ref), custom_call_target="tpu_custom_call" | custom-call | tf_op jit(solution)/shard_map/pallas_call | solution.py:92
  228.0 1.9 fusion.27
  232.3 3.2 fusion
  235.5 7.5 %all-to-all-start.4 = ((bf16[8,128,384]{2,1,0:T(8,128)(2,1)}), bf16[8,128,384]{2,1,0:T(8,128)(2,1)S(1)}, u32[]{:S(2)}, u32[]{:S(2)}) async-start(bf16[8,128,384]{2,1,0:T(8,128)(2,1)} %bitcast.104), calls=%async_computation.4 | async-start | bytes 1572864 | tf_op jit(solution)/shard_map/all_to_all | solution.py:318
  244.3 6.9 %collective-permute-start.4 = (bf16[1024,384]{1,0:T(8,128)(2,1)}, bf16[1024,384]{1,0:T(8,128)(2,1)S(1)}, u32[]{:S(2)}, u32[]{:S(2)}) collective-permute-start(bf16[1024,384]{1,0:T(8,128)(2,1)} %get-tuple-element.14), channel_id=1, source_target_pairs={{8,0},{16,8},{24,16},{32,24},{40,32},{48,40},{56,48},{64,56},{72,6... | collective-permute-start | bytes 2359304 | tf_op jit(solution)/shard_map/ppermute | solution.py:20
  251.2 1.9 collective-permute-start.5
  256.5 6.1 %collective-permute-done.4 = bf16[1024,384]{1,0:T(8,128)(2,1)S(1)} collective-permute-done((bf16[1024,384]{1,0:T(8,128)(2,1)}, bf16[1024,384]{1,0:T(8,128)(2,1)S(1)}, u32[]{:S(2)}, u32[]{:S(2)}) %collective-permute-start.4) | collective-permute-done | bytes 786464 | tf_op jit(solution)/shard_map/ppermute | solution.py:20
  262.6 14.6 %collective-permute-done.5 = bf16[1024,384]{1,0:T(8,128)(2,1)S(1)} collective-permute-done((bf16[1024,384]{1,0:T(8,128)(2,1)}, bf16[1024,384]{1,0:T(8,128)(2,1)S(1)}, u32[]{:S(2)}, u32[]{:S(2)}) %collective-permute-start.5) | collective-permute-done | bytes 786464 | tf_op jit(solution)/shard_map/ppermute | solution.py:20
  277.2 2.6 fusion.1
  279.8 6.1 %all-to-all-start.3 = ((bf16[8,128,384]{2,1,0:T(8,128)(2,1)}), bf16[8,128,384]{2,1,0:T(8,128)(2,1)S(1)}, u32[]{:S(2)}, u32[]{:S(2)}) async-start(bf16[8,128,384]{2,1,0:T(8,128)(2,1)} %bitcast.38), calls=%async_computation.3 | async-start | bytes 1572864 | tf_op jit(solution)/shard_map/all_to_all | solution.py:317
  286.1 2.8 copy.157
  289.0 8.1 %all-to-all-done.3 = bf16[8,128,384]{2,1,0:T(8,128)(2,1)S(1)} async-done(((bf16[8,128,384]{2,1,0:T(8,128)(2,1)}), bf16[8,128,384]{2,1,0:T(8,128)(2,1)S(1)}, u32[]{:S(2)}, u32[]{:S(2)}) %all-to-all-start.3) | async-done | bytes 786464 | tf_op jit(solution)/shard_map/all_to_all | solution.py:317
  297.1 4.7 %all-to-all-start.2 = ((bf16[2,1024,384]{2,0,1:T(2,128)(2,1)}), bf16[2,1024,384]{2,0,1:T(2,128)(2,1)S(1)}, u32[]{:S(2)}, u32[]{:S(2)}) async-start(bf16[2,1024,384]{2,0,1:T(2,128)(2,1)} %copy.157), calls=%async_computation.2 | async-start | bytes 3145728 | tf_op jit(solution)/shard_map/all_to_all | solution.py:314
  303.8 10.9 %all-to-all-done.2 = bf16[2,1024,384]{2,0,1:T(2,128)(2,1)S(1)} async-done(((bf16[2,1024,384]{2,0,1:T(2,128)(2,1)}), bf16[2,1024,384]{2,0,1:T(2,128)(2,1)S(1)}, u32[]{:S(2)}, u32[]{:S(2)}) %all-to-all-start.2) | async-done | bytes 1572896 | tf_op jit(solution)/shard_map/all_to_all | solution.py:314
  314.6 2.9 fusion.24
  (70 shorter events, 35.3 us)
Async XLA Ops:
  5.1 25.6 %all-to-all-start.1 = ((bf16[2,128,3072]{1,0,2:T(2,128)(2,1)}), bf16[2,128,3072]{1,0,2:T(2,128)(2,1)S(1)}, u32[]{:S(2)}, u32[]{:S(2)}) async-start(bf16[2,128,3072]{1,0,2:T(2,128)(2,1)} %copy.147), calls=%async_computation.1 | async-start | bytes 3145728 | tf_op jit(solution)/shard_map/all_to_all | solution.py:218
  15.3 19.6 %copy-start.7 = (s32[3,256,9]{1,0,2:T(4,128)S(1)}, s32[3,256,9]{1,0,2:T(4,128)}, u32[]{:S(2)}) copy-start(s32[3,256,9]{1,0,2:T(4,128)} %param.9) | copy-start | bytes 82948
  30.7 78.6 %all-to-all-start = ((bf16[2,128,3072]{1,0,2:T(2,128)(2,1)}), bf16[2,128,3072]{1,0,2:T(2,128)(2,1)S(1)}, u32[]{:S(2)}, u32[]{:S(2)}) async-start(bf16[2,128,3072]{1,0,2:T(2,128)(2,1)} %copy.145), calls=%async_computation | async-start | bytes 3145728 | tf_op jit(solution)/shard_map/all_to_all | solution.py:221
  37.4 74.8 %collective-permute-start.2 = (bf16[1024,384]{1,0:T(8,128)(2,1)}, bf16[1024,384]{1,0:T(8,128)(2,1)}, u32[]{:S(2)}, u32[]{:S(2)}) collective-permute-start(bf16[1024,384]{1,0:T(8,128)(2,1)} %bitcast.97), channel_id=1, source_target_pairs={{0,8},{8,16},{16,24},{24,32},{32,40},{40,48},{48,56},{56,64},{64,7... | collective-permute-start | bytes 2359304 | tf_op jit(solution)/shard_map/ppermute | solution.py:20
  39.4 72.9 %collective-permute-start.3 = (bf16[1024,384]{1,0:T(8,128)(2,1)}, bf16[1024,384]{1,0:T(8,128)(2,1)}, u32[]{:S(2)}, u32[]{:S(2)}) collective-permute-start(bf16[1024,384]{1,0:T(8,128)(2,1)} %bitcast.98), channel_id=1, source_target_pairs={{8,0},{16,8},{24,16},{32,24},{40,32},{48,40},{56,48},{64,56},{72,6... | collective-permute-start | bytes 2359304 | tf_op jit(solution)/shard_map/ppermute | solution.py:20
  48.4 68.3 %collective-permute-start = (bf16[1024,384]{1,0:T(8,128)(2,1)}, bf16[1024,384]{1,0:T(8,128)(2,1)}, u32[]{:S(2)}, u32[]{:S(2)}) collective-permute-start(bf16[1024,384]{1,0:T(8,128)(2,1)} %bitcast.94), channel_id=1, source_target_pairs={{0,8},{8,16},{16,24},{24,32},{32,40},{40,48},{48,56},{56,64},{64,7... | collective-permute-start | bytes 2359304 | tf_op jit(solution)/shard_map/ppermute | solution.py:20
  50.3 66.3 %collective-permute-start.1 = (bf16[1024,384]{1,0:T(8,128)(2,1)}, bf16[1024,384]{1,0:T(8,128)(2,1)}, u32[]{:S(2)}, u32[]{:S(2)}) collective-permute-start(bf16[1024,384]{1,0:T(8,128)(2,1)} %bitcast.95), channel_id=1, source_target_pairs={{8,0},{16,8},{24,16},{32,24},{40,32},{48,40},{56,48},{64,56},{72,6... | collective-permute-start | bytes 2359304 | tf_op jit(solution)/shard_map/ppermute | solution.py:20
  59.5 1.3 copy-start.3
  110.7 1.3 copy-start.4
  112.0 1.1 copy-start.2
  114.9 1.8 copy-start.1
  156.8 14.5 %copy-start = (f32[3328,384]{1,0:T(8,128)S(1)}, f32[3328,384]{1,0:T(8,128)}, u32[]{:S(2)}) copy-start(f32[3328,384]{1,0:T(8,128)} %get-tuple-element.10) | copy-start | bytes 15335428
  161.0 71.4 %collective-permute-start.6 = (bf16[1024,384]{1,0:T(8,128)(2,1)}, bf16[1024,384]{1,0:T(8,128)(2,1)}, u32[]{:S(2)}, u32[]{:S(2)}) collective-permute-start(bf16[1024,384]{1,0:T(8,128)(2,1)} %get-tuple-element.12), channel_id=1, source_target_pairs={{8,0},{16,8},{24,16},{32,24},{40,32},{48,40},{56,48},{64,56},{72,6... | collective-permute-start | bytes 2359304 | tf_op jit(solution)/shard_map/ppermute | solution.py:20
  169.1 63.2 %collective-permute-start.7 = (bf16[1024,384]{1,0:T(8,128)(2,1)}, bf16[1024,384]{1,0:T(8,128)(2,1)}, u32[]{:S(2)}, u32[]{:S(2)}) collective-permute-start(bf16[1024,384]{1,0:T(8,128)(2,1)} %get-tuple-element.13), channel_id=1, source_target_pairs={{0,8},{8,16},{16,24},{24,32},{32,40},{40,48},{48,56},{56,64},{64,7... | collective-permute-start | bytes 2359304 | tf_op jit(solution)/shard_map/ppermute | solution.py:20
  235.5 44.3 %all-to-all-start.4 = ((bf16[8,128,384]{2,1,0:T(8,128)(2,1)}), bf16[8,128,384]{2,1,0:T(8,128)(2,1)S(1)}, u32[]{:S(2)}, u32[]{:S(2)}) async-start(bf16[8,128,384]{2,1,0:T(8,128)(2,1)} %bitcast.104), calls=%async_computation.4 | async-start | bytes 1572864 | tf_op jit(solution)/shard_map/all_to_all | solution.py:318
  244.3 18.3 %collective-permute-start.4 = (bf16[1024,384]{1,0:T(8,128)(2,1)}, bf16[1024,384]{1,0:T(8,128)(2,1)S(1)}, u32[]{:S(2)}, u32[]{:S(2)}) collective-permute-start(bf16[1024,384]{1,0:T(8,128)(2,1)} %get-tuple-element.14), channel_id=1, source_target_pairs={{8,0},{16,8},{24,16},{32,24},{40,32},{48,40},{56,48},{64,56},{72,6... | collective-permute-start | bytes 2359304 | tf_op jit(solution)/shard_map/ppermute | solution.py:20
  251.2 26.0 %collective-permute-start.5 = (bf16[1024,384]{1,0:T(8,128)(2,1)}, bf16[1024,384]{1,0:T(8,128)(2,1)S(1)}, u32[]{:S(2)}, u32[]{:S(2)}) collective-permute-start(bf16[1024,384]{1,0:T(8,128)(2,1)} %get-tuple-element.15), channel_id=1, source_target_pairs={{0,8},{8,16},{16,24},{24,32},{32,40},{40,48},{48,56},{56,64},{64,7... | collective-permute-start | bytes 2359304 | tf_op jit(solution)/shard_map/ppermute | solution.py:20
  279.8 6.1 %copy-start.5 = (bf16[1024,384]{1,0:T(8,128)(2,1)S(1)}, bf16[1024,384]{1,0:T(8,128)(2,1)}, u32[]{:S(2)}) copy-start(bf16[1024,384]{1,0:T(8,128)(2,1)} %get-tuple-element.8) | copy-start | bytes 2359300
  279.8 6.1 %copy-start.6 = (bf16[1024,384]{1,0:T(8,128)(2,1)S(1)}, bf16[1024,384]{1,0:T(8,128)(2,1)}, u32[]{:S(2)}) copy-start(bf16[1024,384]{1,0:T(8,128)(2,1)} %get-tuple-element.9) | copy-start | bytes 2359300
  279.8 17.2 %all-to-all-start.3 = ((bf16[8,128,384]{2,1,0:T(8,128)(2,1)}), bf16[8,128,384]{2,1,0:T(8,128)(2,1)S(1)}, u32[]{:S(2)}, u32[]{:S(2)}) async-start(bf16[8,128,384]{2,1,0:T(8,128)(2,1)} %bitcast.38), calls=%async_computation.3 | async-start | bytes 1572864 | tf_op jit(solution)/shard_map/all_to_all | solution.py:317
  297.1 17.6 %all-to-all-start.2 = ((bf16[2,1024,384]{2,0,1:T(2,128)(2,1)}), bf16[2,1024,384]{2,0,1:T(2,128)(2,1)S(1)}, u32[]{:S(2)}, u32[]{:S(2)}) async-start(bf16[2,1024,384]{2,0,1:T(2,128)(2,1)} %copy.157), calls=%async_computation.2 | async-start | bytes 3145728 | tf_op jit(solution)/shard_map/all_to_all | solution.py:314

commit v8 on v4

--- a/solution.py
+++ b/solution.py
@@ -225,8 +225,9 @@
     frame_keys = moved[1]
     frame_values = moved[2]
     offset = 1
-    earlier = passed_along((frame_keys, frame_values), "blk", offset)
-    later = passed_along((frame_keys, frame_values), "blk", -offset)
+    frame_both = jnp.stack([frame_keys, frame_values])
+    earlier = passed_along(frame_both, "blk", offset)
+    later = passed_along(frame_both, "blk", -offset)
     earlier_keys = [earlier[0]]
     earlier_values = [earlier[1]]
     later_keys = [later[0]]

time: 314 us -> 321 us (1.022)
  Pallas kernels: 127 us -> 146 us
  starting transfers between devices: 66.5 us -> 55.2 us
  other arithmetic: 25.2 us -> 20.2 us
  local copies, waits for them, and re-layouts: 47 us -> 51.9 us
    pallas_call x2, Pallas kernels: 90 us -> 109 us  [butterfly_sum(): pl.pallas_call(functools.partial(reduce_kernel, count), out_shape=jax.Sha...]
    ppermute x8 -> x6, starting transfers between devices: 42.9 us -> 30.7 us  [passed_along(): return lax.ppermute(block, axis, route)]
    ppermute x8 -> x6, waiting for transfers between devices: 21.3 us -> 20 us  [passed_along(): return lax.ppermute(block, axis, route)]
    another operation x2 -> x3, other arithmetic: 8.42 us -> 7.44 us
  transfers between devices with their start and end apart: 12 -> 10, of which waited for: 5 -> 5; matrix products, arithmetic and copies ran while one was open for 18% -> 16% of each run, Pallas kernels for 29% -> 34%
where the time goes in v8:
time: 321 us; the launch traced here: 320 us
  Pallas kernels  146 us (45%)
  starting transfers between devices  55.2 us (17%)
  local copies, waits for them, and re-layouts  51.9 us (16%)
  waiting for transfers between devices  41.7 us (13%)
  other arithmetic  20.2 us (6%)
  matrix products  4.15 us (1%)
    pallas_call x2, Pallas kernels, butterfly_sum(): pl.pallas_call(functools.partial(reduce_kernel, count), out_shape=jax.Sha...  109 us
    pallas_call x1, Pallas kernels, attend(): pl.pallas_call(attention_kernel, out_shape=(jax.ShapeDtypeStruct((count,...  36.7 us
    ppermute x6, starting transfers between devices, passed_along(): return lax.ppermute(block, axis, route)  30.7 us
    ppermute x6, waiting for transfers between devices, passed_along(): return lax.ppermute(block, axis, route)  20 us
    all_to_all x1, waiting for transfers between devices, per_device(): lax.all_to_all(jnp.stack([keys, values]), 'head', split_axis=2, concat_ax...  15.4 us
    all_to_all x1, starting transfers between devices, per_device(): lax.all_to_all(jnp.stack([key_rows, value_rows]), 'head', split_axis=1, c...  7.98 us
  transfers between devices with their start and end apart: 10, of which 5 were waited for; matrix products, arithmetic and copies ran while one was open for 16% of the time, Pallas kernels for 34%

profile of v8, /device:TPU:160, one launch (start us, length us, event | category | flops | bytes accessed | tf_op | source)
XLA Modules:
  0.0 319.7 jit_solution(17167256454274329781)
XLA Ops:
  2.1 2.9 copy.141
  5.1 5.8 %all-to-all-start.1 = ((bf16[2,128,3072]{1,0,2:T(2,128)(2,1)}), bf16[2,128,3072]{1,0,2:T(2,128)(2,1)S(1)}, u32[]{:S(2)}, u32[]{:S(2)}) async-start(bf16[2,128,3072]{1,0,2:T(2,128)(2,1)} %copy.141), calls=%async_computation.1 | async-start | bytes 3145728 | tf_op jit(solution)/shard_map/all_to_all | solution.py:218
  12.3 2.9 copy.139
  15.3 15.4 %all-to-all-done.1 = bf16[2,128,3072]{1,0,2:T(2,128)(2,1)S(1)} async-done(((bf16[2,128,3072]{1,0,2:T(2,128)(2,1)}), bf16[2,128,3072]{1,0,2:T(2,128)(2,1)S(1)}, u32[]{:S(2)}, u32[]{:S(2)}) %all-to-all-start.1) | async-done | bytes 1572896 | tf_op jit(solution)/shard_map/all_to_all | solution.py:218
  30.7 4.8 %all-to-all-start = ((bf16[2,128,3072]{1,0,2:T(2,128)(2,1)}), bf16[2,128,3072]{1,0,2:T(2,128)(2,1)}, u32[]{:S(2)}, u32[]{:S(2)}) async-start(bf16[2,128,3072]{1,0,2:T(2,128)(2,1)} %copy.139), calls=%async_computation | async-start | bytes 3145728 | tf_op jit(solution)/shard_map/all_to_all | solution.py:221
  37.8 1.9 collective-permute-start
  40.1 8.0 %collective-permute-start.1 = (bf16[2,1024,384]{2,1,0:T(8,128)(2,1)}, bf16[2,1024,384]{2,1,0:T(8,128)(2,1)}, u32[]{:S(2)}, u32[]{:S(2)}) collective-permute-start(bf16[2,1024,384]{2,1,0:T(8,128)(2,1)} %pad_maximum_fusion.6), channel_id=1, source_target_pairs={{8,0},{16,8},{24,16},{32,24},{40,32},{48,40},{56,48},{64,56},{72,6... | collective-permute-start | bytes 4718600 | tf_op jit(solution)/shard_map/ppermute | solution.py:20
  55.4 55.9 %shard_map.84 = bf16[32,48,128]{2,1,0:T(8,128)(2,1)} custom-call(bf16[32,48,128]{2,1,0:T(8,128)(2,1)} %reshape.61.x_ref), custom_call_target="tpu_custom_call" | custom-call | tf_op jit(solution)/shard_map/pallas_call | solution.py:92
  112.5 3.7 %copy.140 = bf16[2,128,8,384]{3,1,2,0:T(8,128)(2,1)S(1)} copy(bf16[2,128,8,384]{1,0,3,2:T(2,128)(2,1)} %bitcast.2) | data formatting | bytes 3145728 | tf_op jit(solution)/shard_map/all_to_all | solution.py:221
  123.1 1.8 pad_maximum_fusion.k_ref
  124.9 36.7 %shard_map.85 = (bf16[1024,384]{1,0:T(8,128)(2,1)}, bf16[1024,384]{1,0:T(8,128)(2,1)}, f32[3328,384]{1,0:T(8,128)}, f32[3328,384]{1,0:T(8,128)}) custom-call(s32[216]{0:T(256)} %reshape.59.index_ref, bf16[1024,384]{1,0:T(8,128)(2,1)} %bitcast.114, bf16[1024,384]{1,0:T(8,128)(2,1)} %bitcast.113, bf16[3328,384]{1,0:T(8,128)(2,1)} %pad_maximum_fusion.k_ref, ...), custom_call_target="tpu_custom_call" | custom-call | flops 6341787648 | bytes 18481152 | tf_op jit(solution)/shard_map/pallas_call | solution.py:187
  161.6 4.3 %convert.8 = bf16[3328,384]{1,0:T(8,128)(2,1)} convert(f32[3328,384]{1,0:T(8,128)} %get-tuple-element.10) | non-fusion elementwise | flops 1277952 | bytes 7667712 | tf_op jit(solution)/shard_map/convert.3
  165.9 1.8 convert.9
  167.9 2.7 copy.149
  170.7 6.0 %all-to-all-start.2 = ((bf16[2,1024,384]{2,0,1:T(2,128)(2,1)}), bf16[2,1024,384]{2,0,1:T(2,128)(2,1)S(1)}, u32[]{:S(2)}, u32[]{:S(2)}) async-start(bf16[2,1024,384]{2,0,1:T(2,128)(2,1)} %copy.149), calls=%async_computation.2 | async-start | bytes 3145728 | tf_op jit(solution)/shard_map/all_to_all | solution.py:315
  179.8 53.0 %shard_map.86 = f32[32,48,128]{2,1,0:T(8,128)} custom-call(f32[32,48,128]{2,1,0:T(8,128)} %reshape_reshape.3.x_ref), custom_call_target="tpu_custom_call" | custom-call | tf_op jit(solution)/shard_map/pallas_call | solution.py:92
  234.1 2.6 fusion.24
  236.7 9.1 %collective-permute-start.2 = (bf16[1024,384]{1,0:T(8,128)(2,1)}, bf16[1024,384]{1,0:T(8,128)(2,1)}, u32[]{:S(2)}, u32[]{:S(2)}) collective-permute-start(bf16[1024,384]{1,0:T(8,128)(2,1)} %get-tuple-element.12), channel_id=1, source_target_pairs={{8,0},{16,8},{24,16},{32,24},{40,32},{48,40},{56,48},{64,56},{72,6... | collective-permute-start | bytes 2359304 | tf_op jit(solution)/shard_map/ppermute | solution.py:20
  245.8 1.9 collective-permute-start.3
  249.0 7.9 %collective-permute-start.4 = (bf16[1024,384]{1,0:T(8,128)(2,1)}, bf16[1024,384]{1,0:T(8,128)(2,1)}, u32[]{:S(2)}, u32[]{:S(2)}) collective-permute-start(bf16[1024,384]{1,0:T(8,128)(2,1)} %get-tuple-element.14), channel_id=1, source_target_pairs={{8,0},{16,8},{24,16},{32,24},{40,32},{48,40},{56,48},{64,56},{72,6... | collective-permute-start | bytes 2359304 | tf_op jit(solution)/shard_map/ppermute | solution.py:20
  256.9 1.9 collective-permute-start.5
  259.9 2.4 copy.162
  264.7 13.8 %collective-permute-done.3 = bf16[1024,384]{1,0:T(8,128)(2,1)} collective-permute-done((bf16[1024,384]{1,0:T(8,128)(2,1)S(1)}, bf16[1024,384]{1,0:T(8,128)(2,1)}, u32[]{:S(2)}, u32[]{:S(2)}) %collective-permute-start.3) | collective-permute-done | bytes 786464 | tf_op jit(solution)/shard_map/ppermute | solution.py:20
  278.5 2.3 fusion.4
  280.8 3.3 %collective-permute-done.4 = bf16[1024,384]{1,0:T(8,128)(2,1)} collective-permute-done((bf16[1024,384]{1,0:T(8,128)(2,1)}, bf16[1024,384]{1,0:T(8,128)(2,1)}, u32[]{:S(2)}, u32[]{:S(2)}) %collective-permute-start.4) | collective-permute-done | bytes 786464 | tf_op jit(solution)/shard_map/ppermute | solution.py:20
  284.1 2.9 collective-permute-done.5
  287.0 2.3 fusion.5
  289.4 2.8 copy.158
  292.2 8.0 %all-to-all-start.3 = ((bf16[2,1024,384]{2,0,1:T(2,128)(2,1)}), bf16[2,1024,384]{2,0,1:T(2,128)(2,1)S(1)}, u32[]{:S(2)}, u32[]{:S(2)}) async-start(bf16[2,1024,384]{2,0,1:T(2,128)(2,1)} %copy.158), calls=%async_computation.3 | async-start | bytes 3145728 | tf_op jit(solution)/shard_map/all_to_all | solution.py:318
  300.2 2.9 fusion.27
  306.8 6.2 %all-to-all-done.3 = bf16[2,1024,384]{2,0,1:T(2,128)(2,1)S(1)} async-done(((bf16[2,1024,384]{2,0,1:T(2,128)(2,1)}), bf16[2,1024,384]{2,0,1:T(2,128)(2,1)S(1)}, u32[]{:S(2)}, u32[]{:S(2)}) %all-to-all-start.3) | async-done | bytes 1572896 | tf_op jit(solution)/shard_map/all_to_all | solution.py:318
  313.1 2.9 fusion.26
  (70 shorter events, 38.0 us)
Async XLA Ops:
  5.1 25.6 %all-to-all-start.1 = ((bf16[2,128,3072]{1,0,2:T(2,128)(2,1)}), bf16[2,128,3072]{1,0,2:T(2,128)(2,1)S(1)}, u32[]{:S(2)}, u32[]{:S(2)}) async-start(bf16[2,128,3072]{1,0,2:T(2,128)(2,1)} %copy.141), calls=%async_computation.1 | async-start | bytes 3145728 | tf_op jit(solution)/shard_map/all_to_all | solution.py:218
  30.7 81.8 %all-to-all-start = ((bf16[2,128,3072]{1,0,2:T(2,128)(2,1)}), bf16[2,128,3072]{1,0,2:T(2,128)(2,1)}, u32[]{:S(2)}, u32[]{:S(2)}) async-start(bf16[2,128,3072]{1,0,2:T(2,128)(2,1)} %copy.139), calls=%async_computation | async-start | bytes 3145728 | tf_op jit(solution)/shard_map/all_to_all | solution.py:221
  36.5 3.3 %copy-start.6 = (s32[3,256,9]{1,0,2:T(4,128)S(1)}, s32[3,256,9]{1,0,2:T(4,128)}, u32[]{:S(2)}) copy-start(s32[3,256,9]{1,0,2:T(4,128)} %param.9) | copy-start | bytes 82948
  37.8 79.8 %collective-permute-start = (bf16[2,1024,384]{2,1,0:T(8,128)(2,1)}, bf16[2,1024,384]{2,1,0:T(8,128)(2,1)}, u32[]{:S(2)}, u32[]{:S(2)}) collective-permute-start(bf16[2,1024,384]{2,1,0:T(8,128)(2,1)} %pad_maximum_fusion.6), channel_id=1, source_target_pairs={{0,8},{8,16},{16,24},{24,32},{32,40},{40,48},{48,56},{56,64},{64,7... | collective-permute-start | bytes 4718600 | tf_op jit(solution)/shard_map/ppermute | solution.py:20
  40.1 79.1 %collective-permute-start.1 = (bf16[2,1024,384]{2,1,0:T(8,128)(2,1)}, bf16[2,1024,384]{2,1,0:T(8,128)(2,1)}, u32[]{:S(2)}, u32[]{:S(2)}) collective-permute-start(bf16[2,1024,384]{2,1,0:T(8,128)(2,1)} %pad_maximum_fusion.6), channel_id=1, source_target_pairs={{8,0},{16,8},{24,16},{32,24},{40,32},{48,40},{56,48},{64,56},{72,6... | collective-permute-start | bytes 4718600 | tf_op jit(solution)/shard_map/ppermute | solution.py:20
  50.2 1.3 copy-start.3
  161.6 4.3 %copy-start = (f32[3328,384]{1,0:T(8,128)S(1)}, f32[3328,384]{1,0:T(8,128)}, u32[]{:S(2)}) copy-start(f32[3328,384]{1,0:T(8,128)} %get-tuple-element.11) | copy-start | bytes 15335428
  165.9 1.8 copy-start.4
  165.9 1.8 copy-start.5
  170.7 121.5 %all-to-all-start.2 = ((bf16[2,1024,384]{2,0,1:T(2,128)(2,1)}), bf16[2,1024,384]{2,0,1:T(2,128)(2,1)S(1)}, u32[]{:S(2)}, u32[]{:S(2)}) async-start(bf16[2,1024,384]{2,0,1:T(2,128)(2,1)} %copy.149), calls=%async_computation.2 | async-start | bytes 3145728 | tf_op jit(solution)/shard_map/all_to_all | solution.py:315
  234.1 13.6 %copy-start.2 = (bf16[3328,384]{1,0:T(8,128)(2,1)S(1)}, bf16[3328,384]{1,0:T(8,128)(2,1)}, u32[]{:S(2)}) copy-start(bf16[3328,384]{1,0:T(8,128)(2,1)} %convert.9) | copy-start | bytes 7667716
  236.7 28.0 %collective-permute-start.2 = (bf16[1024,384]{1,0:T(8,128)(2,1)}, bf16[1024,384]{1,0:T(8,128)(2,1)}, u32[]{:S(2)}, u32[]{:S(2)}) collective-permute-start(bf16[1024,384]{1,0:T(8,128)(2,1)} %get-tuple-element.12), channel_id=1, source_target_pairs={{8,0},{16,8},{24,16},{32,24},{40,32},{48,40},{56,48},{64,56},{72,6... | collective-permute-start | bytes 2359304 | tf_op jit(solution)/shard_map/ppermute | solution.py:20
  245.8 32.7 %collective-permute-start.3 = (bf16[1024,384]{1,0:T(8,128)(2,1)S(1)}, bf16[1024,384]{1,0:T(8,128)(2,1)}, u32[]{:S(2)}, u32[]{:S(2)}) collective-permute-start(bf16[1024,384]{1,0:T(8,128)(2,1)S(1)} %get-tuple-element.13), channel_id=1, source_target_pairs={{0,8},{8,16},{16,24},{24,32},{32,40},{40,48},{48,56},{56,64},{64,7... | collective-permute-start | bytes 2359304 | tf_op jit(solution)/shard_map/ppermute | solution.py:20
  249.0 35.1 %collective-permute-start.4 = (bf16[1024,384]{1,0:T(8,128)(2,1)}, bf16[1024,384]{1,0:T(8,128)(2,1)}, u32[]{:S(2)}, u32[]{:S(2)}) collective-permute-start(bf16[1024,384]{1,0:T(8,128)(2,1)} %get-tuple-element.14), channel_id=1, source_target_pairs={{8,0},{16,8},{24,16},{32,24},{40,32},{48,40},{56,48},{64,56},{72,6... | collective-permute-start | bytes 2359304 | tf_op jit(solution)/shard_map/ppermute | solution.py:20
  256.9 30.1 %collective-permute-start.5 = (bf16[1024,384]{1,0:T(8,128)(2,1)}, bf16[1024,384]{1,0:T(8,128)(2,1)}, u32[]{:S(2)}, u32[]{:S(2)}) collective-permute-start(bf16[1024,384]{1,0:T(8,128)(2,1)} %get-tuple-element.15), channel_id=1, source_target_pairs={{0,8},{8,16},{16,24},{24,32},{32,40},{40,48},{48,56},{56,64},{64,7... | collective-permute-start | bytes 2359304 | tf_op jit(solution)/shard_map/ppermute | solution.py:20
  263.6 14.9 %copy-start.1 = (f32[8,128,3,128]{3,2,1,0:T(4,128)S(1)}, f32[8,128,3,128]{3,2,1,0:T(4,128)}, u32[]{:S(2)}) copy-start(f32[8,128,3,128]{3,2,1,0:T(4,128)} %copy.162) | copy-start | bytes 4718596
  292.2 20.8 %all-to-all-start.3 = ((bf16[2,1024,384]{2,0,1:T(2,128)(2,1)}), bf16[2,1024,384]{2,0,1:T(2,128)(2,1)S(1)}, u32[]{:S(2)}, u32[]{:S(2)}) async-start(bf16[2,1024,384]{2,0,1:T(2,128)(2,1)} %copy.158), calls=%async_computation.3 | async-start | bytes 3145728 | tf_op jit(solution)/shard_map/all_to_all | solution.py:318
